TPU v7x, 32 devices: a whole 2x2x4 slice. The times are simulated.
32 devices in a mesh: dp: 8 (over z, core), tensor: 4 (over y, x).
Axes of the slice: x: 2, y: 2, z: 4, core: 2. Of those that a mesh axis runs over, the one named last changes fastest.
Arguments:
- tokens: bfloat16 [16384, 2048], P(('dp', 'tensor')), may hold values from -6 to 6
- cotangent: bfloat16 [16384, 2048], P(('dp', 'tensor')), may hold values from -6 to 6
- seq_ids: int32 [16384], P('dp'), may hold values from 0 to 15, as said below
- block_ids: int32 [16384], P('dp'), may hold values from 0 to 7, as said below
- groups: int32 [8], replicated, may hold values from 0 to 3, as said below
- qkv_weight: float32 [3, 2048, 2048], P(None, 'dp', 'tensor'), may hold values from -0.125 to 0.125
- out_weight: float32 [2048, 2048], P('tensor', 'dp'), may hold values from -2 to 2
- gate_weight: float32 [2, 2048, 8192], P(None, 'dp', 'tensor'), may hold values from -0.125 to 0.125
- down_weight: float32 [8192, 2048], P('tensor', 'dp'), may hold values from -0.0625 to 0.0625
- norm_gains: float32 [2, 2048], replicated, may hold values from 0.5 to 1.5
- qkv_first: float32 [4, 3, 2048, 2048], P(None, None, 'dp', 'tensor'), may hold values from -24 to 24
- out_first: float32 [4, 2048, 2048], P(None, 'tensor', 'dp'), may hold values from -6 to 6
- gate_first: float32 [4, 2, 2048, 8192], P(None, None, 'dp', 'tensor'), may hold values from -6 to 6
- down_first: float32 [4, 8192, 2048], P(None, 'tensor', 'dp'), may hold values from -24 to 24
- gains_first: float32 [4, 2, 2048], replicated, may hold values from -32 to 32
- qkv_second: float32 [4, 3, 2048, 2048], P(None, None, 'dp', 'tensor'), may hold values from 77.824 to 311.296
- out_second: float32 [4, 2048, 2048], P(None, 'tensor', 'dp'), may hold values from 0.77824 to 3.11296
- gate_second: float32 [4, 2, 2048, 8192], P(None, None, 'dp', 'tensor'), may hold values from 13.5168 to 53.248
- down_second: float32 [4, 8192, 2048], P(None, 'tensor', 'dp'), may hold values from 77.824 to 311.296
- gains_second: float32 [4, 2, 2048], replicated, may hold values from 106.496 to 409.6
- qkv_outer: float32 [3, 2048, 2048], P(None, 'dp', 'tensor'), may hold values from -0.1875 to 0.1875
- out_outer: float32 [2048, 2048], P('tensor', 'dp'), may hold values from -2.5 to 2.5
- gate_outer: float32 [2, 2048, 8192], P(None, 'dp', 'tensor'), may hold values from -0.1875 to 0.1875
- down_outer: float32 [8192, 2048], P('tensor', 'dp'), may hold values from -0.09375 to 0.09375
- gains_outer: float32 [2, 2048], replicated, may hold values from -1.5 to 1.5
Outputs:
- layer_out: bfloat16 [16384, 2048], P(('dp', 'tensor'))
- tokens_grad: float32 [16384, 2048], P(('dp', 'tensor'))
- qkv_first_new: float32 [4, 3, 2048, 2048], P(None, None, 'dp', 'tensor')
- qkv_second_new: float32 [4, 3, 2048, 2048], P(None, None, 'dp', 'tensor')
- qkv_delta: float32 [3, 2048, 2048], P(None, 'dp', 'tensor')
- qkv_outer_new: float32 [3, 2048, 2048], P(None, 'dp', 'tensor')
- qkv_master: float32 [3, 2048, 2048], P(None, 'dp', 'tensor')
- qkv_low: bfloat16 [3, 2048, 2048], P(None, 'dp', 'tensor')
- out_first_new: float32 [4, 2048, 2048], P(None, 'tensor', 'dp')
- out_second_new: float32 [4, 2048, 2048], P(None, 'tensor', 'dp')
- out_delta: float32 [2048, 2048], P('tensor', 'dp')
- out_outer_new: float32 [2048, 2048], P('tensor', 'dp')
- out_master: float32 [2048, 2048], P('tensor', 'dp')
- out_low: bfloat16 [2048, 2048], P('tensor', 'dp')
- gate_first_new: float32 [4, 2, 2048, 8192], P(None, None, 'dp', 'tensor')
- gate_second_new: float32 [4, 2, 2048, 8192], P(None, None, 'dp', 'tensor')
- gate_delta: float32 [2, 2048, 8192], P(None, 'dp', 'tensor')
- gate_outer_new: float32 [2, 2048, 8192], P(None, 'dp', 'tensor')
- gate_master: float32 [2, 2048, 8192], P(None, 'dp', 'tensor')
- gate_low: bfloat16 [2, 2048, 8192], P(None, 'dp', 'tensor')
- down_first_new: float32 [4, 8192, 2048], P(None, 'tensor', 'dp')
- down_second_new: float32 [4, 8192, 2048], P(None, 'tensor', 'dp')
- down_delta: float32 [8192, 2048], P('tensor', 'dp')
- down_outer_new: float32 [8192, 2048], P('tensor', 'dp')
- down_master: float32 [8192, 2048], P('tensor', 'dp')
- down_low: bfloat16 [8192, 2048], P('tensor', 'dp')
- gains_first_new: float32 [4, 2, 2048], replicated
- gains_second_new: float32 [4, 2, 2048], replicated
- gains_delta: float32 [2, 2048], replicated
- gains_outer_new: float32 [2, 2048], replicated
- gains_master: float32 [2, 2048], replicated
- gains_low: bfloat16 [2, 2048], replicated
Inputs may be any that keep to these rules, and one draw needn't show every extreme that they name: `seq_ids`: each aligned run of 2048 tokens holds two whole sequences, each one or more tokens long; ids never fall within a run and differ between runs. `block_ids`: A token's block is its position within its sequence divided by 256, rounded down; some run holds a sequence of 2047 tokens. `groups`: each group holds 2 shards.
All inputs are finite; a program needn't handle non-finite values.
Results may differ from a plain program's by a relative error of at most 0.023.
Values may be sent and summed in bfloat16 or wider, within the bound.
A program may use at most 512 MiB of HBM per device.

v0:
```python
import jax
import jax.numpy as jnp
from jax import lax
from jax.sharding import PartitionSpec as P

HDIM = 64
GROUPS = 4
STEP = 4


norm_eps = 1e-05
rope_base = 130000.0
beta_first = 0.9
beta_second = 0.95
adam_eps = 1e-08
outer_rate = 0.7
outer_beta = 0.9
inner_rates = (0.04, 0.6, 0.04, 0.02, 0.35)
decays = (0.1, 0.1, 0.1, 0.1, 0.0)
contract_rows = (((0,), (0,)), ((), ()))
contract_cols = (((1,), (1,)), ((), ()))


def as_sent(array):

    def short(part):
        return part.astype(jnp.bfloat16) if part.dtype == jnp.float32 else part

    return jax.tree.map(short, array)


def rotate(values):
    middle = values.shape[-1] // 2
    return jnp.concatenate([-values[..., middle:], values[..., :middle]], axis=-1)


def tables(seq_part, head_dim):
    length = seq_part.shape[0]
    places = jnp.arange(length, dtype=jnp.int32)
    before = jnp.sum((seq_part[None, :] < seq_part[:, None]).astype(jnp.int32), axis=1)
    where_at = (places - before).astype(jnp.float32)
    inverse = rope_base ** (-(jnp.arange(head_dim // 2, dtype=jnp.float32) * 2.0 / head_dim))
    angles = where_at[:, None] * inverse[None, :]
    angles = jnp.concatenate([angles, angles], axis=1)
    return (jnp.cos(angles)[:, None, :], jnp.sin(angles)[:, None, :])


def normed(field_rows, gain_row):
    factor = lax.rsqrt(jnp.mean(field_rows * field_rows, axis=-1, keepdims=True) + norm_eps)
    scaled = field_rows * factor
    return ((scaled * gain_row).astype(jnp.bfloat16), scaled, factor)


def norm_back(upstream, scaled, factor, gain_row):
    inside = upstream * gain_row
    return factor * (inside - scaled * jnp.mean(inside * scaled, axis=-1, keepdims=True))


def update(weight, gradient, first_old, second_old, outer_old, step_rate, decay_rate):
    first_new = beta_first * first_old + (1.0 - beta_first) * gradient
    second_new = beta_second * second_old + (1.0 - beta_second) * gradient * gradient
    fix_first = 1.0 - beta_first**STEP
    fix_second = 1.0 - beta_second**STEP
    stepped = weight[None] - step_rate * (
        first_new / fix_first / (jnp.sqrt(second_new / fix_second) + adam_eps)
        + decay_rate * weight[None]
    )
    change = jnp.mean(weight[None] - stepped, axis=0)
    outer_new = outer_beta * outer_old + change
    master = weight - outer_rate * (change + outer_beta * outer_new)
    return [first_new, second_new, change, outer_new, master, master.astype(jnp.bfloat16)]


def on_device(
    tokens,
    cotangent,
    seq_ids,
    block_ids,
    groups,
    qkv_weight,
    out_weight,
    gate_weight,
    down_weight,
    norm_gains,
    qkv_first,
    out_first,
    gate_first,
    down_first,
    gains_first,
    qkv_second,
    out_second,
    gate_second,
    down_second,
    gains_second,
    qkv_outer,
    out_outer,
    gate_outer,
    down_outer,
    gains_outer,
):
    masters = (qkv_weight, out_weight, gate_weight, down_weight)
    rounded = tuple((weight.astype(jnp.bfloat16) for weight in masters))
    gathered = jax.tree.map(
        lambda part, own: part.astype(own.dtype),
        lax.all_gather(as_sent(rounded), "dp", axis=1, tiled=True),
        rounded,
    )
    qkv_full, out_full, gate_full, down_full = gathered
    field_in = tokens.astype(jnp.float32)
    local_rows = field_in.shape[0]
    normed_one, scaled_one, factor_one = normed(field_in, norm_gains[0])
    normed_all, cotan_all = (
        lax.all_gather(normed_one, "tensor", axis=0, tiled=True),
        lax.all_gather(cotangent, "tensor", axis=0, tiled=True),
    )
    shard_rows = normed_all.shape[0]
    local_heads = qkv_full.shape[2] // HDIM
    block_rows = min(512, shard_rows)
    blocks = shard_rows // block_rows
    score_scale = HDIM ** (-0.5)
    cosine, sine_table = tables(seq_ids, HDIM)

    def project(member_id):
        return jnp.dot(normed_all, qkv_full[member_id], preferred_element_type=jnp.float32).reshape(
            shard_rows, local_heads, HDIM
        )

    query_raw = project(0)
    key_raw = project(1)
    queries = (query_raw * cosine + rotate(query_raw) * sine_table).astype(jnp.bfloat16)
    keys_all = (key_raw * cosine + rotate(key_raw) * sine_table).astype(jnp.bfloat16)
    values_all = project(2).astype(jnp.bfloat16)

    def scores_of(offset):
        query_block = lax.dynamic_slice_in_dim(queries, offset, block_rows, 0)
        seq_block = lax.dynamic_slice_in_dim(seq_ids, offset, block_rows, 0)
        kind_block = lax.dynamic_slice_in_dim(block_ids, offset, block_rows, 0)
        allowed = (seq_block[:, None] == seq_ids[None, :]) & (
            kind_block[:, None] >= block_ids[None, :]
        )
        logits = (
            jnp.einsum("qhd,khd->hqk", query_block, keys_all, preferred_element_type=jnp.float32)
            * score_scale
        )
        return jnp.where(allowed[None], logits, -jnp.inf)

    def forward_block(number):
        logits = scores_of(number * block_rows)
        row_peak = jnp.max(logits, axis=-1, keepdims=True)
        totals = jnp.sum(jnp.exp(logits - row_peak), axis=-1, keepdims=True)
        logsum = row_peak + jnp.log(totals)
        probs_low = jnp.exp(logits - logsum).astype(jnp.bfloat16)
        mixture = jnp.einsum(
            "hqk,khd->qhd", probs_low, values_all, preferred_element_type=jnp.float32
        )
        return (mixture.astype(jnp.bfloat16), logsum)

    mixed_blocks, logsums = lax.map(forward_block, jnp.arange(blocks))
    mixed_all = mixed_blocks.reshape(shard_rows, local_heads * HDIM)
    slab = mixed_all
    attn_rows = lax.psum_scatter(
        jnp.dot(slab, out_full, preferred_element_type=jnp.float32),
        "tensor",
        scatter_dimension=0,
        tiled=True,
    )
    residual = field_in + attn_rows
    normed_two, scaled_two, factor_two = normed(residual, norm_gains[1])
    ffn_input = lax.all_gather(normed_two, "tensor", axis=0, tiled=True)
    gate_pre = jnp.dot(ffn_input, gate_full[0], preferred_element_type=jnp.float32)
    up_pre = jnp.dot(ffn_input, gate_full[1], preferred_element_type=jnp.float32)
    sigmoid_gate = jax.nn.sigmoid(gate_pre)
    swish = gate_pre * sigmoid_gate
    hidden = (swish * up_pre).astype(jnp.bfloat16)
    slab = hidden
    ffn_part = lax.psum_scatter(
        jnp.dot(slab, down_full, preferred_element_type=jnp.float32).astype(jnp.bfloat16),
        "tensor",
        scatter_dimension=0,
        tiled=True,
    ).astype(jnp.float32)
    layer_out = (residual + ffn_part).astype(jnp.bfloat16)
    regathered = jax.tree.map(
        lambda part, own: part.astype(own.dtype),
        lax.all_gather(as_sent(rounded), "dp", axis=1, tiled=True),
        rounded,
    )
    qkv_back, out_back, gate_back, down_back = regathered
    down_grad = lax.dot_general(
        hidden, cotan_all, contract_rows, preferred_element_type=jnp.float32
    )
    hidden_grad = lax.dot_general(
        cotan_all, down_back, contract_cols, preferred_element_type=jnp.float32
    )
    gate_grad_low = (
        hidden_grad * up_pre * sigmoid_gate * (1.0 + gate_pre * (1.0 - sigmoid_gate))
    ).astype(jnp.bfloat16)
    up_grad_low = (hidden_grad * swish).astype(jnp.bfloat16)
    gate_grad = jnp.stack(
        [
            lax.dot_general(
                ffn_input, gate_grad_low, contract_rows, preferred_element_type=jnp.float32
            ),
            lax.dot_general(
                ffn_input, up_grad_low, contract_rows, preferred_element_type=jnp.float32
            ),
        ]
    )
    ffn_back_rows = lax.psum_scatter(
        lax.dot_general(
            gate_grad_low, gate_back[0], contract_cols, preferred_element_type=jnp.float32
        )
        + lax.dot_general(
            up_grad_low, gate_back[1], contract_cols, preferred_element_type=jnp.float32
        ),
        "tensor",
        scatter_dimension=0,
        tiled=True,
    )
    cotan_rows = cotangent.astype(jnp.float32)
    resid_grad = cotan_rows + norm_back(ffn_back_rows, scaled_two, factor_two, norm_gains[1])
    gain_two = jnp.sum(ffn_back_rows * scaled_two, axis=0)
    resid_all = lax.all_gather(resid_grad.astype(jnp.bfloat16), "tensor", axis=0, tiled=True)
    out_grad = lax.dot_general(
        mixed_all, resid_all, contract_rows, preferred_element_type=jnp.float32
    )
    mixed_grad = (
        lax.dot_general(resid_all, out_back, contract_cols, preferred_element_type=jnp.float32)
        .astype(jnp.bfloat16)
        .reshape(shard_rows, local_heads, HDIM)
    )

    def back_block(carried, number):
        key_acc, value_acc = carried
        offset = number * block_rows
        logits = scores_of(offset)
        query_block = lax.dynamic_slice_in_dim(queries, offset, block_rows, 0)
        grad_block = lax.dynamic_slice_in_dim(mixed_grad, offset, block_rows, 0)
        probs = jnp.exp(logits - logsums[number])
        probs_low = probs.astype(jnp.bfloat16)
        prob_grad = jnp.einsum(
            "qhd,khd->hqk", grad_block, values_all, preferred_element_type=jnp.float32
        )
        center = jnp.sum(probs * prob_grad, axis=-1, keepdims=True)
        score_grad = (probs * (prob_grad - center)).astype(jnp.bfloat16)
        query_grad = (
            jnp.einsum("hqk,khd->qhd", score_grad, keys_all, preferred_element_type=jnp.float32)
            * score_scale
        )
        key_acc = (
            key_acc
            + jnp.einsum(
                "hqk,qhd->khd", score_grad, query_block, preferred_element_type=jnp.float32
            )
            * score_scale
        )
        value_acc = value_acc + jnp.einsum(
            "hqk,qhd->khd", probs_low, grad_block, preferred_element_type=jnp.float32
        )
        return ((key_acc, value_acc), query_grad)

    zeros_heads = jnp.zeros((shard_rows, local_heads, HDIM), jnp.float32)
    (key_grad, value_grad), query_grads = lax.scan(
        back_block, (zeros_heads, zeros_heads), jnp.arange(blocks)
    )
    query_grad_all = query_grads.reshape(shard_rows, local_heads, HDIM)
    query_back = (
        (query_grad_all * cosine - rotate(query_grad_all) * sine_table)
        .astype(jnp.bfloat16)
        .reshape(shard_rows, local_heads * HDIM)
    )
    key_back = (
        (key_grad * cosine - rotate(key_grad) * sine_table)
        .astype(jnp.bfloat16)
        .reshape(shard_rows, local_heads * HDIM)
    )
    value_back = value_grad.astype(jnp.bfloat16).reshape(shard_rows, local_heads * HDIM)
    raw_grads = (query_back, key_back, value_back)
    qkv_grad = jnp.stack(
        [
            lax.dot_general(normed_all, member, contract_rows, preferred_element_type=jnp.float32)
            for member in raw_grads
        ]
    )
    summed = jnp.zeros((local_rows * lax.axis_size("tensor"), qkv_back.shape[1]), jnp.float32)
    for attn_position in range(3):
        slab = raw_grads[attn_position]
        summed = summed + lax.dot_general(
            slab, qkv_back[attn_position], contract_cols, preferred_element_type=jnp.float32
        )
    in_grad_rows = lax.psum_scatter(
        summed.astype(jnp.bfloat16), "tensor", scatter_dimension=0, tiled=True
    ).astype(jnp.float32)
    tokens_grad = resid_grad + norm_back(in_grad_rows, scaled_one, factor_one, norm_gains[0])
    gain_one = jnp.sum(in_grad_rows * scaled_one, axis=0)
    own_group = (jnp.arange(GROUPS, dtype=jnp.int32) == groups[lax.axis_index("dp")]).astype(
        jnp.float32
    )
    gain_slots = own_group[:, None, None] * jnp.stack([gain_one, gain_two])[None]
    gain_grad = lax.psum(gain_slots, ("dp", "tensor"))
    received = (
        lax.all_to_all(
            qkv_grad.astype(jnp.bfloat16), "dp", split_axis=1, concat_axis=0, tiled=True
        ).astype(qkv_grad.dtype),
        lax.all_to_all(
            out_grad.astype(jnp.bfloat16), "dp", split_axis=1, concat_axis=0, tiled=True
        ).astype(out_grad.dtype),
        lax.all_to_all(
            gate_grad.astype(jnp.bfloat16), "dp", split_axis=1, concat_axis=0, tiled=True
        ).astype(gate_grad.dtype),
        lax.all_to_all(
            down_grad.astype(jnp.bfloat16), "dp", split_axis=1, concat_axis=0, tiled=True
        ).astype(down_grad.dtype),
    )
    sources = lax.axis_size("dp")
    shaped = (
        received[0].reshape((sources, 3) + received[0].shape[1:]),
        received[1].reshape((sources, -1) + received[1].shape[1:]),
        received[2].reshape((sources, 2) + received[2].shape[1:]),
        received[3].reshape((sources, -1) + received[3].shape[1:]),
    )
    picker = (groups[None, :] == jnp.arange(GROUPS, dtype=jnp.int32)[:, None]).astype(jnp.float32)
    group_grads = tuple(
        (
            jnp.einsum("gs,s...->g...", picker, member, precision=lax.Precision.HIGHEST)
            for member in shaped
        )
    )
    weights_all = (qkv_weight, out_weight, gate_weight, down_weight, norm_gains)
    grads_all = group_grads + (gain_grad,)
    firsts = (qkv_first, out_first, gate_first, down_first, gains_first)
    seconds = (qkv_second, out_second, gate_second, down_second, gains_second)
    outers = (qkv_outer, out_outer, gate_outer, down_outer, gains_outer)
    results = []
    for position in range(5):
        results.extend(
            update(
                weights_all[position],
                grads_all[position],
                firsts[position],
                seconds[position],
                outers[position],
                inner_rates[position],
                decays[position],
            )
        )
    return (layer_out, tokens_grad) + tuple(results)


def solution(mesh):
    in_specs = (
        P(("dp", "tensor"), None),
        P(("dp", "tensor"), None),
        P("dp"),
        P("dp"),
        P(),
        P(None, "dp", "tensor"),
        P("tensor", "dp"),
        P(None, "dp", "tensor"),
        P("tensor", "dp"),
        P(),
        P(None, None, "dp", "tensor"),
        P(None, "tensor", "dp"),
        P(None, None, "dp", "tensor"),
        P(None, "tensor", "dp"),
        P(),
        P(None, None, "dp", "tensor"),
        P(None, "tensor", "dp"),
        P(None, None, "dp", "tensor"),
        P(None, "tensor", "dp"),
        P(),
        P(None, "dp", "tensor"),
        P("tensor", "dp"),
        P(None, "dp", "tensor"),
        P("tensor", "dp"),
        P(),
    )
    out_specs = (
        P(("dp", "tensor"), None),
        P(("dp", "tensor"), None),
        P(None, None, "dp", "tensor"),
        P(None, None, "dp", "tensor"),
        P(None, "dp", "tensor"),
        P(None, "dp", "tensor"),
        P(None, "dp", "tensor"),
        P(None, "dp", "tensor"),
        P(None, "tensor", "dp"),
        P(None, "tensor", "dp"),
        P("tensor", "dp"),
        P("tensor", "dp"),
        P("tensor", "dp"),
        P("tensor", "dp"),
        P(None, None, "dp", "tensor"),
        P(None, None, "dp", "tensor"),
        P(None, "dp", "tensor"),
        P(None, "dp", "tensor"),
        P(None, "dp", "tensor"),
        P(None, "dp", "tensor"),
        P(None, "tensor", "dp"),
        P(None, "tensor", "dp"),
        P("tensor", "dp"),
        P("tensor", "dp"),
        P("tensor", "dp"),
        P("tensor", "dp"),
        P(),
        P(),
        P(),
        P(),
        P(),
        P(),
    )
    return jax.shard_map(
        on_device, mesh=mesh, in_specs=in_specs, out_specs=out_specs, check_vma=False
    )
```

profile of v0, /device:TPU:1, one launch (start us, length us, event | category | flops | bytes accessed | tf_op | source)
XLA Modules:
  0.0 2626.5 jit_solution(16412822041520565266)
XLA Ops:
  19.8 58.5 %all-gather.11.cloned.1.call-done = bf16[3,2048,512]{2,1,0:T(8,128)(2,1)} async-done(((bf16[3,256,512]{2,1,0:T(8,128)(2,1)}), bf16[3,2048,512]{2,1,0:T(8,128)(2,1)}) %all-gather.11.cloned.1.call-update) | async-done | bytes 6291472 | tf_op jit(solution)/shard_map/all_gather | solution.py:105
  94.1 72.3 %all-gather.9.cloned.1.call-done = bf16[2048,2048]{1,0:T(8,128)(2,1)} async-done(((bf16[512,2048]{1,0:T(8,128)(2,1)}), bf16[2048,2048]{1,0:T(8,128)(2,1)}) %all-gather.9.cloned.1.call-update) | async-done | bytes 8388624 | tf_op jit(solution)/shard_map/all_gather | solution.py:113
  193.1 193.6 %while.27 = (s32[]{:T(128)}, bf16[4,512,8,64]{1,3,2,0:T(8,128)(2,1)}, f32[4,8,512,1]{2,1,3,0:T(8,128)}, s32[4]{0:T(128)S(1)}, s32[2048]{0:T(1024)S(1)}, /*index=...) while((s32[]{:T(128)}, ...), condition=%wide.region_5.6_spmd, body=%wide.region_2.5_spmd.sunk | while | flops 2243162112 | bytes 110260432 | solution.py:158
  195.4 14.6 fusion.178
  210.0 15.0 exponential_reduce_fusion.2
  225.6 15.8 fusion.179
  243.7 14.6 fusion.178
  258.3 15.0 exponential_reduce_fusion.2
  273.9 15.8 fusion.179
  292.0 14.6 fusion.178
  306.7 15.0 exponential_reduce_fusion.2
  322.2 15.8 fusion.179
  340.3 14.6 fusion.178
  355.0 15.0 exponential_reduce_fusion.2
  370.6 15.8 fusion.179
  392.7 12.9 fusion.121
  413.2 146.4 %reduce-scatter.5.cloned.1.call-done = f32[512,2048]{1,0:T(8,128)} async-done(((f32[2048,2048]{1,0:T(8,128)}), f32[512,2048]{1,0:T(8,128)}) %reduce-scatter.5.cloned.1.call-update) | async-done | bytes 4194320 | tf_op jit(solution)/shard_map/reduce_scatter | solution.py:161
  568.9 144.4 %all-gather.17.cloned.1.call-done = bf16[2,2048,2048]{2,1,0:T(8,128)(2,1)} async-done(((bf16[2,256,2048]{2,1,0:T(8,128)(2,1)}), bf16[2,2048,2048]{2,1,0:T(8,128)(2,1)}) %all-gather.17.cloned.1.call-update) | async-done | bytes 16777232 | tf_op jit(solution)/shard_map/all_gather | solution.py:105
  713.2 87.4 %all-gather.15.cloned.1.call-done = bf16[2048,2048]{1,0:T(8,128)(2,1)} async-done(((bf16[512,2048]{1,0:T(8,128)(2,1)}), bf16[2048,2048]{1,0:T(8,128)(2,1)}) %all-gather.15.cloned.1.call-update) | async-done | bytes 8388624 | tf_op jit(solution)/shard_map/all_gather | solution.py:169
  800.6 24.5 fusion.45
  825.1 21.1 fusion.44
  846.2 43.8 %all-gather.21.cloned.1.call-done = bf16[2048,2048]{1,0:T(8,128)(2,1)} async-done(((bf16[512,2048]{1,0:T(8,128)(2,1)}), bf16[2048,2048]{1,0:T(8,128)(2,1)}) %all-gather.21.cloned.1.call-update) | async-done | bytes 8388624 | tf_op jit(solution)/shard_map/all_gather | solution.py:114
  890.0 85.2 %all-gather.19.cloned.1.call-done = bf16[2048,2048]{1,0:T(8,128)(2,1)} async-done(((bf16[2048,256]{1,0:T(8,128)(2,1)}), bf16[2048,2048]{1,0:T(8,128)(2,1)}) %all-gather.19.cloned.1.call-update) | async-done | bytes 8388624 | tf_op jit(solution)/shard_map/all_gather | solution.py:105
  975.2 36.9 %multiply_convert_fusion.1 = (bf16[2048,2048]{1,0:T(8,128)(2,1)}, bf16[2048,2048]{1,0:T(8,128)(2,1)}, bf16[2048,2048]{1,0:T(8,128)(2,1)}) fusion(f32[2048,2048]{1,0:T(8,128)} %fusion.44, f32[2048,2048]{1,0:T(8,128)} %fusion.45, bf16[2048,2048]{1,0:T(8,128)(2,1)} %all-gather.21.cloned.1.call-done, bf16[2048,2048]{1,0:T(8,128)(2,1)} %all-gather.19.cloned.1.call-done), kind=kOutput, calls=%fused_computation.50 | convolution fusion | flops 17242783744 | bytes 75497472 | tf_op jit(solution)/shard_map/dot_general | solution.py:192
  1012.1 24.3 fusion.43
  1036.5 26.8 %convolution_add_fusion = f32[2048,2048]{1,0:T(8,128)} fusion(f32[2048,2048]{1,0:T(8,128)} %fusion.43, bf16[2048,2048]{1,0:T(8,128)(2,1)} %get-tuple-element.437, bf16[2,2048,2048]{2,1,0:T(8,128)(2,1)} %all-gather.17.cloned.1.call-done), kind=kOutput, calls=%fused_computation.58 | convolution fusion | flops 17184063488 | bytes 50331648 | tf_op jit(solution)/shard_map/dot_general | solution.py:213
  1063.4 151.4 %reduce-scatter.9.cloned.1.call-done = f32[512,2048]{1,0:T(8,128)} async-done(((f32[2048,2048]{1,0:T(8,128)}), f32[512,2048]{1,0:T(8,128)}) %reduce-scatter.9.cloned.1.call-update) | async-done | bytes 4194320 | tf_op jit(solution)/shard_map/reduce_scatter | solution.py:209
  1226.1 23.8 convolution_convert_fusion
  1267.6 22.4 convert_bitcast_fusion
  1290.0 23.7 convert_bitcast_fusion.1
  1319.9 48.9 %copy.190 = bf16[2,2048,2048]{2,0,1:T(2,128)(2,1)} copy(bf16[2,2048,2048]{2,1,0:T(8,128)(2,1)S(1)} %pad_maximum_fusion) | data formatting | bytes 33554432 | tf_op jit(solution)/shard_map/stack | solution.py:199
  1378.8 441.2 %while.28 = (s32[]{:T(128)}, f32[2048,8,64]{0,2,1:T(8,128)}, f32[2048,8,64]{0,2,1:T(8,128)}, f32[4,512,8,64]{1,3,2,0:T(8,128)}, s32[4]{0:T(128)S(1)}, /*index=5*...) while((s32[]{:T(128)}, f32[2048,8,64]{0,2,1:T(8,128)}, ...), condition=%wide.region_13.14_spmd.clone, body=%wide.region_11.13_spmd.clone.sunk | while | flops 5452853248 | bytes 347189568 | solution.py:263
  1384.2 17.4 fusion.189
  1401.6 24.6 multiply_reduce_fusion.5
  1426.2 27.4 %multiply_convert_fusion.6 = bf16[8,512,2048]{2,1,0:T(8,128)(2,1)} fusion(f32[8,512,2048]{2,1,0:T(8,128)} %get-tuple-element.612, f32[8,512,2048]{2,1,0:T(8,128)} %fusion.189, f32[8,512]{1,0:T(8,128)S(1)} %get-tuple-element.613), kind=kLoop, calls=%fused_computation.17.clone.1 | loop fusion | flops 25165824 | bytes 83902464 | tf_op jit(solution)/shard_map/while/body/eval_jaxpr/convert_element_type | solution.py:245
  1453.6 15.8 bitcast_add_fusion.5
  1492.6 17.4 fusion.189
  1510.0 24.6 multiply_reduce_fusion.5
  1534.5 27.4 %multiply_convert_fusion.6 = bf16[8,512,2048]{2,1,0:T(8,128)(2,1)} fusion(f32[8,512,2048]{2,1,0:T(8,128)} %get-tuple-element.612, f32[8,512,2048]{2,1,0:T(8,128)} %fusion.189, f32[8,512]{1,0:T(8,128)S(1)} %get-tuple-element.613), kind=kLoop, calls=%fused_computation.17.clone.1 | loop fusion | flops 25165824 | bytes 83902464 | tf_op jit(solution)/shard_map/while/body/eval_jaxpr/convert_element_type | solution.py:245
  1561.9 17.0 bitcast_add_fusion.5
  1578.9 12.4 bitcast_add_fusion.4
  1603.3 17.4 fusion.189
  1620.7 24.6 multiply_reduce_fusion.5
  1645.3 27.4 %multiply_convert_fusion.6 = bf16[8,512,2048]{2,1,0:T(8,128)(2,1)} fusion(f32[8,512,2048]{2,1,0:T(8,128)} %get-tuple-element.612, f32[8,512,2048]{2,1,0:T(8,128)} %fusion.189, f32[8,512]{1,0:T(8,128)S(1)} %get-tuple-element.613), kind=kLoop, calls=%fused_computation.17.clone.1 | loop fusion | flops 25165824 | bytes 83902464 | tf_op jit(solution)/shard_map/while/body/eval_jaxpr/convert_element_type | solution.py:245
  1672.7 17.0 bitcast_add_fusion.5
  1689.6 12.4 bitcast_add_fusion.4
  1714.1 17.4 fusion.189
  1731.5 24.6 multiply_reduce_fusion.5
  1756.0 27.4 %multiply_convert_fusion.6 = bf16[8,512,2048]{2,1,0:T(8,128)(2,1)} fusion(f32[8,512,2048]{2,1,0:T(8,128)} %get-tuple-element.612, f32[8,512,2048]{2,1,0:T(8,128)} %fusion.189, f32[8,512]{1,0:T(8,128)S(1)} %get-tuple-element.613), kind=kLoop, calls=%fused_computation.17.clone.1 | loop fusion | flops 25165824 | bytes 83902464 | tf_op jit(solution)/shard_map/while/body/eval_jaxpr/convert_element_type | solution.py:245
  1783.4 17.0 bitcast_add_fusion.5
  1800.4 12.4 bitcast_add_fusion.4
  1842.5 13.1 fusion.83
  1866.0 17.0 add_convert_fusion
  1886.1 23.9 convolution_convert_fusion.1
  1910.0 48.5 %subtract_reduce_fusion.1 = (f32[2048,256]{1,0:T(8,128)}, f32[4,2048,256]{2,0,1:T(4,128)}, f32[4,2048,256]{2,0,1:T(4,128)}) fusion(f32[2048,256]{1,0:T(8,128)} %get-tuple-element.457, f32[2048,256]{1,0:T(8,128)} %param.37, f32[4,2048,256]{2,1,0:T(8,128)} %param.47, f32[4,2048,256]{2,1,0:T(8,128)} %param.42, bf16[2048,8,256]{2,0,1:T(8,128)(2,1)} %all-to-all-done.3, ...), kind=kOutput, calls=%fused_computation.74 | convolution fusion | flops 66584608 | bytes 48234528 | tf_op jit(solution)/shard_map/gs,s...->g.../dot_general | solution.py:325
  1996.2 209.1 %all-to-all-done.2 = bf16[2,2048,2048]{2,0,1:T(2,128)(2,1)} async-done(((bf16[2,2048,2048]{2,0,1:T(2,128)(2,1)}), bf16[2,2048,2048]{2,0,1:T(2,128)(2,1)}, u32[]{:S(2)}, u32[]{:S(2)}) %all-to-all-start.2) | async-done | bytes 16777248 | tf_op jit(solution)/shard_map/all_to_all | solution.py:308
  2228.6 27.4 %copy.181 = bf16[3,2048,512]{2,0,1:T(4,128)(2,1)} copy(bf16[3,2048,512]{2,1,0:T(8,128)(2,1)S(1)} %pad_maximum_fusion.1) | data formatting | bytes 12582912 | tf_op jit(solution)/shard_map/stack | solution.py:279
  2270.3 81.1 %subtract_reduce_fusion = (f32[2,256,2048]{2,1,0:T(8,128)}, f32[4,2,256,2048]{3,0,2,1:T(4,128)}, f32[4,2,256,2048]{3,0,2,1:T(4,128)}) fusion(f32[2,256,2048]{2,1,0:T(8,128)} %get-tuple-element.443, f32[2,256,2048]{2,1,0:T(8,128)S(1)} %copy-done.14, f32[4,2,256,2048]{3,2,1,0:T(8,128)} %param.46, f32[4,2,256,2048]{3,2,1,0:T(8,128)} %param.41, ...), kind=kOutput, calls=%fused_computation.47 | convolution fusion | flops 133169184 | bytes 96469024 | tf_op jit(solution)/shard_map/gs,s...->g.../dot_general | solution.py:325
  2351.4 19.2 copy.203
  2370.6 18.8 copy.202
  2389.5 12.1 fusion.111
  2415.0 32.5 %all-to-all-done = bf16[3,2048,512]{2,0,1:T(4,128)(2,1)} async-done(((bf16[3,2048,512]{2,0,1:T(4,128)(2,1)}), bf16[3,2048,512]{2,0,1:T(4,128)(2,1)}, u32[]{:S(2)}, u32[]{:S(2)}) %all-to-all-start) | async-done | bytes 6291488 | tf_op jit(solution)/shard_map/all_to_all | solution.py:302
  2447.5 31.5 %subtract_reduce_fusion.2 = (f32[3,256,512]{2,1,0:T(8,128)}, f32[4,3,256,512]{3,0,2,1:T(4,128)}, f32[4,3,256,512]{3,0,2,1:T(4,128)S(1)}) fusion(f32[3,256,512]{2,1,0:T(8,128)} %get-tuple-element.459, f32[3,256,512]{2,1,0:T(8,128)S(1)} %copy-done.22, f32[4,3,256,512]{3,2,1,0:T(8,128)} %param.44, f32[4,3,256,512]{3,2,1,0:T(8,128)} %param.39, ...), kind=kOutput, calls=%fused_computation.91 | convolution fusion | flops 49938464 | bytes 36175904 | tf_op jit(solution)/shard_map/gs,s...->g.../dot_general | solution.py:325
  2506.2 111.0 %all-reduce.2.cloned.1.call-done = f32[4,2,2048]{2,1,0:T(2,128)} async-done(((f32[4,2,2048]{2,1,0:T(2,128)}), f32[4,2,2048]{2,1,0:T(2,128)}) %all-reduce.2.cloned.1.call-update) | async-done | bytes 65552 | tf_op jit(solution)/shard_map/psum | solution.py:300
  (324 shorter events, 334.5 us)
Async XLA Ops:
  7.2 71.1 %all-gather.11.cloned.1.call-start = ((), (), s32[]{:S(2)}) async-start(), calls=%async_computation.9 | async-start | bytes 7077888 | tf_op jit(solution)/shard_map/all_gather | solution.py:105
  11.1 155.3 %all-gather.9.cloned.1.call-start = ((), (), s32[]{:S(2)}) async-start(), calls=%async_computation.8 | async-start | bytes 10485760 | tf_op jit(solution)/shard_map/all_gather | solution.py:113
  11.6 8.2 copy-start.59
  12.3 7.6 copy-start.51
  14.1 378.5 %all-gather.13.cloned.1.call-start = ((), (), s32[]{:S(2)}) async-start(), calls=%async_computation.10 | async-start | bytes 2359296 | tf_op jit(solution)/shard_map/all_gather | solution.py:105
  15.2 544.4 %reduce-scatter.5.cloned.1.call-start = ((), (), s32[]{:S(2)}) async-start(), calls=%async_computation.11 | async-start | bytes 20971520 | tf_op jit(solution)/shard_map/reduce_scatter | solution.py:161
  15.2 68.4 %copy-start.67 = (f32[32]{0:T(128)}, f32[32]{0:T(128)S(1)}, u32[]{:S(2)}) copy-start(f32[32]{0:T(128)S(1)} %negate_power_fusion) | copy-start | bytes 388
  17.1 66.6 %copy-start.61 = (s32[2048]{0:T(1024)}, s32[2048]{0:T(1024)S(1)}, u32[]{:S(2)}) copy-start(s32[2048]{0:T(1024)S(1)} %convert_reduce_fusion) | copy-start | bytes 24580
  166.4 7.8 copy-start.32
  166.4 7.8 copy-start.71
  183.7 9.4 copy-start.41
  386.7 5.9 copy-start.1
  405.6 153.9 %copy-start.7 = (bf16[512,2048]{1,0:T(8,128)(2,1)S(1)}, bf16[512,2048]{1,0:T(8,128)(2,1)}, u32[]{:S(2)}) copy-start(bf16[512,2048]{1,0:T(8,128)(2,1)} %param.29) | copy-start | bytes 6291460
  405.6 307.6 %all-gather.17.cloned.1.call-start = ((), (), s32[]{:S(2)}) async-start(), calls=%async_computation.13 | async-start | bytes 18874368 | tf_op jit(solution)/shard_map/all_gather | solution.py:105
  413.1 151.2 %copy-start.48 = (f32[1,2048]{1,0:T(1,128)S(1)}, f32[1,2048]{1,0:T(1,128)}, u32[]{:S(2)}) copy-start(f32[1,2048]{1,0:T(1,128)} %get-tuple-element.470) | copy-start | bytes 24580
  413.1 387.5 %all-gather.15.cloned.1.call-start = ((), (), s32[]{:S(2)}) async-start(), calls=%async_computation.12 | async-start | bytes 10485760 | tf_op jit(solution)/shard_map/all_gather | solution.py:169
  566.1 323.9 %all-gather.21.cloned.1.call-start = ((), (), s32[]{:S(2)}) async-start(), calls=%async_computation.16 | async-start | bytes 10485760 | tf_op jit(solution)/shard_map/all_gather | solution.py:114
  566.8 408.4 %all-gather.19.cloned.1.call-start = ((), (), s32[]{:S(2)}) async-start(), calls=%async_computation.14 | async-start | bytes 9437184 | tf_op jit(solution)/shard_map/all_gather | solution.py:105
  568.8 646.0 %reduce-scatter.9.cloned.1.call-start = ((), (), s32[]{:S(2)}) async-start(), calls=%async_computation.17 | async-start | bytes 20971520 | tf_op jit(solution)/shard_map/reduce_scatter | solution.py:209
  800.6 24.5 copy-start.70
  800.6 24.5 copy-start.72
  1063.3 151.5 %copy-start.49 = (f32[1,2048]{1,0:T(1,128)S(1)}, f32[1,2048]{1,0:T(1,128)}, u32[]{:S(2)}) copy-start(f32[1,2048]{1,0:T(1,128)} %get-tuple-element.470) | copy-start | bytes 24580
  1063.3 151.5 %copy-start.57 = (f32[512]{0:T(512)S(1)}, f32[512]{0:T(512)}, u32[]{:S(2)}) copy-start(f32[512]{0:T(512)} %copy-done.56) | copy-start | bytes 6148
  1063.3 157.3 %copy-start.12 = (bf16[512,2048]{1,0:T(8,128)(2,1)S(1)}, bf16[512,2048]{1,0:T(8,128)(2,1)}, u32[]{:S(2)}) copy-start(bf16[512,2048]{1,0:T(8,128)(2,1)} %param.30) | copy-start | bytes 6291460
  1063.3 305.5 %all-gather.23.cloned.1.call-start = ((), (), s32[]{:S(2)}) async-start(), calls=%async_computation.18 | async-start | bytes 10485760 | tf_op jit(solution)/shard_map/all_gather | solution.py:223
  1214.8 5.8 copy-start.5
  1214.8 5.9 copy-start.9
  1261.2 575.5 %all-to-all-start.3 = ((bf16[2048,8,256]{2,0,1:T(8,128)(2,1)}), bf16[2048,8,256]{2,0,1:T(8,128)(2,1)}, u32[]{:S(2)}, u32[]{:S(2)}) async-start(bf16[2048,8,256]{2,0,1:T(8,128)(2,1)} %copy.195), calls=%async_computation.7 | async-start | bytes 16777216 | tf_op jit(solution)/shard_map/all_to_all | solution.py:311
  1368.8 10.0 copy-start.2
  1368.8 10.0 copy-start.40
  1368.8 10.0 copy-start.42
  1469.3 12.1 copy-start
  1578.9 13.3 copy-start
  1689.6 13.3 copy-start
  1800.4 13.3 copy-start
  1836.8 368.5 %all-to-all-start.2 = ((bf16[2,2048,2048]{2,0,1:T(2,128)(2,1)}), bf16[2,2048,2048]{2,0,1:T(2,128)(2,1)}, u32[]{:S(2)}, u32[]{:S(2)}) async-start(bf16[2,2048,2048]{2,0,1:T(2,128)(2,1)} %copy.190), calls=%async_computation.6 | async-start | bytes 33554432 | tf_op jit(solution)/shard_map/all_to_all | solution.py:308
  1842.5 651.6 %reduce-scatter.11.cloned.1.call-start = ((), (), s32[]{:S(2)}) async-start(), calls=%async_computation.19 | async-start | bytes 10485760 | tf_op jit(solution)/shard_map/reduce_scatter | solution.py:291
  1842.5 13.1 copy-start.26
  1883.1 614.9 %reduce-scatter.7.cloned.1.call-start = ((), (), s32[]{:S(2)}) async-start(), calls=%async_computation.15 | async-start | bytes 10485760 | tf_op jit(solution)/shard_map/reduce_scatter | solution.py:176
  1958.5 8.6 copy-start.16
  1967.2 4.9 copy-start.11
  1972.1 17.3 slice-start
  1974.8 14.6 slice-start.1
  1996.2 214.3 %copy-start.27 = (bf16[2048,8,64]{0,2,1:T(8,128)(2,1)S(1)}, bf16[2048,8,64]{0,2,1:T(8,128)(2,1)}, u32[]{:S(2)}) copy-start(bf16[2048,8,64]{0,2,1:T(8,128)(2,1)} %get-tuple-element.465) | copy-start | bytes 6291460
  2205.3 53.3 %all-to-all-start.1 = ((bf16[512,8,256]{2,0,1:T(8,128)(2,1)}), bf16[512,8,256]{2,0,1:T(8,128)(2,1)}, u32[]{:S(2)}, u32[]{:S(2)}) async-start(bf16[512,8,256]{2,0,1:T(8,128)(2,1)} %bitcast.236), calls=%async_computation.5 | async-start | bytes 4194304 | tf_op jit(solution)/shard_map/all_to_all | solution.py:305
  2210.4 8.7 copy-start.35
  2219.1 8.7 copy-start.36
  2256.0 8.4 copy-start.18
  2258.6 188.8 %all-to-all-start = ((bf16[3,2048,512]{2,0,1:T(4,128)(2,1)}), bf16[3,2048,512]{2,0,1:T(4,128)(2,1)}, u32[]{:S(2)}, u32[]{:S(2)}) async-start(bf16[3,2048,512]{2,0,1:T(4,128)(2,1)} %copy.181), calls=%async_computation.4 | async-start | bytes 16777216 | tf_op jit(solution)/shard_map/all_to_all | solution.py:302
  2264.4 352.8 %all-reduce.2.cloned.1.call-start = ((), (), s32[]{:S(2)}) async-start(), calls=%async_computation.20 | async-start | bytes 131072 | tf_op jit(solution)/shard_map/psum | solution.py:300
  2264.4 5.9 copy-start.14
  2351.4 19.2 copy-start.13
  2389.5 12.1 copy-start.34
  2389.5 12.1 copy-start.43
  2389.5 12.1 copy-start.73
  2411.9 35.5 %copy-start.22 = (f32[3,256,512]{2,1,0:T(8,128)S(1)}, f32[3,256,512]{2,1,0:T(8,128)}, u32[]{:S(2)}) copy-start(f32[3,256,512]{2,1,0:T(8,128)} %param.34) | copy-start | bytes 4718596
  2486.5 4.6 copy-start.23
  2486.5 4.6 copy-start.37
  2486.5 4.6 copy-start.38
  2497.9 119.4 %copy-start.47 = (f32[2,2048]{1,0:T(2,128)S(1)}, f32[2,2048]{1,0:T(2,128)}, u32[]{:S(2)}) copy-start(f32[2,2048]{1,0:T(2,128)} %param.38) | copy-start | bytes 49156
  2497.9 119.4 %copy-start.53 = (f32[2,2048]{1,0:T(2,128)S(1)}, f32[2,2048]{1,0:T(2,128)}, u32[]{:S(2)}) copy-start(f32[2,2048]{1,0:T(2,128)} %broadcast_multiply_fusion.13) | copy-start | bytes 49156
  2497.9 119.4 %copy-start.54 = (f32[4,2,2048]{2,1,0:T(2,128)S(1)}, f32[4,2,2048]{2,1,0:T(2,128)}, u32[]{:S(2)}) copy-start(f32[4,2,2048]{2,1,0:T(2,128)} %param.48) | copy-start | bytes 196612
  2497.9 119.4 %copy-start.55 = (f32[4,2,2048]{2,1,0:T(2,128)S(1)}, f32[4,2,2048]{2,1,0:T(2,128)}, u32[]{:S(2)}) copy-start(f32[4,2,2048]{2,1,0:T(2,128)} %param.43) | copy-start | bytes 196612
  2497.9 121.1 %copy-start.66 = (f32[2,2048]{1,0:T(2,128)S(1)}, f32[2,2048]{1,0:T(2,128)}, u32[]{:S(2)}) copy-start(f32[2,2048]{1,0:T(2,128)} %param.53) | copy-start | bytes 49156
  (33 other events, 90.9 us)
Sparse Core Ops, SparseCore 0:
  11.2 67.1 all-gather.10
  80.8 85.5 all-gather.8
  168.6 31.1 all-gather.12
  405.7 153.7 reduce-scatter.4
  561.6 151.6 all-gather.16
  715.5 85.0 all-gather.14
  802.5 87.4 all-gather.20
  892.1 83.0 all-gather.18
  1063.5 151.3 reduce-scatter.8
  1223.4 87.4 all-gather.22
  1883.2 85.6 reduce-scatter.10
  1971.8 86.3 reduce-scatter.6
  2498.0 119.2 all-reduce.1
where the time goes:
time: 2640 us; the launch traced here: 2630 us
  waiting for transfers between devices  1150 us (44%)
  matrix products  944 us (36%)
  other arithmetic  277 us (10%)
  local copies, waits for them, and re-layouts  207 us (8%)
    all_gather x4, waiting for transfers between devices, on_device(): lax.all_gather(as_sent(rounded), 'dp', axis=1, tiled=True)  288 us
    all_to_all x1, waiting for transfers between devices, on_device(): lax.all_to_all(gate_grad.astype(jnp.bfloat16), 'dp', split_axis=1, concat...  209 us
    dot_general x4, matrix products, on_device(): jnp.einsum('gs,s...->g...', picker, member, precision=lax.Precision.HIGHEST)  170 us
    dot_general x8, matrix products, scores_of(): jnp.einsum('qhd,khd->hqk', query_block, keys_all, preferred_element_type=...  157 us
    reduce_scatter x1, waiting for transfers between devices, on_device(): lax.psum_scatter(lax.dot_general(gate_grad_low, gate_back[0], contract_co...  151 us
    reduce_scatter x1, waiting for transfers between devices, on_device(): lax.psum_scatter(jnp.dot(slab, out_full, preferred_element_type=jnp.float...  146 us
    psum x1, waiting for transfers between devices, on_device(): gain_grad = lax.psum(gain_slots, ('dp', 'tensor'))  111 us
    convert_element_type x4, other arithmetic, back_block(): score_grad = (probs * (prob_grad - center)).astype(jnp.bfloat16)  110 us
  transfers between devices with their start and end apart: 17, of which 12 were waited for; matrix products, arithmetic and copies ran while one was open for 50% of the time, Pallas kernels for 0%

commit v1 on v0

v1 whole, which is shorter than its diff:
```python
import functools

import jax
import jax.numpy as jnp
from jax import lax
from jax.experimental import pallas as pl
from jax.experimental.pallas import tpu as pltpu
from jax.sharding import PartitionSpec as P

NT = (((1,), (1,)), ((), ()))
TN = (((0,), (0,)), ((), ()))
NEG = -1e30
LANES = 128


def swap_halves(u):
    lane = lax.broadcasted_iota(jnp.int32, u.shape, 1)
    return jnp.where(lane % 64 < 32, pltpu.roll(u, 96, 1), pltpu.roll(u, 32, 1))


def head_parts(u):
    lane = lax.broadcasted_iota(jnp.int32, u.shape, 1)
    zero = jnp.zeros_like(u)
    return jnp.where(lane < 64, u, zero), jnp.where(lane < 64, zero, u)


def fwd_kernel(tq, tk, info, q_ref, k_ref, v_ref, cos_ref, sin_ref, lo_ref, hi_ref,
               o_ref, qr_ref, kr_ref, vr_ref, lse_ref, q2, v2, m_s, l_s, acc):
    rows = q_ref.shape[0]
    step = 256
    def prep(i, c):
        at = pl.ds(pl.multiple_of(i * step, step), step)
        cos, sin = cos_ref[at, :], sin_ref[at, :]
        q = q_ref[at, :]
        q = (q * cos + swap_halves(q) * sin).astype(jnp.bfloat16) * jnp.bfloat16(0.125)
        k = k_ref[at, :]
        k = (k * cos + swap_halves(k) * sin).astype(jnp.bfloat16)
        v = v_ref[at, :].astype(jnp.bfloat16)
        qr_ref[at, :] = q
        kr_ref[at, :] = k
        vr_ref[at, :] = v
        q2[0, at, :], q2[1, at, :] = head_parts(q)
        v2[0, at, :], v2[1, at, :] = head_parts(v)
        return c
    lax.fori_loop(0, rows // step, prep, 0)

    def q_tile(i, c):
        at = pl.ds(pl.multiple_of(i * tq, tq), tq)
        m_s[...] = jnp.full_like(m_s, -1e29)
        l_s[...] = jnp.zeros_like(l_s)
        acc[...] = jnp.zeros_like(acc)
        first = info[0, i] // tk
        last = (info[3, i] + tk - 1) // tk

        def tile(j, masked):
            ks = pl.multiple_of(j * tk, tk)
            kat = pl.ds(ks, tk)
            k = kr_ref[kat, :]
            if masked:
                key = lax.broadcasted_iota(jnp.int32, (tq, tk), 1) + ks
                ok = (key >= lo_ref[at, :]) & (key < hi_ref[at, :])
            for h in range(2):
                s = lax.dot_general(q2[h, at, :], k, NT, preferred_element_type=jnp.float32)
                if masked:
                    s = jnp.where(ok, s, NEG)
                m_old = m_s[h]
                m_new = jnp.maximum(m_old, jnp.max(s, axis=1, keepdims=True))
                p = jnp.exp(s - m_new[:, :1])
                alpha = jnp.exp(m_old - m_new)
                l_s[h] = alpha * l_s[h] + jnp.sum(p, axis=1, keepdims=True)
                acc[h] = acc[h] * alpha + jnp.dot(
                    p.astype(jnp.bfloat16), v2[h, kat, :], preferred_element_type=jnp.float32)
                m_s[h] = m_new

        def kv_tile(j, c):
            ks = j * tk
            full = (info[1, i] <= ks) & (info[2, i] >= ks + tk)
            @pl.when(full)
            def _():
                tile(j, False)
            @pl.when(jnp.logical_not(full))
            def _():
                tile(j, True)
            return c
        lax.fori_loop(first, last, kv_tile, 0)
        l0, l1 = l_s[0], l_s[1]
        o_ref[at, :] = (acc[0] / l0 + acc[1] / l1).astype(jnp.bfloat16)
        lane = lax.broadcasted_iota(jnp.int32, (tq, LANES), 1)
        lse = jnp.where(lane < 64, m_s[0] + jnp.log(l0), m_s[1] + jnp.log(l1))
        flat = lse.T
        lse_ref[0, 0:1, at] = flat[0:1, :]
        lse_ref[0, 1:2, at] = flat[64:65, :]
        return c
    lax.fori_loop(0, rows // tq, q_tile, 0)


def attn_fwd(info, proj, cos, sin, lo, hi, tq, tk):
    rows, width = proj.shape
    pairs = width // 3 // LANES
    full = lambda p: (0, 0)
    blk = (rows, LANES)
    outs = [jax.ShapeDtypeStruct((rows, pairs * LANES), jnp.bfloat16)] * 4 + [
        jax.ShapeDtypeStruct((pairs, 2, rows), jnp.float32)]
    pair_spec = pl.BlockSpec(blk, lambda p: (0, p))
    area = rows * rows * pairs * 2 * 0.6
    return pl.pallas_call(
        functools.partial(fwd_kernel, tq, tk),
        out_shape=outs,
        grid=(pairs,),
        in_specs=[
            pl.BlockSpec(memory_space=pltpu.SMEM),
            pl.BlockSpec(blk, lambda p: (0, p)),
            pl.BlockSpec(blk, lambda p: (0, p + pairs)),
            pl.BlockSpec(blk, lambda p: (0, p + 2 * pairs)),
            pl.BlockSpec(blk, full), pl.BlockSpec(blk, full),
            pl.BlockSpec((rows, 1), full), pl.BlockSpec((rows, 1), full)],
        out_specs=[pair_spec] * 4 + [pl.BlockSpec((1, 2, rows), lambda p: (p, 0, 0))],
        scratch_shapes=[pltpu.VMEM((2, rows, LANES), jnp.bfloat16), pltpu.VMEM((2, rows, LANES), jnp.bfloat16),
                        pltpu.VMEM((2, tq, LANES), jnp.float32), pltpu.VMEM((2, tq, LANES), jnp.float32),
                        pltpu.VMEM((2, tq, LANES), jnp.float32)],
        compiler_params=pltpu.CompilerParams(vmem_limit_bytes=48 << 20),
        cost_estimate=pl.CostEstimate(flops=int(4 * area * 64), transcendentals=int(area), bytes_accessed=rows * width * 4),
        name="attn_fwd",
    )(info, proj, proj, proj, cos, sin, lo, hi)


def bwd_kernel(tq, tk, info, q_ref, k_ref, v_ref, o_ref, do_ref, lse_ref, cos_ref, sin_ref, lo_ref, hi_ref,
               dq_ref, dk_ref, dv_ref, q2, k2, v2, g2, delta, dq_acc, dk_acc, dv_acc):
    rows = q_ref.shape[0]
    step = 256
    def prep(i, c):
        at = pl.ds(pl.multiple_of(i * step, step), step)
        q2[0, at, :], q2[1, at, :] = head_parts(q_ref[at, :])
        k2[0, at, :], k2[1, at, :] = head_parts(k_ref[at, :])
        v2[0, at, :], v2[1, at, :] = head_parts(v_ref[at, :])
        g = do_ref[at, :]
        g2[0, at, :], g2[1, at, :] = head_parts(g)
        prod = (g.astype(jnp.float32) * o_ref[at, :].astype(jnp.float32)).T
        delta[0:1, at] = jnp.sum(prod[:64], axis=0, keepdims=True)
        delta[1:2, at] = jnp.sum(prod[64:], axis=0, keepdims=True)
        dq_acc[at, :] = jnp.zeros((step, LANES), jnp.float32)
        return c
    lax.fori_loop(0, rows // step, prep, 0)

    def k_tile(j, c):
        ks = pl.multiple_of(j * tk, tk)
        kat = pl.ds(ks, tk)
        dk_acc[...] = jnp.zeros_like(dk_acc)
        dv_acc[...] = jnp.zeros_like(dv_acc)
        first = info[4, j] // tq
        last = (info[5, j] + tq - 1) // tq

        def tile(i, masked):
            at = pl.ds(pl.multiple_of(i * tq, tq), tq)
            if masked:
                key = lax.broadcasted_iota(jnp.int32, (tk, tq), 0) + ks
                ok = (key >= lo_ref[0:1, at]) & (key < hi_ref[0:1, at])
            for h in range(2):
                kh, qh, gh = k2[h, kat, :], q2[h, at, :], g2[h, at, :]
                s = lax.dot_general(kh, qh, NT, preferred_element_type=jnp.float32)
                if masked:
                    s = jnp.where(ok, s, NEG)
                p = jnp.exp(s - lse_ref[0, h:h + 1, at])
                dp = lax.dot_general(v2[h, kat, :], gh, NT, preferred_element_type=jnp.float32)
                ds = (p * (dp - delta[h:h + 1, at])).astype(jnp.bfloat16)
                dv_acc[...] += jnp.dot(p.astype(jnp.bfloat16), gh, preferred_element_type=jnp.float32)
                dk_acc[...] += jnp.dot(ds, qh, preferred_element_type=jnp.float32)
                dq_acc[at, :] += lax.dot_general(ds, kh, TN, preferred_element_type=jnp.float32)

        def q_loop(i, c):
            full = (info[1, i] <= ks) & (info[2, i] >= ks + tk)
            @pl.when(full)
            def _():
                tile(i, False)
            @pl.when(jnp.logical_not(full))
            def _():
                tile(i, True)
            return c
        lax.fori_loop(first, last, q_loop, 0)
        cos, sin = cos_ref[kat, :], sin_ref[kat, :]
        dk = dk_acc[...]
        dk_ref[kat, :] = (dk * cos - swap_halves(dk) * sin).astype(jnp.bfloat16)
        dv_ref[kat, :] = dv_acc[...].astype(jnp.bfloat16)
        return c
    lax.fori_loop(0, rows // tk, k_tile, 0)

    def finish(i, c):
        at = pl.ds(pl.multiple_of(i * step, step), step)
        dq = dq_acc[at, :] * 0.125
        dq_ref[at, :] = (dq * cos_ref[at, :] - swap_halves(dq) * sin_ref[at, :]).astype(jnp.bfloat16)
        return c
    lax.fori_loop(0, rows // step, finish, 0)


def attn_bwd(info, q, k, v, o, do, lse, cos, sin, lo, hi, tq, tk):
    rows, width = q.shape
    pairs = width // LANES
    full = lambda p: (0, 0)
    blk = (rows, LANES)
    pair_spec = pl.BlockSpec(blk, lambda p: (0, p))
    area = rows * rows * pairs * 2 * 0.6
    return pl.pallas_call(
        functools.partial(bwd_kernel, tq, tk),
        out_shape=[jax.ShapeDtypeStruct((rows, width), jnp.bfloat16)] * 3,
        grid=(pairs,),
        in_specs=[pl.BlockSpec(memory_space=pltpu.SMEM)] + [pair_spec] * 5 + [
            pl.BlockSpec((1, 2, rows), lambda p: (p, 0, 0)),
            pl.BlockSpec(blk, full), pl.BlockSpec(blk, full),
            pl.BlockSpec((1, rows), full), pl.BlockSpec((1, rows), full)],
        out_specs=[pair_spec] * 3,
        scratch_shapes=[pltpu.VMEM((2, rows, LANES), jnp.bfloat16)] * 4 + [
            pltpu.VMEM((2, rows), jnp.float32), pltpu.VMEM((rows, LANES), jnp.float32),
            pltpu.VMEM((tk, LANES), jnp.float32), pltpu.VMEM((tk, LANES), jnp.float32)],
        compiler_params=pltpu.CompilerParams(vmem_limit_bytes=48 << 20),
        cost_estimate=pl.CostEstimate(flops=int(10 * area * 64), transcendentals=int(area), bytes_accessed=rows * width * 16),
        name="attn_bwd",
    )(info, q, k, v, o, do, lse, cos, sin, lo, hi)


def layout_of(seq, block, tq, tk):
    rows = seq.shape[0]
    code = seq * 8 + block
    lo = jnp.sum((seq[None, :] < seq[:, None]).astype(jnp.int32), axis=1)
    hi = jnp.sum((code[None, :] <= code[:, None]).astype(jnp.int32), axis=1)
    lt, ht = lo.reshape(-1, tq), hi.reshape(-1, tq)
    start = jnp.arange(rows // tk, dtype=jnp.int32)[:, None] * tk
    qlo = jnp.sum((hi[None, :] <= start).astype(jnp.int32), axis=1)
    qhi = jnp.sum((lo[None, :] < start + tk).astype(jnp.int32), axis=1)
    info = jnp.stack([lt.min(1), lt.max(1), ht.min(1), ht.max(1), qlo, qhi]) if tq == tk else None
    return lo, hi, info


def rope_tables(lo, base=130000.0):
    rows = lo.shape[0]
    where_at = (jnp.arange(rows, dtype=jnp.int32) - lo).astype(jnp.float32)
    inverse = base ** (-(jnp.arange(32, dtype=jnp.float32) * 2.0 / 64))
    ang = where_at[:, None] * inverse[None, :]
    cos, sin = jnp.cos(ang), jnp.sin(ang)
    return jnp.concatenate([cos] * 4, axis=1), jnp.concatenate([-sin, sin, -sin, sin], axis=1)


HDIM = 64
GROUPS = 4
STEP = 4

norm_eps = 1e-05
beta_first = 0.9
beta_second = 0.95
adam_eps = 1e-08
outer_rate = 0.7
outer_beta = 0.9
inner_rates = (0.04, 0.6, 0.04, 0.02, 0.35)
decays = (0.1, 0.1, 0.1, 0.1, 0.0)
fix_first = 1.0 - beta_first**STEP
fix_second = 1.0 - beta_second**STEP
TILE = 512


def normed(field_rows, gain_row):
    factor = lax.rsqrt(jnp.mean(field_rows * field_rows, axis=-1, keepdims=True) + norm_eps)
    scaled = field_rows * factor
    return ((scaled * gain_row).astype(jnp.bfloat16), scaled, factor)


def norm_back(upstream, scaled, factor, gain_row):
    inside = upstream * gain_row
    return factor * (inside - scaled * jnp.mean(inside * scaled, axis=-1, keepdims=True))


def update(weight, gradient, first_old, second_old, outer_old, step_rate, decay_rate):
    first_new = beta_first * first_old + (1.0 - beta_first) * gradient
    second_new = beta_second * second_old + (1.0 - beta_second) * gradient * gradient
    ratio = first_new / fix_first / (jnp.sqrt(second_new / fix_second) + adam_eps)
    change = step_rate * (jnp.mean(ratio, axis=0) + decay_rate * weight)
    outer_new = outer_beta * outer_old + change
    master = weight - outer_rate * (change + outer_beta * outer_new)
    return [first_new, second_new, change, outer_new, master, master.astype(jnp.bfloat16)]


def opt_kernel(per, turned, rate, decay, order, *refs):
    (recv, first, second, weight, outer), (first_new, second_new, delta, outer_new, master, low) = refs[:5], refs[-6:]
    rows, cols = weight.shape[-2:]
    step_r, step_c = min(rows, 16), min(cols, 256)
    if turned:
        step_r, step_c = min(rows, 128), min(cols, 128)
    lead = (0,) * (len(weight.shape) - 2)

    def chunk(i, carry):
        r = pl.multiple_of((i // (cols // step_c)) * step_r, step_r)
        c = pl.multiple_of((i % (cols // step_c)) * step_c, step_c)
        at = (pl.ds(r, step_r), pl.ds(c, step_c))
        w = weight[lead + at]
        total = jnp.zeros_like(w)
        for g in range(GROUPS):
            grad = None
            for j in range(per):
                source = order[g * per + j]
                if turned:
                    part = recv[source, pl.ds(c, step_c), pl.ds(r, step_r)].astype(jnp.float32)
                else:
                    part = recv[(source,) + at].astype(jnp.float32)
                grad = part if grad is None else grad + part
            if turned:
                grad = grad.T
            m = beta_first * first[(g,) + lead + at] + (1.0 - beta_first) * grad
            v = beta_second * second[(g,) + lead + at] + (1.0 - beta_second) * grad * grad
            first_new[(g,) + lead + at] = m
            second_new[(g,) + lead + at] = v
            total = total + m / (jnp.sqrt(v * (1.0 / fix_second)) + adam_eps)
        change = rate * (total * (1.0 / (fix_first * GROUPS)) + decay * w)
        moved = outer_beta * outer[lead + at] + change
        fresh = w - outer_rate * (change + outer_beta * moved)
        delta[lead + at] = change
        outer_new[lead + at] = moved
        master[lead + at] = fresh
        low[lead + at] = fresh.astype(jnp.bfloat16)
        return carry

    lax.fori_loop(0, (rows // step_r) * (cols // step_c), chunk, 0)


def optimize(order, recv, weight, first, second, outer, position, turned=False, member=None, before=None):
    sources = recv.shape[0]
    stacked = weight.ndim == 3
    rows, cols = weight.shape[-2:]
    members = weight.shape[0] if stacked and member is None else 1
    base = member or 0
    area = 65536
    if turned:
        br, bc = max(128, min(rows, area // cols)), cols
    else:
        br, bc = max(16, min(rows, area // cols)), cols
    blocks = rows // br
    lead = (1,) if stacked else ()

    def pick(m):
        return (base + m,) if stacked else ()

    if turned:
        recv_spec = pl.BlockSpec((sources, bc, br), lambda m, i: (0, 0, i))
    else:
        recv_spec = pl.BlockSpec((sources, br, bc), lambda m, i: (0, i, m))
    one = pl.BlockSpec(lead + (br, bc), lambda m, i: pick(m) + (i, 0))
    many = pl.BlockSpec((GROUPS,) + lead + (br, bc), lambda m, i: (0,) + pick(m) + (i, 0))
    f32 = jnp.float32
    outs = [
        jax.ShapeDtypeStruct(first.shape, f32),
        jax.ShapeDtypeStruct(first.shape, f32),
        jax.ShapeDtypeStruct(weight.shape, f32),
        jax.ShapeDtypeStruct(weight.shape, f32),
        jax.ShapeDtypeStruct(weight.shape, f32),
        jax.ShapeDtypeStruct(weight.shape, jnp.bfloat16),
    ]
    operands = [order, recv, first, second, weight, outer]
    specs = [pl.BlockSpec(memory_space=pltpu.SMEM), recv_spec, many, many, one, one]
    aliases = {}
    if before is not None:
        aliases = {len(operands) + k: k for k in range(6)}
        operands += list(before)
        specs += [pl.BlockSpec(memory_space=pl.ANY)] * 6
    count = members * rows * cols
    return pl.pallas_call(
        functools.partial(
            opt_kernel, sources // GROUPS, turned, inner_rates[position], decays[position]
        ),
        out_shape=outs,
        grid=(members, blocks),
        in_specs=specs,
        out_specs=[many, many, one, one, one, one],
        input_output_aliases=aliases,
        compiler_params=pltpu.CompilerParams(vmem_limit_bytes=40 << 20),
        cost_estimate=pl.CostEstimate(
            flops=60 * count, transcendentals=8 * count, bytes_accessed=(86 + 2 * sources) * count
        ),
        name="optimize",
    )(*operands)


def dot(left, right):
    return jnp.dot(left, right, preferred_element_type=jnp.float32)


def dot_cols(left, right):
    return lax.dot_general(left, right, (((1,), (1,)), ((), ())), preferred_element_type=jnp.float32)


def dot_rows(left, right):
    return lax.dot_general(left, right, (((0,), (0,)), ((), ())), preferred_element_type=jnp.float32)


def gather_rows(part, axis):
    return lax.all_gather(part, axis, axis=0, tiled=True)


def spread_rows(part):
    count = lax.axis_size("tensor")
    copies = jnp.broadcast_to(part[None], (count,) + part.shape)
    return lax.all_to_all(copies, "tensor", split_axis=0, concat_axis=0).reshape((-1,) + part.shape[1:])


def sum_rows(part):
    count = lax.axis_size("tensor")
    blocks = part.reshape((count, part.shape[0] // count) + part.shape[1:])
    return jnp.sum(lax.all_to_all(blocks, "tensor", split_axis=0, concat_axis=0).astype(jnp.float32), axis=0)


def scatter_rows(part):
    return lax.psum_scatter(part, "tensor", scatter_dimension=0, tiled=True).astype(jnp.float32)


def to_owners(grad):
    count = lax.axis_size("dp")
    blocks = grad.astype(jnp.bfloat16).reshape((count, grad.shape[0] // count) + grad.shape[1:])
    return lax.all_to_all(blocks, "dp", split_axis=0, concat_axis=0)


def on_device(
    tokens,
    cotangent,
    seq_ids,
    block_ids,
    groups,
    qkv_weight,
    out_weight,
    gate_weight,
    down_weight,
    norm_gains,
    qkv_first,
    out_first,
    gate_first,
    down_first,
    gains_first,
    qkv_second,
    out_second,
    gate_second,
    down_second,
    gains_second,
    qkv_outer,
    out_outer,
    gate_outer,
    down_outer,
    gains_outer,
):
    bf16 = jnp.bfloat16
    field_in = tokens.astype(jnp.float32)
    normed_one, scaled_one, factor_one = normed(field_in, norm_gains[0])
    normed_all = spread_rows(normed_one)
    qkv_full = gather_rows(
        jnp.concatenate([qkv_weight[m].astype(bf16) for m in range(3)], axis=1), "dp"
    )
    out_full = gather_rows(out_weight.T.astype(bf16), "dp")
    wide = gate_weight.shape[2]
    gate_full = gather_rows(gate_weight[0].astype(bf16), "dp")
    up_full = gather_rows(gate_weight[1].astype(bf16), "dp")
    down_full = gather_rows(down_weight.T.astype(bf16), "dp")
    cotan_all = spread_rows(lax.optimization_barrier((cotangent, normed_all))[0])

    lo, hi, info = layout_of(seq_ids, block_ids, TILE, TILE)
    cosine, sine_table = rope_tables(lo)
    order = jnp.argsort(groups, stable=True).astype(jnp.int32)

    projected = dot(normed_all, qkv_full)
    mixed_all, queries, keys_all, values_all, logsums = attn_fwd(
        info, projected, cosine, sine_table, lo[:, None], hi[:, None], TILE, TILE
    )
    attn_rows = sum_rows(dot_cols(mixed_all, out_full).astype(bf16))
    residual = field_in + attn_rows
    normed_two, scaled_two, factor_two = normed(residual, norm_gains[1])
    ffn_input = gather_rows(normed_two, "tensor")
    gate_pre = dot(ffn_input, gate_full)
    up_pre = dot(ffn_input, up_full)
    sigmoid_gate = jax.nn.sigmoid(gate_pre)
    swish = gate_pre * sigmoid_gate
    hidden = (swish * up_pre).astype(bf16)
    down_recv = to_owners(dot_rows(cotan_all, hidden))
    ffn_part = scatter_rows(dot_cols(hidden, down_full).astype(bf16))
    layer_out = (residual + ffn_part).astype(bf16)
    hidden_grad = dot(cotan_all, down_full)
    gate_grad_low = (
        hidden_grad * up_pre * sigmoid_gate * (1.0 + gate_pre * (1.0 - sigmoid_gate))
    ).astype(bf16)
    up_grad_low = (hidden_grad * swish).astype(bf16)
    ffn_back_rows = scatter_rows(
        (dot_cols(gate_grad_low, gate_full) + dot_cols(up_grad_low, up_full)).astype(bf16)
    )
    gate_recv = to_owners(dot_rows(ffn_input, gate_grad_low))
    up_recv = to_owners(dot_rows(ffn_input, up_grad_low))
    cotan_rows = cotangent.astype(jnp.float32)
    resid_grad = cotan_rows + norm_back(ffn_back_rows, scaled_two, factor_two, norm_gains[1])
    gain_two = jnp.sum(ffn_back_rows * scaled_two, axis=0)
    resid_all = gather_rows(resid_grad.astype(bf16), "tensor")
    mixed_grad = dot(resid_all, out_full).astype(bf16)
    out_recv = to_owners(dot_rows(resid_all, mixed_all))
    raw_grads = attn_bwd(
        info, queries, keys_all, values_all, mixed_all, mixed_grad, logsums,
        cosine, sine_table, lo[None], hi[None], TILE, TILE,
    )
    raw_all = jnp.concatenate(raw_grads, axis=1)
    in_grad_rows = scatter_rows(dot_cols(raw_all, qkv_full).astype(bf16))
    qkv_recv = to_owners(dot_rows(normed_all, raw_all))
    tokens_grad = resid_grad + norm_back(in_grad_rows, scaled_one, factor_one, norm_gains[0])
    gain_one = jnp.sum(in_grad_rows * scaled_one, axis=0)
    own_group = (jnp.arange(GROUPS, dtype=jnp.int32) == groups[lax.axis_index("dp")]).astype(
        jnp.float32
    )
    gain_slots = own_group[:, None, None] * jnp.stack([gain_one, gain_two])[None]
    gain_grad = lax.psum(gain_slots, ("dp", "tensor"))

    down_new = optimize(
        order, down_recv, down_weight, down_first, down_second, down_outer, 3, turned=True
    )
    gate_half = optimize(
        order, gate_recv, gate_weight, gate_first, gate_second, gate_outer, 2, member=0
    )
    gate_new = optimize(
        order, up_recv, gate_weight, gate_first, gate_second, gate_outer, 2, member=1, before=gate_half
    )
    out_new = optimize(
        order, out_recv, out_weight, out_first, out_second, out_outer, 1, turned=True
    )
    qkv_new = optimize(order, qkv_recv, qkv_weight, qkv_first, qkv_second, qkv_outer, 0)
    gains_new = update(
        norm_gains, gain_grad, gains_first, gains_second, gains_outer, inner_rates[4], decays[4]
    )
    return (layer_out, tokens_grad, *qkv_new, *out_new, *gate_new, *down_new, *gains_new)


def solution(mesh):
    in_specs = (
        P(("dp", "tensor"), None),
        P(("dp", "tensor"), None),
        P("dp"),
        P("dp"),
        P(),
        P(None, "dp", "tensor"),
        P("tensor", "dp"),
        P(None, "dp", "tensor"),
        P("tensor", "dp"),
        P(),
        P(None, None, "dp", "tensor"),
        P(None, "tensor", "dp"),
        P(None, None, "dp", "tensor"),
        P(None, "tensor", "dp"),
        P(),
        P(None, None, "dp", "tensor"),
        P(None, "tensor", "dp"),
        P(None, None, "dp", "tensor"),
        P(None, "tensor", "dp"),
        P(),
        P(None, "dp", "tensor"),
        P("tensor", "dp"),
        P(None, "dp", "tensor"),
        P("tensor", "dp"),
        P(),
    )
    out_specs = (
        P(("dp", "tensor"), None),
        P(("dp", "tensor"), None),
        P(None, None, "dp", "tensor"),
        P(None, None, "dp", "tensor"),
        P(None, "dp", "tensor"),
        P(None, "dp", "tensor"),
        P(None, "dp", "tensor"),
        P(None, "dp", "tensor"),
        P(None, "tensor", "dp"),
        P(None, "tensor", "dp"),
        P("tensor", "dp"),
        P("tensor", "dp"),
        P("tensor", "dp"),
        P("tensor", "dp"),
        P(None, None, "dp", "tensor"),
        P(None, None, "dp", "tensor"),
        P(None, "dp", "tensor"),
        P(None, "dp", "tensor"),
        P(None, "dp", "tensor"),
        P(None, "dp", "tensor"),
        P(None, "tensor", "dp"),
        P(None, "tensor", "dp"),
        P("tensor", "dp"),
        P("tensor", "dp"),
        P("tensor", "dp"),
        P("tensor", "dp"),
        P(),
        P(),
        P(),
        P(),
        P(),
        P(),
    )
    return jax.shard_map(
        on_device, mesh=mesh, in_specs=in_specs, out_specs=out_specs, check_vma=False
    )
```

time: 2640 us -> 1700 us (0.64)
  matrix products: 944 us -> 313 us
  Pallas kernels: 0 us -> 249 us
  waiting for transfers between devices: 1150 us -> 915 us
  other arithmetic: 277 us -> 50.3 us
  local copies, waits for them, and re-layouts: 207 us -> 32.7 us
  blocking collectives: 0 us -> 94 us
    dot_general x53 -> x15, matrix products: 944 us -> 313 us  [the longest x5 115 us: dot(): return jnp.dot(left, right, preferred_element_type=jnp.float32)]
    pallas_call x0 -> x7, Pallas kernels: none -> 249 us  [the longest x5 87.6 us: optimize(): pl.pallas_call(functools.partial(opt_kernel, sources // GROUPS, turned, i...]
    reduce_scatter x4 -> x3, waiting for transfers between devices: 298 us -> 54.8 us  [scatter_rows(): lax.psum_scatter(part, 'tensor', scatter_dimension=0, tiled=True)]
    all_to_all x4 -> x7, waiting for transfers between devices: 244 us -> 451 us  [the longest x5 375 us: to_owners(): return lax.all_to_all(blocks, 'dp', split_axis=0, concat_axis=0)]
    all_gather x8 -> x7, waiting for transfers between devices: 492 us -> 295 us  [gather_rows(): return lax.all_gather(part, axis, axis=0, tiled=True)]
    convert_element_type x11 -> x4, other arithmetic: 122 us -> 6.16 us  [the longest x1 4.35 us: on_device(): resid_all = gather_rows(resid_grad.astype(bf16), 'tensor')]
    all_to_all x0 -> x1, blocking collectives: none -> 94 us  [sum_rows(): lax.all_to_all(blocks, 'tensor', split_axis=0, concat_axis=0)]
    another operation x2 -> x1, local copies, waits for them, and re-layouts: 76.3 us -> 0.02 us  [layout_of(): jnp.stack([lt.min(1), lt.max(1), ht.min(1), ht.max(1), qlo, qhi])]
  transfers between devices with their start and end apart: 17 -> 18, of which waited for: 12 -> 11; matrix products, arithmetic and copies ran while one was open for 50% -> 17% of each run, Pallas kernels for 0% -> 15%
where the time goes in v1:
time: 1700 us; the launch traced here: 1710 us
  waiting for transfers between devices  915 us (54%)
  matrix products  313 us (18%)
  Pallas kernels  249 us (15%)
  blocking collectives  94 us (6%)
  other arithmetic  50.3 us (3%)
  starting transfers between devices  39.6 us (2%)
  local copies, waits for them, and re-layouts  32.7 us (2%)
    all_to_all x5, waiting for transfers between devices, to_owners(): return lax.all_to_all(blocks, 'dp', split_axis=0, concat_axis=0)  375 us
    all_gather x7, waiting for transfers between devices, gather_rows(): return lax.all_gather(part, axis, axis=0, tiled=True)  295 us
    dot_general x5, matrix products, dot(): return jnp.dot(left, right, preferred_element_type=jnp.float32)  115 us
    psum x1, waiting for transfers between devices, on_device(): gain_grad = lax.psum(gain_slots, ('dp', 'tensor'))  113 us
    dot_general x5, matrix products, dot_rows(): lax.dot_general(left, right, (((0,), (0,)), ((), ())), preferred_element_...  99.8 us
    dot_general x5, matrix products, dot_cols(): lax.dot_general(left, right, (((1,), (1,)), ((), ())), preferred_element_...  97.8 us
    all_to_all x1, blocking collectives, sum_rows(): lax.all_to_all(blocks, 'tensor', split_axis=0, concat_axis=0)  94 us
    pallas_call x5, Pallas kernels, optimize(): pl.pallas_call(functools.partial(opt_kernel, sources // GROUPS, turned, i...  87.6 us
  transfers between devices with their start and end apart: 18, of which 11 were waited for; matrix products, arithmetic and copies ran while one was open for 17% of the time, Pallas kernels for 15%

profile of v1, /device:TPU:1, one launch (start us, length us, event | category | flops | bytes accessed | tf_op | source)
XLA Modules:
  0.0 1708.3 jit_solution(15836561776335353503)
XLA Ops:
  7.3 1.6 convert.9
  11.1 4.5 broadcast_in_dim.10
  15.5 5.8 all-to-all-start
  22.2 2.5 convert.10
  26.4 1.8 convert_reduce_fusion.1
  28.3 1.8 convert_reduce_fusion.2
  32.4 3.7 fusion.25
  36.2 1.7 pad_maximum_fusion
  37.9 76.2 %all-to-all-done = bf16[4,512,2048]{2,1,0:T(8,128)(2,1)} async-done(((bf16[4,512,2048]{2,1,0:T(8,128)(2,1)}), bf16[4,512,2048]{2,1,0:T(8,128)(2,1)}, u32[]{:S(2)}, u32[]{:S(2)}) %all-to-all-start) | async-done | bytes 8388640 | tf_op jit(solution)/shard_map/all_to_all | solution.py:398
  114.1 20.1 %fusion.35.q_ref.k_ref.v_ref = f32[2048,1536]{1,0:T(8,128)} fusion(bf16[2048,2048]{1,0:T(8,128)(2,1)} %bitcast.7, bf16[2048,1536]{1,0:T(8,128)(2,1)} %all-gather.10.cloned.1.call-done), kind=kOutput, calls=%fused_computation.93 | convolution fusion | flops 12884901888 | bytes 27262976 | tf_op jit(solution)/shard_map/dot_general | solution.py:380
  134.2 79.5 %attn_fwd.1 = (bf16[2048,512]{1,0:T(8,128)(2,1)}, bf16[2048,512]{1,0:T(8,128)(2,1)}, bf16[2048,512]{1,0:T(8,128)(2,1)}, bf16[2048,512]{1,0:T(8,128)(2,1)}, f32[4,2,2048]{2,1,0:T(2,128)S(1)}) custom-call(s32[6,4]{1,0:T(8,128)S(1)} %stack.36.info, f32[2048,1536]{1,0:T(8,128)} %fusion.35.q_ref.k_ref.v_ref, f32[2048,1536]{1,0:T(8,128)} %fusion.35.q_ref.k_ref.v_ref, ...), custom_call_target="tpu_custom_call" | custom-call | flops 5153960960 | bytes 12582912 | tf_op jit(solution)/shard_map/attn_fwd/pallas_call | solution.py:106
  213.7 6.7 convolution_convert_fusion.5
  220.4 94.0 %all_to_all.40 = bf16[4,512,2048]{2,1,0:T(8,128)(2,1)S(1)} all-to-all(bf16[4,512,2048]{2,1,0:T(8,128)(2,1)S(1)} %bitcast.76), channel_id=1, replica_groups=mesh['dp'=8,'tensor'=4] {'tensor'}, dimensions={0} | all-to-all | bytes 16777216 | tf_op jit(solution)/shard_map/all_to_all | solution.py:404
  314.4 3.9 convert_reduce_fusion
  318.3 2.8 multiply_reduce_fusion
  321.2 2.1 copy-done.23
  323.3 1.7 multiply_convert_fusion.3
  326.8 6.1 broadcast_in_dim.12
  332.9 5.6 all-to-all-start.2
  338.6 160.2 %all-gather.14.cloned.1.call-done = bf16[2048,2048]{1,0:T(8,128)(2,1)} async-done(((bf16[512,2048]{1,0:T(8,128)(2,1)}), bf16[2048,2048]{1,0:T(8,128)(2,1)}) %all-gather.14.cloned.1.call-update) | async-done | bytes 8388624 | tf_op jit(solution)/shard_map/all_gather | solution.py:392
  498.8 24.2 %fusion.6 = f32[2048,2048]{1,0:T(8,128)} fusion(bf16[2048,2048]{1,0:T(8,128)(2,1)} %all-gather.14.cloned.1.call-done, bf16[1,2048,2048]{2,1,0:T(8,128)(2,1)} %all-gather.20.cloned.1.call-done), kind=kOutput, calls=%fused_computation.14 | convolution fusion | flops 17179869184 | bytes 33554432 | tf_op jit(solution)/shard_map/dot_general | solution.py:380
  523.0 76.1 %all-gather.22.cloned.1.call-done = bf16[1,2048,2048]{2,1,0:T(8,128)(2,1)} async-done(((bf16[1,256,2048]{2,1,0:T(8,128)(2,1)}), bf16[1,2048,2048]{2,1,0:T(8,128)(2,1)}) %all-gather.22.cloned.1.call-update) | async-done | bytes 8388624 | tf_op jit(solution)/shard_map/all_gather | solution.py:392
  599.2 24.2 %fusion.2 = f32[2048,2048]{1,0:T(8,128)} fusion(bf16[2048,2048]{1,0:T(8,128)(2,1)} %all-gather.14.cloned.1.call-done, bf16[1,2048,2048]{2,1,0:T(8,128)(2,1)} %all-gather.22.cloned.1.call-done), kind=kOutput, calls=%fused_computation.10 | convolution fusion | flops 17179869184 | bytes 33554432 | tf_op jit(solution)/shard_map/dot_general | solution.py:380
  623.4 58.8 %all-gather.16.cloned.1.call-done = bf16[2048,2048]{0,1:T(8,128)(2,1)} async-done(((bf16[256,2048]{0,1:T(8,128)(2,1)}), bf16[2048,2048]{0,1:T(8,128)(2,1)}) %all-gather.16.cloned.1.call-update) | async-done | bytes 8388624 | tf_op jit(solution)/shard_map/all_gather | solution.py:392
  682.2 36.8 %multiply_convert_fusion = (bf16[2048,2048]{1,0:T(8,128)(2,1)}, bf16[2048,2048]{1,0:T(8,128)(2,1)}, bf16[2048,2048]{1,0:T(8,128)(2,1)}) fusion(f32[2048,2048]{1,0:T(8,128)} %fusion.6, f32[2048,2048]{1,0:T(8,128)} %fusion.2, bf16[2048,2048]{1,0:T(8,128)(2,1)} %bitcast.19, bf16[2048,2048]{0,1:T(8,128)(2,1)} %all-gather.16.cloned.1.call-done), kind=kOutput, calls=%fused_computation.1 | convolution fusion | flops 17242783744 | bytes 75497472 | tf_op jit(solution)/shard_map/dot_general | solution.py:380
  719.0 24.3 %fusion.4 = f32[2048,2048]{1,0:T(8,128)} fusion(bf16[2048,2048]{1,0:T(8,128)(2,1)} %get-tuple-element.130, bf16[1,2048,2048]{2,1,0:T(8,128)(2,1)} %all-gather.20.cloned.1.call-done), kind=kOutput, calls=%fused_computation.12 | convolution fusion | flops 17179869184 | bytes 33554432 | tf_op jit(solution)/shard_map/dot_general | solution.py:384
  743.3 25.7 %add_convert_fusion = bf16[2048,2048]{1,0:T(8,128)(2,1)} fusion(f32[2048,2048]{1,0:T(8,128)} %fusion.4, bf16[2048,2048]{1,0:T(8,128)(2,1)} %get-tuple-element.129, bf16[1,2048,2048]{2,1,0:T(8,128)(2,1)} %all-gather.22.cloned.1.call-done), kind=kOutput, calls=%fused_computation | convolution fusion | flops 17188257792 | bytes 41943040 | tf_op jit(solution)/shard_map/dot_general | solution.py:384
  769.0 23.7 %convolution_convert_fusion.2 = bf16[2048,2048]{1,0:T(8,128)(2,1)} fusion(bf16[2048,2048]{1,0:T(8,128)(2,1)} %all-gather.14.cloned.1.call-done, bf16[2048,2048]{1,0:T(8,128)(2,1)} %get-tuple-element.129), kind=kOutput, calls=%fused_computation.18 | convolution fusion | flops 17184063488 | bytes 25165824 | tf_op jit(solution)/shard_map/dot_general | solution.py:388
  792.7 5.2 all-to-all-start.5
  798.3 54.8 %reduce-scatter.6.cloned.1.call-done = bf16[512,2048]{1,0:T(8,128)(2,1)} async-done(((bf16[2048,2048]{1,0:T(8,128)(2,1)}), bf16[512,2048]{1,0:T(8,128)(2,1)}) %reduce-scatter.6.cloned.1.call-update) | async-done | bytes 2097168 | tf_op jit(solution)/shard_map/reduce_scatter | solution.py:408
  853.1 4.7 fusion.20
  858.5 4.3 fusion.28
  862.8 23.7 %convolution_convert_fusion.1 = bf16[2048,2048]{1,0:T(8,128)(2,1)} fusion(bf16[2048,2048]{1,0:T(8,128)(2,1)} %all-gather.14.cloned.1.call-done, bf16[2048,2048]{1,0:T(8,128)(2,1)} %get-tuple-element.130), kind=kOutput, calls=%fused_computation.17 | convolution fusion | flops 17184063488 | bytes 25165824 | tf_op jit(solution)/shard_map/dot_general | solution.py:388
  886.5 94.4 %all-to-all-done.5.refs_0_ = bf16[8,256,2048]{2,1,0:T(8,128)(2,1)} async-done(((bf16[8,256,2048]{2,1,0:T(8,128)(2,1)}), bf16[8,256,2048]{2,1,0:T(8,128)(2,1)}, u32[]{:S(2)}, u32[]{:S(2)}) %all-to-all-start.5) | async-done | bytes 8388640 | tf_op jit(solution)/shard_map/all_to_all | solution.py:414
  980.9 5.8 all-to-all-start.6
  986.8 10.0 convolution_convert_fusion.8.do_ref
  996.8 82.0 %attn_bwd.1 = (bf16[2048,512]{1,0:T(8,128)(2,1)S(1)}, bf16[2048,512]{1,0:T(8,128)(2,1)}, bf16[2048,512]{1,0:T(8,128)(2,1)}) custom-call(s32[6,4]{1,0:T(8,128)S(1)} %stack.36.info, bf16[2048,512]{1,0:T(8,128)(2,1)} %get-tuple-element.74.q_ref, bf16[2048,512]{1,0:T(8,128)(2,1)} %get-tuple-element.75.k_ref, bf16[2048,512]{1,0:T(8,128)(2,1)} %get-tuple-element.76.v_ref, ...), custom_call_target="tpu_custom_call" | custom-call | flops 12884901888 | bytes 16777216 | tf_op jit(solution)/shard_map/attn_bwd/pallas_call | solution.py:202
  1079.0 1.9 constant_dynamic-update-slice_fusion.1
  1081.2 2.7 copy-done.30
  1083.9 17.4 %convolution_convert_fusion.3 = bf16[2048,2048]{1,0:T(8,128)(2,1)} fusion(bf16[2048,1536]{1,0:T(8,128)(2,1)S(1)} %constant_dynamic-update-slice_fusion, bf16[2048,1536]{1,0:T(8,128)(2,1)} %all-gather.10.cloned.1.call-done), kind=kOutput, calls=%fused_computation.19 | convolution fusion | flops 12889096192 | bytes 20971520 | tf_op jit(solution)/shard_map/dot_general | solution.py:384
  1101.4 23.9 %convolution_convert_fusion = bf16[2048,2048]{1,0:T(8,128)(2,1)} fusion(bf16[2048,2048]{1,0:T(8,128)(2,1)} %bitcast.19, bf16[2048,2048]{1,0:T(8,128)(2,1)} %get-tuple-element.131), kind=kOutput, calls=%fused_computation.16 | convolution fusion | flops 17184063488 | bytes 25165824 | tf_op jit(solution)/shard_map/dot_general | solution.py:388
  1125.2 44.5 %all-to-all-done.6.refs_0_ = bf16[8,256,2048]{2,1,0:T(8,128)(2,1)} async-done(((bf16[8,256,2048]{2,1,0:T(8,128)(2,1)}), bf16[8,256,2048]{2,1,0:T(8,128)(2,1)}, u32[]{:S(2)}, u32[]{:S(2)}) %all-to-all-start.6) | async-done | bytes 8388640 | tf_op jit(solution)/shard_map/all_to_all | solution.py:414
  1169.8 5.8 all-to-all-start.7
  1175.6 23.6 %convolution_convert_fusion.4 = bf16[2048,2048]{1,0:T(8,128)(2,1)} fusion(bf16[2048,2048]{1,0:T(8,128)(2,1)} %get-tuple-element.131, bf16[2048,2048]{0,1:T(8,128)(2,1)} %all-gather.16.cloned.1.call-done), kind=kOutput, calls=%fused_computation.20 | convolution fusion | flops 17184063488 | bytes 25165824 | tf_op jit(solution)/shard_map/dot_general | solution.py:384
  1199.2 1.6 copy-done.51
  1200.8 9.5 convolution_convert_fusion.7
  1210.2 148.4 %all-to-all-done.7.refs_0_ = bf16[8,256,2048]{2,1,0:T(8,128)(2,1)} async-done(((bf16[8,256,2048]{2,1,0:T(8,128)(2,1)}), bf16[8,256,2048]{2,1,0:T(8,128)(2,1)}, u32[]{:S(2)}, u32[]{:S(2)}) %all-to-all-start.7) | async-done | bytes 8388640 | tf_op jit(solution)/shard_map/all_to_all | solution.py:414
  1358.6 4.8 all-to-all-start.4
  1363.4 19.1 %convolution_convert_fusion.6 = bf16[2048,1536]{1,0:T(8,128)(2,1)} fusion(bf16[2048,2048]{1,0:T(8,128)(2,1)} %bitcast.7, bf16[2048,1536]{1,0:T(8,128)(2,1)} %copy-done.30), kind=kOutput, calls=%fused_computation.22 | convolution fusion | flops 12888047616 | bytes 20971520 | tf_op jit(solution)/shard_map/dot_general | solution.py:388
  1382.5 29.0 %all-to-all-done.4.refs_0_ = bf16[8,256,512]{2,1,0:T(8,128)(2,1)S(1)} async-done(((bf16[8,256,512]{2,1,0:T(8,128)(2,1)}), bf16[8,256,512]{2,1,0:T(8,128)(2,1)S(1)}, u32[]{:S(2)}, u32[]{:S(2)}) %all-to-all-start.4) | async-done | bytes 2097184 | tf_op jit(solution)/shard_map/all_to_all | solution.py:414
  1411.4 5.7 all-to-all-start.3
  1419.4 2.2 copy-done
  1421.6 2.2 copy-done.2
  1423.7 21.9 %optimize.7 = (f32[4,2,256,2048]{3,2,1,0:T(8,128)}, f32[4,2,256,2048]{3,2,1,0:T(8,128)}, f32[2,256,2048]{2,1,0:T(8,128)}, f32[2,256,2048]{2,1,0:T(8,128)}, f32[2...) custom-call(s32[8]{0:T(128)S(1)} %get-tuple-element.81.order, bf16[8,256,2048]{2,1,0:T(8,128)(2,1)} %all-to-all-done.6.refs_0_, ...), custom_call_target="tpu_custom_call" | custom-call | flops 31457280 | bytes 53477376 | tf_op jit(solution)/shard_map/optimize/pallas_call | solution.py:362
  1445.7 1.6 copy-done.5
  1447.3 22.2 %optimize.9 = (f32[4,2048,256]{2,1,0:T(8,128)}, f32[4,2048,256]{2,1,0:T(8,128)}, f32[2048,256]{1,0:T(8,128)}, f32[2048,256]{1,0:T(8,128)}, f32[2048,256]{1,0:T(8,128)}, /*index=5*/bf16[2048,256]{1,0:T(8,128)(2,1)}) custom-call(s32[8]{0:T(128)S(1)} %get-tuple-element.81.order, bf16[8,256,2048]{2,1,0:T(8,128)(2,1)} %all-to-all-done.7.refs_0_, ...), custom_call_target="tpu_custom_call" | custom-call | flops 31457280 | bytes 53477376 | tf_op jit(solution)/shard_map/optimize/pallas_call | solution.py:362
  1469.6 22.0 %optimize.8 = (f32[4,2,256,2048]{3,2,1,0:T(8,128)}, f32[4,2,256,2048]{3,2,1,0:T(8,128)}, f32[2,256,2048]{2,1,0:T(8,128)}, f32[2,256,2048]{2,1,0:T(8,128)}, f32[2...) custom-call(s32[8]{0:T(128)S(1)} %get-tuple-element.81.order, ...), custom_call_target="tpu_custom_call", output_to_operand_aliasing={{0}: (6, {}), {1}: (7, {}), {2}: (8, {}), {3}: (9, {}), {4}... | custom-call | flops 31457280 | bytes 53477376 | tf_op jit(solution)/shard_map/optimize/pallas_call | solution.py:362
  1491.6 4.7 optimize.6
  1496.3 58.9 %all-to-all-done.3.refs_0_ = bf16[8,256,1536]{2,1,0:T(8,128)(2,1)} async-done(((bf16[8,256,1536]{2,1,0:T(8,128)(2,1)}), bf16[8,256,1536]{2,1,0:T(8,128)(2,1)}, u32[]{:S(2)}, u32[]{:S(2)}) %all-to-all-start.3) | async-done | bytes 6291488 | tf_op jit(solution)/shard_map/all_to_all | solution.py:414
  1558.1 16.7 optimize.5
  1574.8 2.9 fusion.23
  1578.6 7.7 fusion.16
  1586.3 112.9 %all-reduce.2.cloned.1.call-done = f32[4,2,2048]{2,1,0:T(2,128)} async-done(((f32[4,2,2048]{2,1,0:T(2,128)}), f32[4,2,2048]{2,1,0:T(2,128)}) %all-reduce.2.cloned.1.call-update) | async-done | bytes 65552 | tf_op jit(solution)/shard_map/psum | solution.py:507
  1699.1 1.7 fusion.27
  (163 shorter events, 17.0 us)
Async XLA Ops:
  7.2 2.7 copy-start.25
  7.2 3.2 copy-start.36
  7.2 106.9 %all-gather.10.cloned.1.call-start = ((), (), s32[]{:S(2)}) async-start(), calls=%async_computation.11 | async-start | bytes 7077888 | tf_op jit(solution)/shard_map/all_gather | solution.py:392
  10.5 5.1 copy-start.43
  10.5 5.0 copy-start.34
  10.5 310.7 %copy-start.31 = (f32[1,2048]{1,0:T(1,128)}, f32[1,2048]{1,0:T(1,128)S(1)}, u32[]{:S(2)}) copy-start(f32[1,2048]{1,0:T(1,128)S(1)} %get-tuple-element.139) | copy-start | bytes 24580
  15.5 5.9 copy-start.14
  15.5 98.6 %all-to-all-start = ((bf16[4,512,2048]{2,1,0:T(8,128)(2,1)}), bf16[4,512,2048]{2,1,0:T(8,128)(2,1)}, u32[]{:S(2)}, u32[]{:S(2)}) async-start(bf16[4,512,2048]{2,1,0:T(8,128)(2,1)} %broadcast_in_dim.10), calls=%async_computation | async-start | bytes 16777216 | tf_op jit(solution)/shard_map/all_to_all | solution.py:398
  21.3 5.1 copy-start.49
  21.3 5.1 copy-start.50
  21.3 192.3 %all-gather.12.cloned.1.call-start = ((), (), s32[]{:S(2)}) async-start(), calls=%async_computation.12 | async-start | bytes 2359296 | tf_op jit(solution)/shard_map/all_gather | solution.py:392
  22.1 316.4 %all-gather.20.cloned.1.call-start = ((), (), s32[]{:S(2)}) async-start(), calls=%async_computation.20 | async-start | bytes 9437184 | tf_op jit(solution)/shard_map/all_gather | solution.py:392
  26.2 472.7 %all-gather.14.cloned.1.call-start = ((), (), s32[]{:S(2)}) async-start(), calls=%async_computation.13 | async-start | bytes 10485760 | tf_op jit(solution)/shard_map/all_gather | solution.py:392
  28.2 7.9 copy-start.21
  30.1 6.1 copy-start.19
  37.9 96.3 %copy-start.7 = (f32[2048,128]{1,0:T(8,128)}, f32[2048,128]{1,0:T(8,128)S(1)}, u32[]{:S(2)}) copy-start(f32[2048,128]{1,0:T(8,128)S(1)} %get-tuple-element.146.cos_ref) | copy-start | bytes 3145732
  37.9 96.3 %copy-start.9 = (f32[2048,128]{1,0:T(8,128)}, f32[2048,128]{1,0:T(8,128)S(1)}, u32[]{:S(2)}) copy-start(f32[2048,128]{1,0:T(8,128)S(1)} %get-tuple-element.147.sin_ref) | copy-start | bytes 3145732
  114.1 20.1 %copy-start.11 = (s32[2048,1]{1,0:T(8,128)S(1)}, s32[2048,1]{1,0:T(8,128)}, u32[]{:S(2)}) copy-start(s32[2048,1]{1,0:T(8,128)} %copy.69.hi_ref) | copy-start | bytes 24580
  314.4 3.9 copy-start.26
  321.1 4.5 copy-start.4
  321.2 5.6 copy-start.40
  325.0 274.1 %all-gather.22.cloned.1.call-start = ((), (), s32[]{:S(2)}) async-start(), calls=%async_computation.21 | async-start | bytes 9437184 | tf_op jit(solution)/shard_map/all_gather | solution.py:392
  325.6 356.6 %all-gather.16.cloned.1.call-start = ((), (), s32[]{:S(2)}) async-start(), calls=%async_computation.14 | async-start | bytes 9437184 | tf_op jit(solution)/shard_map/all_gather | solution.py:392
  332.9 290.5 %all-to-all-start.2 = ((bf16[4,512,2048]{2,1,0:T(8,128)(2,1)}), bf16[4,512,2048]{2,1,0:T(8,128)(2,1)}, u32[]{:S(2)}, u32[]{:S(2)}) async-start(bf16[4,512,2048]{2,1,0:T(8,128)(2,1)} %broadcast_in_dim.12), calls=%async_computation.3 | async-start | bytes 16777216 | tf_op jit(solution)/shard_map/all_to_all | solution.py:398
  338.5 514.6 %reduce-scatter.6.cloned.1.call-start = ((), (), s32[]{:S(2)}) async-start(), calls=%async_computation.16 | async-start | bytes 10485760 | tf_op jit(solution)/shard_map/reduce_scatter | solution.py:408
  792.7 60.4 %copy-start.32 = (f32[1,2048]{1,0:T(1,128)S(1)}, f32[1,2048]{1,0:T(1,128)}, u32[]{:S(2)}) copy-start(f32[1,2048]{1,0:T(1,128)} %copy-done.31) | copy-start | bytes 24580
  792.7 60.4 %copy-start.41 = (f32[512]{0:T(512)S(1)}, f32[512]{0:T(512)}, u32[]{:S(2)}) copy-start(f32[512]{0:T(512)} %copy-done.40) | copy-start | bytes 6148
  792.7 188.2 %all-to-all-start.5 = ((bf16[8,256,2048]{2,1,0:T(8,128)(2,1)}), bf16[8,256,2048]{2,1,0:T(8,128)(2,1)}, u32[]{:S(2)}, u32[]{:S(2)}) async-start(bf16[8,256,2048]{2,1,0:T(8,128)(2,1)} %bitcast.74), calls=%async_computation.8 | async-start | bytes 16777216 | tf_op jit(solution)/shard_map/all_to_all | solution.py:414
  797.9 60.5 %copy-start.28 = (bf16[512,2048]{1,0:T(8,128)(2,1)S(1)}, bf16[512,2048]{1,0:T(8,128)(2,1)}, u32[]{:S(2)}) copy-start(bf16[512,2048]{1,0:T(8,128)(2,1)} %param.26) | copy-start | bytes 6291460
  797.9 188.9 %all-gather.18.cloned.1.call-start = ((), (), s32[]{:S(2)}) async-start(), calls=%async_computation.17 | async-start | bytes 10485760 | tf_op jit(solution)/shard_map/all_gather | solution.py:392
  853.1 5.3 copy-start.24
  980.9 188.8 %all-to-all-start.6 = ((bf16[8,256,2048]{2,1,0:T(8,128)(2,1)}), bf16[8,256,2048]{2,1,0:T(8,128)(2,1)}, u32[]{:S(2)}, u32[]{:S(2)}) async-start(bf16[8,256,2048]{2,1,0:T(8,128)(2,1)} %bitcast.73), calls=%async_computation.9 | async-start | bytes 16777216 | tf_op jit(solution)/shard_map/all_to_all | solution.py:414
  986.7 10.1 copy-start.8
  986.7 10.1 copy-start.10
  986.7 10.1 copy-start.20
  986.7 10.1 copy-start.22
  986.8 588.0 %reduce-scatter.8.cloned.1.call-start = ((), (), s32[]{:S(2)}) async-start(), calls=%async_computation.18 | async-start | bytes 10485760 | tf_op jit(solution)/shard_map/reduce_scatter | solution.py:408
  1078.8 2.2 copy-start.29
  1081.2 2.7 copy-start.30
  1169.8 188.8 %all-to-all-start.7 = ((bf16[8,256,2048]{2,1,0:T(8,128)(2,1)}), bf16[8,256,2048]{2,1,0:T(8,128)(2,1)}, u32[]{:S(2)}, u32[]{:S(2)}) async-start(bf16[8,256,2048]{2,1,0:T(8,128)(2,1)} %bitcast.75), calls=%async_computation.10 | async-start | bytes 16777216 | tf_op jit(solution)/shard_map/all_to_all | solution.py:414
  1175.6 403.0 %reduce-scatter.4.cloned.1.call-start = ((), (), s32[]{:S(2)}) async-start(), calls=%async_computation.15 | async-start | bytes 10485760 | tf_op jit(solution)/shard_map/reduce_scatter | solution.py:408
  1358.6 52.8 %all-to-all-start.4 = ((bf16[8,256,512]{2,1,0:T(8,128)(2,1)}), bf16[8,256,512]{2,1,0:T(8,128)(2,1)S(1)}, u32[]{:S(2)}, u32[]{:S(2)}) async-start(bf16[8,256,512]{2,1,0:T(8,128)(2,1)} %bitcast.78), calls=%async_computation.7 | async-start | bytes 4194304 | tf_op jit(solution)/shard_map/all_to_all | solution.py:414
  1411.4 5.7 copy-start.52
  1411.4 143.8 %all-to-all-start.3 = ((bf16[8,256,1536]{2,1,0:T(8,128)(2,1)}), bf16[8,256,1536]{2,1,0:T(8,128)(2,1)}, u32[]{:S(2)}, u32[]{:S(2)}) async-start(bf16[8,256,1536]{2,1,0:T(8,128)(2,1)} %bitcast.77), calls=%async_computation.6 | async-start | bytes 12582912 | tf_op jit(solution)/shard_map/all_to_all | solution.py:414
  1417.2 282.0 %all-reduce.2.cloned.1.call-start = ((), (), s32[]{:S(2)}) async-start(), calls=%async_computation.19 | async-start | bytes 131072 | tf_op jit(solution)/shard_map/psum | solution.py:507
  1419.4 2.2 copy-start
  1423.7 21.9 %copy-start.16 = (f32[2048,256]{1,0:T(8,128)S(1)}, f32[2048,256]{1,0:T(8,128)}, u32[]{:S(2)}) copy-start(f32[2048,256]{1,0:T(8,128)} %refs_4_.9) | copy-start | bytes 6291460
  1447.3 22.2 %copy-start.1 = (f32[2,256,2048]{2,1,0:T(8,128)S(1)}, f32[2,256,2048]{2,1,0:T(8,128)}, u32[]{:S(2)}) copy-start(f32[2,256,2048]{2,1,0:T(8,128)} %refs_3_.8) | copy-start | bytes 12582916
  1447.3 22.2 %copy-start.3 = (f32[2,256,2048]{2,1,0:T(8,128)S(1)}, f32[2,256,2048]{2,1,0:T(8,128)}, u32[]{:S(2)}) copy-start(f32[2,256,2048]{2,1,0:T(8,128)} %refs_4_.8) | copy-start | bytes 12582916
  1469.5 22.1 %copy-start.12 = (f32[4,512,256]{2,1,0:T(8,128)S(1)}, f32[4,512,256]{2,1,0:T(8,128)}, u32[]{:S(2)}) copy-start(f32[4,512,256]{2,1,0:T(8,128)} %refs_1_.6) | copy-start | bytes 6291460
  1469.5 22.1 %copy-start.13 = (f32[4,512,256]{2,1,0:T(8,128)S(1)}, f32[4,512,256]{2,1,0:T(8,128)}, u32[]{:S(2)}) copy-start(f32[4,512,256]{2,1,0:T(8,128)} %refs_2_.6) | copy-start | bytes 6291460
  1469.5 22.1 %copy-start.15 = (f32[512,256]{1,0:T(8,128)S(1)}, f32[512,256]{1,0:T(8,128)}, u32[]{:S(2)}) copy-start(f32[512,256]{1,0:T(8,128)} %refs_3_.6) | copy-start | bytes 1572868
  1469.5 22.1 %copy-start.18 = (f32[512,256]{1,0:T(8,128)S(1)}, f32[512,256]{1,0:T(8,128)}, u32[]{:S(2)}) copy-start(f32[512,256]{1,0:T(8,128)} %refs_4_.6) | copy-start | bytes 1572868
  1558.1 16.7 copy-start.27
  1558.1 16.7 copy-start.35
  1558.1 16.7 copy-start.44
  1558.1 19.7 %copy-start.45 = (f32[2048]{0:T(1024)S(1)}, f32[2048]{0:T(1024)}, u32[]{:S(2)}) copy-start(f32[2048]{0:T(1024)} %get-tuple-element.112) | copy-start | bytes 24580
  1558.1 20.5 %copy-start.33 = (f32[1,2048]{1,0:T(1,128)S(1)}, f32[1,2048]{1,0:T(1,128)}, u32[]{:S(2)}) copy-start(f32[1,2048]{1,0:T(1,128)} %copy-done.31) | copy-start | bytes 24580
  1558.1 20.5 %copy-start.42 = (f32[512]{0:T(512)S(1)}, f32[512]{0:T(512)}, u32[]{:S(2)}) copy-start(f32[512]{0:T(512)} %copy-done.40) | copy-start | bytes 6148
  1558.1 20.5 %copy-start.47 = (f32[512]{0:T(512)S(1)}, f32[512]{0:T(512)}, u32[]{:S(2)}) copy-start(f32[512]{0:T(512)} %copy-done.46) | copy-start | bytes 6148
  1578.5 120.6 %copy-start.38 = (f32[4,2,2048]{2,1,0:T(2,128)S(1)}, f32[4,2,2048]{2,1,0:T(2,128)}, u32[]{:S(2)}) copy-start(f32[4,2,2048]{2,1,0:T(2,128)} %param.44) | copy-start | bytes 196612
  1578.5 120.6 %copy-start.39 = (f32[4,2,2048]{2,1,0:T(2,128)S(1)}, f32[4,2,2048]{2,1,0:T(2,128)}, u32[]{:S(2)}) copy-start(f32[4,2,2048]{2,1,0:T(2,128)} %param.39) | copy-start | bytes 196612
  1578.5 122.3 %copy-start.37 = (f32[2,2048]{1,0:T(2,128)S(1)}, f32[2,2048]{1,0:T(2,128)}, u32[]{:S(2)}) copy-start(f32[2,2048]{1,0:T(2,128)} %param.34) | copy-start | bytes 49156
  1578.5 122.3 %copy-start.48 = (f32[2,2048]{1,0:T(2,128)S(1)}, f32[2,2048]{1,0:T(2,128)}, u32[]{:S(2)}) copy-start(f32[2,2048]{1,0:T(2,128)} %param.49) | copy-start | bytes 49156
  (7 other events, 10.9 us)
Sparse Core Ops, SparseCore 0:
  10.2 67.1 all-gather.9
  79.6 29.2 all-gather.11
  111.1 80.8 all-gather.19
  325.2 173.6 all-gather.13
  500.9 98.2 all-gather.21
  601.2 80.9 all-gather.15
  769.2 83.8 reduce-scatter.5
  862.9 87.4 all-gather.17
  1101.5 105.4 reduce-scatter.7
  1209.9 86.3 reduce-scatter.3
  1578.6 120.4 all-reduce.1

commit v2 on v1

--- a/solution.py
+++ b/solution.py
@@ -239,7 +239,6 @@
     return jnp.concatenate([cos] * 4, axis=1), jnp.concatenate([-sin, sin, -sin, sin], axis=1)
 
 
-HDIM = 64
 GROUPS = 4
 STEP = 4
 
@@ -388,6 +387,23 @@
     return lax.dot_general(left, right, (((0,), (0,)), ((), ())), preferred_element_type=jnp.float32)
 
 
+def after(value, *others):
+    return lax.optimization_barrier((value,) + others)[0]
+
+
+def tick_kernel(source, mark):
+    mark[...] = jnp.zeros_like(mark)
+
+
+def tick(value):
+    return pl.pallas_call(
+        tick_kernel,
+        out_shape=jax.ShapeDtypeStruct((8, LANES), jnp.float32),
+        in_specs=[pl.BlockSpec(memory_space=pl.ANY)],
+        compiler_params=pltpu.CompilerParams(has_side_effects=True),
+    )(value)
+
+
 def gather_rows(part, axis):
     return lax.all_gather(part, axis, axis=0, tiled=True)
 
@@ -395,17 +411,22 @@
 def spread_rows(part):
     count = lax.axis_size("tensor")
     copies = jnp.broadcast_to(part[None], (count,) + part.shape)
-    return lax.all_to_all(copies, "tensor", split_axis=0, concat_axis=0).reshape((-1,) + part.shape[1:])
+    parts = lax.all_to_all(copies, "tensor", split_axis=0, concat_axis=0)
+    return parts.reshape((-1,) + part.shape[1:])
 
 
 def sum_rows(part):
     count = lax.axis_size("tensor")
     blocks = part.reshape((count, part.shape[0] // count) + part.shape[1:])
-    return jnp.sum(lax.all_to_all(blocks, "tensor", split_axis=0, concat_axis=0).astype(jnp.float32), axis=0)
+    parts = lax.all_to_all(blocks, "tensor", split_axis=0, concat_axis=0)
+    return jnp.sum(parts.astype(jnp.float32), axis=0)
 
 
 def scatter_rows(part):
-    return lax.psum_scatter(part, "tensor", scatter_dimension=0, tiled=True).astype(jnp.float32)
+    summed = lax.psum_scatter(
+        part.astype(jnp.bfloat16), "tensor", scatter_dimension=0, tiled=True
+    )
+    return summed.astype(jnp.float32)
 
 
 def to_owners(grad):
@@ -414,7 +435,7 @@
     return lax.all_to_all(blocks, "dp", split_axis=0, concat_axis=0)
 
 
-def on_device(
+def step(
     tokens,
     cotangent,
     seq_ids,
@@ -445,15 +466,12 @@
     field_in = tokens.astype(jnp.float32)
     normed_one, scaled_one, factor_one = normed(field_in, norm_gains[0])
     normed_all = spread_rows(normed_one)
-    qkv_full = gather_rows(
-        jnp.concatenate([qkv_weight[m].astype(bf16) for m in range(3)], axis=1), "dp"
-    )
+    qkv_full = gather_rows(jnp.concatenate([qkv_weight[m].astype(bf16) for m in range(3)], axis=1), "dp")
     out_full = gather_rows(out_weight.T.astype(bf16), "dp")
-    wide = gate_weight.shape[2]
     gate_full = gather_rows(gate_weight[0].astype(bf16), "dp")
     up_full = gather_rows(gate_weight[1].astype(bf16), "dp")
     down_full = gather_rows(down_weight.T.astype(bf16), "dp")
-    cotan_all = spread_rows(lax.optimization_barrier((cotangent, normed_all))[0])
+    cotan_all = spread_rows(after(cotangent, normed_all))
 
     lo, hi, info = layout_of(seq_ids, block_ids, TILE, TILE)
     cosine, sine_table = rope_tables(lo)
@@ -466,25 +484,33 @@
     attn_rows = sum_rows(dot_cols(mixed_all, out_full).astype(bf16))
     residual = field_in + attn_rows
     normed_two, scaled_two, factor_two = normed(residual, norm_gains[1])
+    normed_two, gate_full, up_full, down_full = lax.optimization_barrier(
+        (normed_two, gate_full, up_full, down_full)
+    )
     ffn_input = gather_rows(normed_two, "tensor")
     gate_pre = dot(ffn_input, gate_full)
     up_pre = dot(ffn_input, up_full)
     sigmoid_gate = jax.nn.sigmoid(gate_pre)
     swish = gate_pre * sigmoid_gate
     hidden = (swish * up_pre).astype(bf16)
-    down_recv = to_owners(dot_rows(cotan_all, hidden))
-    ffn_part = scatter_rows(dot_cols(hidden, down_full).astype(bf16))
+    down_grad = dot_rows(cotan_all, hidden).astype(bf16)
+    down_recv = to_owners(down_grad)
+    mark = tick(down_grad)
+    hidden, cotan_all = lax.optimization_barrier((hidden, cotan_all, mark))[:2]
+    ffn_sum = dot_cols(hidden, down_full).astype(bf16)
+    ffn_part = scatter_rows(ffn_sum)
+    cotan_all = after(cotan_all, ffn_sum)
     layer_out = (residual + ffn_part).astype(bf16)
     hidden_grad = dot(cotan_all, down_full)
     gate_grad_low = (
         hidden_grad * up_pre * sigmoid_gate * (1.0 + gate_pre * (1.0 - sigmoid_gate))
     ).astype(bf16)
     up_grad_low = (hidden_grad * swish).astype(bf16)
-    ffn_back_rows = scatter_rows(
-        (dot_cols(gate_grad_low, gate_full) + dot_cols(up_grad_low, up_full)).astype(bf16)
-    )
-    gate_recv = to_owners(dot_rows(ffn_input, gate_grad_low))
-    up_recv = to_owners(dot_rows(ffn_input, up_grad_low))
+    ffn_back = (dot_cols(gate_grad_low, gate_full) + dot_cols(up_grad_low, up_full)).astype(bf16)
+    ffn_back_rows = scatter_rows(ffn_back)
+    ffn_kept = after(ffn_input, ffn_back)
+    gate_recv = to_owners(dot_rows(ffn_kept, gate_grad_low))
+    up_recv = to_owners(dot_rows(ffn_kept, up_grad_low))
     cotan_rows = cotangent.astype(jnp.float32)
     resid_grad = cotan_rows + norm_back(ffn_back_rows, scaled_two, factor_two, norm_gains[1])
     gain_two = jnp.sum(ffn_back_rows * scaled_two, axis=0)
@@ -496,7 +522,7 @@
         cosine, sine_table, lo[None], hi[None], TILE, TILE,
     )
     raw_all = jnp.concatenate(raw_grads, axis=1)
-    in_grad_rows = scatter_rows(dot_cols(raw_all, qkv_full).astype(bf16))
+    in_grad_rows = scatter_rows(dot_cols(raw_all, qkv_full))
     qkv_recv = to_owners(dot_rows(normed_all, raw_all))
     tokens_grad = resid_grad + norm_back(in_grad_rows, scaled_one, factor_one, norm_gains[0])
     gain_one = jnp.sum(in_grad_rows * scaled_one, axis=0)
@@ -505,6 +531,7 @@
     )
     gain_slots = own_group[:, None, None] * jnp.stack([gain_one, gain_two])[None]
     gain_grad = lax.psum(gain_slots, ("dp", "tensor"))
+    order = after(order, gain_slots)
 
     down_new = optimize(
         order, down_recv, down_weight, down_first, down_second, down_outer, 3, turned=True
@@ -518,7 +545,9 @@
     out_new = optimize(
         order, out_recv, out_weight, out_first, out_second, out_outer, 1, turned=True
     )
-    qkv_new = optimize(order, qkv_recv, qkv_weight, qkv_first, qkv_second, qkv_outer, 0)
+    qkv_new = optimize(
+        order, after(qkv_recv, gain_grad), qkv_weight, qkv_first, qkv_second, qkv_outer, 0
+    )
     gains_new = update(
         norm_gains, gain_grad, gains_first, gains_second, gains_outer, inner_rates[4], decays[4]
     )
@@ -587,6 +616,4 @@
         P(),
         P(),
     )
-    return jax.shard_map(
-        on_device, mesh=mesh, in_specs=in_specs, out_specs=out_specs, check_vma=False
-    )
+    return jax.shard_map(step, mesh=mesh, in_specs=in_specs, out_specs=out_specs, check_vma=False)

time: 1700 us -> 1530 us (0.900)
  waiting for transfers between devices: 915 us -> 757 us
    psum x1, waiting for transfers between devices: 113 us -> 1.56 us  [step(): gain_grad = lax.psum(gain_slots, ('dp', 'tensor'))]
    all_gather x7, waiting for transfers between devices: 295 us -> 195 us  [gather_rows(): return lax.all_gather(part, axis, axis=0, tiled=True)]
    all_to_all x5, waiting for transfers between devices: 375 us -> 422 us  [to_owners(): return lax.all_to_all(blocks, 'dp', split_axis=0, concat_axis=0)]
  transfers between devices with their start and end apart: 18 -> 18, of which waited for: 11 -> 10; matrix products, arithmetic and copies ran while one was open for 17% -> 16% of each run, Pallas kernels for 15% -> 14%
where the time goes in v2:
time: 1530 us
  waiting for transfers between devices  757 us (49%)
  matrix products  315 us (21%)
  Pallas kernels  236 us (15%)
  blocking collectives  88.1 us (6%)
  other arithmetic  56.2 us (4%)
  starting transfers between devices  39.8 us (3%)
  local copies, waits for them, and re-layouts  20.7 us (1%)
    all_to_all x5, waiting for transfers between devices, to_owners(): return lax.all_to_all(blocks, 'dp', split_axis=0, concat_axis=0)  422 us
    all_gather x7, waiting for transfers between devices, gather_rows(): return lax.all_gather(part, axis, axis=0, tiled=True)  195 us
    dot_general x5, matrix products, dot(): return jnp.dot(left, right, preferred_element_type=jnp.float32)  116 us
    dot_general x5, matrix products, dot_rows(): lax.dot_general(left, right, (((0,), (0,)), ((), ())), preferred_element_...  101 us
    dot_general x5, matrix products, dot_cols(): lax.dot_general(left, right, (((1,), (1,)), ((), ())), preferred_element_...  98 us
    all_to_all x1, blocking collectives, sum_rows(): parts = lax.all_to_all(blocks, 'tensor', split_axis=0, concat_axis=0)  88.1 us
    pallas_call x5, Pallas kernels, optimize(): pl.pallas_call(functools.partial(opt_kernel, sources // GROUPS, turned, i...  86.6 us
    all_to_all x2, waiting for transfers between devices, spread_rows(): parts = lax.all_to_all(copies, 'tensor', split_axis=0, concat_axis=0)  80.1 us
  transfers between devices with their start and end apart: 18, of which 10 were waited for; matrix products, arithmetic and copies ran while one was open for 16% of the time, Pallas kernels for 14%

profile of v2, /device:TPU:1, one launch (start us, length us, event | category | flops | bytes accessed | tf_op | source)
XLA Modules:
  0.0 1528.1 jit_solution(8772445564756373637)
XLA Ops:
  7.3 1.6 convert.9
  8.9 0.9 pad_maximum_fusion.2
  10.7 2.6 convert.10
  13.4 1.5 fusion.26
  16.5 4.5 broadcast_in_dim.10
  21.0 5.9 all-to-all-start
  27.0 1.1 convert_bitcast_fusion
  28.4 1.8 convert_reduce_fusion.1
  30.2 1.8 convert_reduce_fusion.2
  32.4 1.4 copy.69.hi_ref
  34.4 3.7 fusion.18
  38.1 1.7 pad_maximum_fusion
  39.8 80.1 %all-to-all-done = bf16[4,512,2048]{2,1,0:T(8,128)(2,1)} async-done(((bf16[4,512,2048]{2,1,0:T(8,128)(2,1)}), bf16[4,512,2048]{2,1,0:T(8,128)(2,1)}, u32[]{:S(2)}, u32[]{:S(2)}) %all-to-all-start) | async-done | bytes 8388640 | tf_op jit(solution)/shard_map/all_to_all | solution.py:414
  119.9 19.6 %fusion.28.q_ref.k_ref.v_ref = f32[2048,1536]{1,0:T(8,128)} fusion(bf16[2048,2048]{1,0:T(8,128)(2,1)} %bitcast.7, bf16[2048,1536]{1,0:T(8,128)(2,1)} %all-gather.10.cloned.1.call-done), kind=kOutput, calls=%fused_computation.86 | convolution fusion | flops 12884901888 | bytes 27262976 | tf_op jit(solution)/shard_map/dot_general | solution.py:379
  139.5 73.3 %attn_fwd.1 = (bf16[2048,512]{1,0:T(8,128)(2,1)}, bf16[2048,512]{1,0:T(8,128)(2,1)}, bf16[2048,512]{1,0:T(8,128)(2,1)}, bf16[2048,512]{1,0:T(8,128)(2,1)}, f32[4,2,2048]{2,1,0:T(2,128)S(1)}) custom-call(s32[6,4]{1,0:T(8,128)S(1)} %stack.36.info, f32[2048,1536]{1,0:T(8,128)} %fusion.28.q_ref.k_ref.v_ref, f32[2048,1536]{1,0:T(8,128)} %fusion.28.q_ref.k_ref.v_ref, ...), custom_call_target="tpu_custom_call" | custom-call | flops 5153960960 | bytes 12582912 | tf_op jit(solution)/shard_map/attn_fwd/pallas_call | solution.py:106
  212.8 6.8 convolution_convert_fusion.5
  219.6 88.1 %all_to_all.40 = bf16[4,512,2048]{2,1,0:T(8,128)(2,1)S(1)} all-to-all(bf16[4,512,2048]{2,1,0:T(8,128)(2,1)S(1)} %bitcast.72), channel_id=1, replica_groups=mesh['dp'=8,'tensor'=4] {'tensor'}, dimensions={0} | all-to-all | bytes 16777216 | tf_op jit(solution)/shard_map/all_to_all | solution.py:421
  307.7 3.9 convert_reduce_fusion
  311.6 4.8 multiply_reduce_fusion
  316.4 3.9 multiply_convert_fusion.3
  320.4 37.2 %all-gather.14.cloned.1.call-done = bf16[2048,2048]{0,1:T(8,128)(2,1)} async-done(((bf16[256,2048]{0,1:T(8,128)(2,1)}), bf16[2048,2048]{0,1:T(8,128)(2,1)}) %all-gather.14.cloned.1.call-update) | async-done | bytes 8388624 | tf_op jit(solution)/shard_map/all_gather | solution.py:408
  357.6 6.1 broadcast_in_dim.12
  363.7 6.1 all-to-all-start.2
  369.8 157.8 %all-gather.16.cloned.1.call-done = bf16[2048,2048]{1,0:T(8,128)(2,1)} async-done(((bf16[512,2048]{1,0:T(8,128)(2,1)}), bf16[2048,2048]{1,0:T(8,128)(2,1)}) %all-gather.16.cloned.1.call-update) | async-done | bytes 8388624 | tf_op jit(solution)/shard_map/all_gather | solution.py:408
  527.6 24.2 %fusion.29 = f32[2048,2048]{1,0:T(8,128)} fusion(bf16[2048,2048]{1,0:T(8,128)(2,1)} %all-gather.16.cloned.1.call-done, bf16[2048,2048]{1,0:T(8,128)(2,1)} %bitcast.90), kind=kOutput, calls=%fused_computation.87 | convolution fusion | flops 17179869184 | bytes 33554432 | tf_op jit(solution)/shard_map/dot_general | solution.py:379
  551.8 28.1 %multiply_convert_fusion.2 = (bf16[2048,2048]{1,0:T(8,128)(2,1)}, f32[2048,2048]{1,0:T(8,128)}) fusion(f32[2048,2048]{1,0:T(8,128)} %fusion.29, bf16[2048,2048]{1,0:T(8,128)(2,1)} %all-gather.16.cloned.1.call-done, bf16[2048,2048]{1,0:T(8,128)(2,1)} %bitcast.92), kind=kOutput, calls=%fused_computation.3 | convolution fusion | flops 17205035008 | bytes 58720256 | tf_op jit(solution)/shard_map/dot_general | solution.py:379
  579.9 24.0 %convolution_convert_fusion.4.source = bf16[2048,2048]{1,0:T(8,128)(2,1)} fusion(bf16[2048,2048]{1,0:T(8,128)(2,1)} %bitcast.19, bf16[2048,2048]{1,0:T(8,128)(2,1)} %get-tuple-element.87), kind=kOutput, calls=%fused_computation.13 | convolution fusion | flops 17184063488 | bytes 25165824 | tf_op jit(solution)/shard_map/dot_general | solution.py:387
  604.4 23.6 %convolution_convert_fusion.3 = bf16[2048,2048]{1,0:T(8,128)(2,1)} fusion(bf16[2048,2048]{1,0:T(8,128)(2,1)} %get-tuple-element.87, bf16[2048,2048]{0,1:T(8,128)(2,1)} %all-gather.14.cloned.1.call-done), kind=kOutput, calls=%fused_computation.12 | convolution fusion | flops 17184063488 | bytes 25165824 | tf_op jit(solution)/shard_map/dot_general | solution.py:383
  628.1 34.5 %multiply_convert_fusion = (bf16[2048,2048]{1,0:T(8,128)(2,1)}, bf16[2048,2048]{1,0:T(8,128)(2,1)}) fusion(f32[2048,2048]{1,0:T(8,128)} %fusion.29, f32[2048,2048]{1,0:T(8,128)} %get-tuple-element.164, bf16[2048,2048]{1,0:T(8,128)(2,1)} %bitcast.19, bf16[2048,2048]{0,1:T(8,128)(2,1)} %all-gather.14.cloned.1.call-done), kind=kOutput, calls=%fused_computation.1 | convolution fusion | flops 17234395136 | bytes 67108864 | tf_op jit(solution)/shard_map/dot_general | solution.py:379
  662.5 24.3 %fusion.30 = f32[2048,2048]{1,0:T(8,128)} fusion(bf16[2048,2048]{1,0:T(8,128)(2,1)} %get-tuple-element.150, bf16[2048,2048]{1,0:T(8,128)(2,1)} %bitcast.91), kind=kOutput, calls=%fused_computation.88 | convolution fusion | flops 17179869184 | bytes 33554432 | tf_op jit(solution)/shard_map/dot_general | solution.py:383
  686.9 25.9 %add_convert_fusion = bf16[2048,2048]{1,0:T(8,128)(2,1)} fusion(f32[2048,2048]{1,0:T(8,128)} %fusion.30, bf16[2048,2048]{1,0:T(8,128)(2,1)} %get-tuple-element.149, bf16[2048,2048]{1,0:T(8,128)(2,1)} %bitcast.93), kind=kOutput, calls=%fused_computation | convolution fusion | flops 17188257792 | bytes 41943040 | tf_op jit(solution)/shard_map/dot_general | solution.py:383
  712.8 23.7 %convolution_convert_fusion.1 = bf16[2048,2048]{1,0:T(8,128)(2,1)} fusion(bf16[2048,2048]{1,0:T(8,128)(2,1)} %all-gather.16.cloned.1.call-done, bf16[2048,2048]{1,0:T(8,128)(2,1)} %get-tuple-element.149), kind=kOutput, calls=%fused_computation.10 | convolution fusion | flops 17184063488 | bytes 25165824 | tf_op jit(solution)/shard_map/dot_general | solution.py:387
  736.4 5.5 all-to-all-start.5
  742.0 57.0 %reduce-scatter.6.cloned.1.call-done = bf16[512,2048]{1,0:T(8,128)(2,1)} async-done(((bf16[2048,2048]{1,0:T(8,128)(2,1)}), bf16[512,2048]{1,0:T(8,128)(2,1)}) %reduce-scatter.6.cloned.1.call-update) | async-done | bytes 2097168 | tf_op jit(solution)/shard_map/reduce_scatter | solution.py:426
  799.0 4.2 fusion.13
  803.1 4.9 fusion.21
  808.1 23.8 %convolution_convert_fusion = bf16[2048,2048]{1,0:T(8,128)(2,1)} fusion(bf16[2048,2048]{1,0:T(8,128)(2,1)} %all-gather.16.cloned.1.call-done, bf16[2048,2048]{1,0:T(8,128)(2,1)} %get-tuple-element.150), kind=kOutput, calls=%fused_computation.9 | convolution fusion | flops 17184063488 | bytes 25165824 | tf_op jit(solution)/shard_map/dot_general | solution.py:387
  831.9 93.1 %all-to-all-done.5.refs_0_ = bf16[8,256,2048]{2,1,0:T(8,128)(2,1)} async-done(((bf16[8,256,2048]{2,1,0:T(8,128)(2,1)}), bf16[8,256,2048]{2,1,0:T(8,128)(2,1)}, u32[]{:S(2)}, u32[]{:S(2)}) %all-to-all-start.5) | async-done | bytes 8388640 | tf_op jit(solution)/shard_map/all_to_all | solution.py:435
  925.0 5.8 all-to-all-start.6
  930.9 9.9 convolution_convert_fusion.8.do_ref
  940.7 75.7 %attn_bwd.1 = (bf16[2048,512]{1,0:T(8,128)(2,1)S(1)}, bf16[2048,512]{1,0:T(8,128)(2,1)}, bf16[2048,512]{1,0:T(8,128)(2,1)}) custom-call(s32[6,4]{1,0:T(8,128)S(1)} %stack.36.info, bf16[2048,512]{1,0:T(8,128)(2,1)} %get-tuple-element.91.q_ref, bf16[2048,512]{1,0:T(8,128)(2,1)} %get-tuple-element.92.k_ref, bf16[2048,512]{1,0:T(8,128)(2,1)} %get-tuple-element.93.v_ref, ...), custom_call_target="tpu_custom_call" | custom-call | flops 12884901888 | bytes 16777216 | tf_op jit(solution)/shard_map/attn_bwd/pallas_call | solution.py:202
  1016.6 1.9 constant_dynamic-update-slice_fusion.1
  1018.9 2.7 copy-done.22
  1021.5 17.4 %convolution_convert_fusion.2 = bf16[2048,2048]{1,0:T(8,128)(2,1)} fusion(bf16[2048,1536]{1,0:T(8,128)(2,1)S(1)} %constant_dynamic-update-slice_fusion, bf16[2048,1536]{1,0:T(8,128)(2,1)} %all-gather.10.cloned.1.call-done), kind=kOutput, calls=%fused_computation.11 | convolution fusion | flops 12889096192 | bytes 20971520 | tf_op jit(solution)/shard_map/dot_general | solution.py:383
  1039.0 74.9 %all-to-all-done.6.refs_0_ = bf16[8,256,2048]{2,1,0:T(8,128)(2,1)} async-done(((bf16[8,256,2048]{2,1,0:T(8,128)(2,1)}), bf16[8,256,2048]{2,1,0:T(8,128)(2,1)}, u32[]{:S(2)}, u32[]{:S(2)}) %all-to-all-start.6) | async-done | bytes 8388640 | tf_op jit(solution)/shard_map/all_to_all | solution.py:435
  1113.8 5.8 all-to-all-start.7
  1120.2 1.0 copy-done.38
  1121.2 10.4 convolution_convert_fusion.7
  1131.6 171.1 %all-to-all-done.7.refs_0_ = bf16[8,256,2048]{2,1,0:T(8,128)(2,1)} async-done(((bf16[8,256,2048]{2,1,0:T(8,128)(2,1)}), bf16[8,256,2048]{2,1,0:T(8,128)(2,1)}, u32[]{:S(2)}, u32[]{:S(2)}) %all-to-all-start.7) | async-done | bytes 8388640 | tf_op jit(solution)/shard_map/all_to_all | solution.py:435
  1302.7 4.5 all-to-all-start.4
  1307.1 19.1 %convolution_convert_fusion.6 = bf16[2048,1536]{1,0:T(8,128)(2,1)} fusion(bf16[2048,2048]{1,0:T(8,128)(2,1)} %bitcast.7, bf16[2048,1536]{1,0:T(8,128)(2,1)} %copy-done.22), kind=kOutput, calls=%fused_computation.15 | convolution fusion | flops 12888047616 | bytes 20971520 | tf_op jit(solution)/shard_map/dot_general | solution.py:387
  1326.2 29.0 %all-to-all-done.4.refs_0_ = bf16[8,256,512]{2,1,0:T(8,128)(2,1)S(1)} async-done(((bf16[8,256,512]{2,1,0:T(8,128)(2,1)}), bf16[8,256,512]{2,1,0:T(8,128)(2,1)S(1)}, u32[]{:S(2)}, u32[]{:S(2)}) %all-to-all-start.4) | async-done | bytes 2097184 | tf_op jit(solution)/shard_map/all_to_all | solution.py:435
  1355.2 5.7 all-to-all-start.3
  1361.0 1.0 sort.17
  1363.2 3.6 fusion.16
  1367.6 8.7 fusion.9
  1376.4 4.7 optimize.6
  1381.2 22.0 %optimize.7 = (f32[4,2,256,2048]{3,2,1,0:T(8,128)}, f32[4,2,256,2048]{3,2,1,0:T(8,128)}, f32[2,256,2048]{2,1,0:T(8,128)}, f32[2,256,2048]{2,1,0:T(8,128)}, f32[2...) custom-call(s32[8]{0:T(128)S(1)} %get-tuple-element.99.order, bf16[8,256,2048]{2,1,0:T(8,128)(2,1)} %all-to-all-done.6.refs_0_, ...), custom_call_target="tpu_custom_call" | custom-call | flops 31457280 | bytes 53477376 | tf_op jit(solution)/shard_map/optimize/pallas_call | solution.py:361
  1403.1 21.4 %optimize.9 = (f32[4,2048,256]{2,1,0:T(8,128)}, f32[4,2048,256]{2,1,0:T(8,128)}, f32[2048,256]{1,0:T(8,128)}, f32[2048,256]{1,0:T(8,128)}, f32[2048,256]{1,0:T(8,128)}, /*index=5*/bf16[2048,256]{1,0:T(8,128)(2,1)}) custom-call(s32[8]{0:T(128)S(1)} %get-tuple-element.99.order, bf16[8,256,2048]{2,1,0:T(8,128)(2,1)} %all-to-all-done.7.refs_0_, ...), custom_call_target="tpu_custom_call" | custom-call | flops 31457280 | bytes 53477376 | tf_op jit(solution)/shard_map/optimize/pallas_call | solution.py:361
  1424.6 22.0 %optimize.8 = (f32[4,2,256,2048]{3,2,1,0:T(8,128)}, f32[4,2,256,2048]{3,2,1,0:T(8,128)}, f32[2,256,2048]{2,1,0:T(8,128)}, f32[2,256,2048]{2,1,0:T(8,128)}, f32[2...) custom-call(s32[8]{0:T(128)S(1)} %get-tuple-element.99.order, ...), custom_call_target="tpu_custom_call", output_to_operand_aliasing={{0}: (6, {}), {1}: (7, {}), {2}: (8, {}), {3}: (9, {}), {4}... | custom-call | flops 31457280 | bytes 53477376 | tf_op jit(solution)/shard_map/optimize/pallas_call | solution.py:361
  1446.6 54.2 %all-to-all-done.3.refs_0_ = bf16[8,256,1536]{2,1,0:T(8,128)(2,1)} async-done(((bf16[8,256,1536]{2,1,0:T(8,128)(2,1)}), bf16[8,256,1536]{2,1,0:T(8,128)(2,1)}, u32[]{:S(2)}, u32[]{:S(2)}) %all-to-all-start.3) | async-done | bytes 6291488 | tf_op jit(solution)/shard_map/all_to_all | solution.py:435
  1500.8 1.6 all-reduce.2.cloned.1.call-done
  1502.4 1.7 fusion.20
  1504.7 16.5 %optimize.5 = (f32[4,3,256,512]{3,2,1,0:T(8,128)}, f32[4,3,256,512]{3,2,1,0:T(8,128)}, f32[3,256,512]{2,1,0:T(8,128)}, f32[3,256,512]{2,1,0:T(8,128)}, f32[3,256...) custom-call(s32[8]{0:T(128)S(1)} %get-tuple-element.99.order, bf16[8,256,1536]{2,1,0:T(8,128)(2,1)} %all-to-all-done.3.refs_0_, ...), custom_call_target="tpu_custom_call" | custom-call | flops 23592960 | bytes 40108032 | tf_op jit(solution)/shard_map/optimize/pallas_call | solution.py:361
  (138 shorter events, 8.5 us)
Async XLA Ops:
  7.2 2.7 copy-start.8
  7.2 112.7 %all-gather.10.cloned.1.call-start = ((), (), s32[]{:S(2)}) async-start(), calls=%async_computation.11 | async-start | bytes 7077888 | tf_op jit(solution)/shard_map/all_gather | solution.py:408
  9.8 203.0 %all-gather.12.cloned.1.call-start = ((), (), s32[]{:S(2)}) async-start(), calls=%async_computation.12 | async-start | bytes 2359296 | tf_op jit(solution)/shard_map/all_gather | solution.py:408
  10.7 4.8 copy-start.17
  10.7 5.3 copy-start.27
  10.7 309.7 %all-gather.20.cloned.1.call-start = ((), (), s32[]{:S(2)}) async-start(), calls=%async_computation.20 | async-start | bytes 9437184 | tf_op jit(solution)/shard_map/all_gather | solution.py:408
  14.8 305.5 %all-gather.22.cloned.1.call-start = ((), (), s32[]{:S(2)}) async-start(), calls=%async_computation.21 | async-start | bytes 9437184 | tf_op jit(solution)/shard_map/all_gather | solution.py:408
  15.9 5.1 copy-start.33
  16.0 5.0 copy-start.25
  16.0 300.4 %copy-start.23 = (f32[1,2048]{1,0:T(1,128)}, f32[1,2048]{1,0:T(1,128)S(1)}, u32[]{:S(2)}) copy-start(f32[1,2048]{1,0:T(1,128)S(1)} %get-tuple-element.158) | copy-start | bytes 24580
  21.0 6.0 copy-start.2
  21.0 7.3 copy-start.36
  21.0 7.3 copy-start.37
  21.0 98.9 %all-to-all-start = ((bf16[4,512,2048]{2,1,0:T(8,128)(2,1)}), bf16[4,512,2048]{2,1,0:T(8,128)(2,1)}, u32[]{:S(2)}, u32[]{:S(2)}) async-start(bf16[4,512,2048]{2,1,0:T(8,128)(2,1)} %broadcast_in_dim.10), calls=%async_computation | async-start | bytes 16777216 | tf_op jit(solution)/shard_map/all_to_all | solution.py:414
  27.0 330.6 %all-gather.14.cloned.1.call-start = ((), (), s32[]{:S(2)}) async-start(), calls=%async_computation.13 | async-start | bytes 9437184 | tf_op jit(solution)/shard_map/all_gather | solution.py:408
  28.1 499.5 %all-gather.16.cloned.1.call-start = ((), (), s32[]{:S(2)}) async-start(), calls=%async_computation.14 | async-start | bytes 10485760 | tf_op jit(solution)/shard_map/all_gather | solution.py:408
  30.2 7.9 copy-start.15
  32.0 6.1 copy-start.13
  119.9 19.6 %copy-start.5 = (s32[2048,1]{1,0:T(8,128)S(1)}, s32[2048,1]{1,0:T(8,128)}, u32[]{:S(2)}) copy-start(s32[2048,1]{1,0:T(8,128)} %copy.69.hi_ref) | copy-start | bytes 24580
  307.7 3.9 copy-start.18
  316.4 47.3 %copy-start.31 = (f32[512]{0:T(512)}, f32[512]{0:T(512)S(1)}, u32[]{:S(2)}) copy-start(f32[512]{0:T(512)S(1)} %add_rsqrt_fusion) | copy-start | bytes 6148
  363.7 216.2 %all-to-all-start.2 = ((bf16[4,512,2048]{2,1,0:T(8,128)(2,1)}), bf16[4,512,2048]{2,1,0:T(8,128)(2,1)}, u32[]{:S(2)}, u32[]{:S(2)}) async-start(bf16[4,512,2048]{2,1,0:T(8,128)(2,1)} %broadcast_in_dim.12), calls=%async_computation.2 | async-start | bytes 16777216 | tf_op jit(solution)/shard_map/all_to_all | solution.py:414
  369.8 429.1 %reduce-scatter.6.cloned.1.call-start = ((), (), s32[]{:S(2)}) async-start(), calls=%async_computation.16 | async-start | bytes 10485760 | tf_op jit(solution)/shard_map/reduce_scatter | solution.py:426
  736.4 62.5 %copy-start.24 = (f32[1,2048]{1,0:T(1,128)S(1)}, f32[1,2048]{1,0:T(1,128)}, u32[]{:S(2)}) copy-start(f32[1,2048]{1,0:T(1,128)} %copy-done.23) | copy-start | bytes 24580
  736.4 62.5 %copy-start.32 = (f32[512]{0:T(512)S(1)}, f32[512]{0:T(512)}, u32[]{:S(2)}) copy-start(f32[512]{0:T(512)} %copy-done.31) | copy-start | bytes 6148
  736.4 188.6 %all-to-all-start.5 = ((bf16[8,256,2048]{2,1,0:T(8,128)(2,1)}), bf16[8,256,2048]{2,1,0:T(8,128)(2,1)}, u32[]{:S(2)}, u32[]{:S(2)}) async-start(bf16[8,256,2048]{2,1,0:T(8,128)(2,1)} %bitcast.71), calls=%async_computation.8 | async-start | bytes 16777216 | tf_op jit(solution)/shard_map/all_to_all | solution.py:435
  742.0 188.9 %all-gather.18.cloned.1.call-start = ((), (), s32[]{:S(2)}) async-start(), calls=%async_computation.17 | async-start | bytes 10485760 | tf_op jit(solution)/shard_map/all_gather | solution.py:408
  798.9 4.2 copy-start.19
  798.9 4.2 copy-start.20
  925.0 188.8 %all-to-all-start.6 = ((bf16[8,256,2048]{2,1,0:T(8,128)(2,1)}), bf16[8,256,2048]{2,1,0:T(8,128)(2,1)}, u32[]{:S(2)}, u32[]{:S(2)}) async-start(bf16[8,256,2048]{2,1,0:T(8,128)(2,1)} %bitcast.70), calls=%async_computation.9 | async-start | bytes 16777216 | tf_op jit(solution)/shard_map/all_to_all | solution.py:435
  930.8 9.9 copy-start.14
  930.8 9.9 copy-start.16
  930.8 432.4 %reduce-scatter.8.cloned.1.call-start = ((), (), s32[]{:S(2)}) async-start(), calls=%async_computation.18 | async-start | bytes 10485760 | tf_op jit(solution)/shard_map/reduce_scatter | solution.py:426
  1016.5 2.2 copy-start.21
  1018.8 2.7 copy-start.22
  1113.8 188.8 %all-to-all-start.7 = ((bf16[8,256,2048]{2,1,0:T(8,128)(2,1)}), bf16[8,256,2048]{2,1,0:T(8,128)(2,1)}, u32[]{:S(2)}, u32[]{:S(2)}) async-start(bf16[8,256,2048]{2,1,0:T(8,128)(2,1)} %bitcast.69), calls=%async_computation.10 | async-start | bytes 16777216 | tf_op jit(solution)/shard_map/all_to_all | solution.py:435
  1119.6 1.6 copy-start.38
  1119.6 248.0 %reduce-scatter.4.cloned.1.call-start = ((), (), s32[]{:S(2)}) async-start(), calls=%async_computation.15 | async-start | bytes 10485760 | tf_op jit(solution)/shard_map/reduce_scatter | solution.py:426
  1302.7 52.6 %all-to-all-start.4 = ((bf16[8,256,512]{2,1,0:T(8,128)(2,1)}), bf16[8,256,512]{2,1,0:T(8,128)(2,1)S(1)}, u32[]{:S(2)}, u32[]{:S(2)}) async-start(bf16[8,256,512]{2,1,0:T(8,128)(2,1)} %bitcast.74), calls=%async_computation.7 | async-start | bytes 4194304 | tf_op jit(solution)/shard_map/all_to_all | solution.py:435
  1355.2 5.7 copy-start.39
  1355.2 8.0 copy-start.26
  1355.2 8.0 copy-start.34
  1355.2 145.6 %all-to-all-start.3 = ((bf16[8,256,1536]{2,1,0:T(8,128)(2,1)}), bf16[8,256,1536]{2,1,0:T(8,128)(2,1)}, u32[]{:S(2)}, u32[]{:S(2)}) async-start(bf16[8,256,1536]{2,1,0:T(8,128)(2,1)} %bitcast.73), calls=%async_computation.6 | async-start | bytes 12582912 | tf_op jit(solution)/shard_map/all_to_all | solution.py:435
  1361.0 141.4 %all-reduce.2.cloned.1.call-start = ((), (), s32[]{:S(2)}) async-start(), calls=%async_computation.19 | async-start | bytes 131072 | tf_op jit(solution)/shard_map/psum | solution.py:533
  1367.5 8.8 copy-start.9
  1367.6 8.8 copy-start.12
  1367.6 8.8 copy-start.6
  1367.6 8.8 copy-start.7
  1367.6 13.5 copy-start.1
  1376.4 4.7 copy-start
  1381.1 22.0 %copy-start.3 = (f32[2048,256]{1,0:T(8,128)S(1)}, f32[2048,256]{1,0:T(8,128)}, u32[]{:S(2)}) copy-start(f32[2048,256]{1,0:T(8,128)} %refs_3_.9) | copy-start | bytes 6291460
  1381.1 22.0 %copy-start.10 = (f32[2048,256]{1,0:T(8,128)S(1)}, f32[2048,256]{1,0:T(8,128)}, u32[]{:S(2)}) copy-start(f32[2048,256]{1,0:T(8,128)} %refs_4_.9) | copy-start | bytes 6291460
  1424.5 77.8 %copy-start.29 = (f32[4,2,2048]{2,1,0:T(2,128)S(1)}, f32[4,2,2048]{2,1,0:T(2,128)}, u32[]{:S(2)}) copy-start(f32[4,2,2048]{2,1,0:T(2,128)} %param.44) | copy-start | bytes 196612
  1424.5 77.8 %copy-start.30 = (f32[4,2,2048]{2,1,0:T(2,128)S(1)}, f32[4,2,2048]{2,1,0:T(2,128)}, u32[]{:S(2)}) copy-start(f32[4,2,2048]{2,1,0:T(2,128)} %param.39) | copy-start | bytes 196612
  1424.5 79.5 %copy-start.28 = (f32[2,2048]{1,0:T(2,128)S(1)}, f32[2,2048]{1,0:T(2,128)}, u32[]{:S(2)}) copy-start(f32[2,2048]{1,0:T(2,128)} %param.34) | copy-start | bytes 49156
  1424.6 79.5 %copy-start.35 = (f32[2,2048]{1,0:T(2,128)S(1)}, f32[2,2048]{1,0:T(2,128)}, u32[]{:S(2)}) copy-start(f32[2,2048]{1,0:T(2,128)} %param.49) | copy-start | bytes 49156
  1424.6 80.1 %copy-start.4 = (f32[3,256,512]{2,1,0:T(8,128)S(1)}, f32[3,256,512]{2,1,0:T(8,128)}, u32[]{:S(2)}) copy-start(f32[3,256,512]{2,1,0:T(8,128)} %refs_3_.5) | copy-start | bytes 4718596
  1424.6 80.1 %copy-start.11 = (f32[3,256,512]{2,1,0:T(8,128)S(1)}, f32[3,256,512]{2,1,0:T(8,128)}, u32[]{:S(2)}) copy-start(f32[3,256,512]{2,1,0:T(8,128)} %refs_4_.5) | copy-start | bytes 4718596
Sparse Core Ops, SparseCore 0:
  10.2 67.1 all-gather.9
  79.6 29.2 all-gather.11
  111.1 80.8 all-gather.19
  194.0 80.5 all-gather.21
  276.6 80.9 all-gather.13
  359.9 167.6 all-gather.15
  712.9 85.9 reduce-scatter.5
  808.2 87.4 all-gather.17
  1039.1 109.4 reduce-scatter.7
  1151.5 86.3 reduce-scatter.3
  1367.9 134.4 all-reduce.1

commit v3 on v2

--- a/solution.py
+++ b/solution.py
@@ -276,8 +276,10 @@
     return [first_new, second_new, change, outer_new, master, master.astype(jnp.bfloat16)]
 
 
-def opt_kernel(per, turned, rate, decay, order, *refs):
-    (recv, first, second, weight, outer), (first_new, second_new, delta, outer_new, master, low) = refs[:5], refs[-6:]
+def opt_kernel(per, turned, parts, rate, decay, order, *refs):
+    recvs, (first, second, weight, outer) = refs[:parts], refs[parts : parts + 4]
+    first_new, second_new, delta, outer_new, master, low = refs[-6:]
+    held = recvs[0].shape[0]
     rows, cols = weight.shape[-2:]
     step_r, step_c = min(rows, 16), min(cols, 256)
     if turned:
@@ -294,10 +296,13 @@
             grad = None
             for j in range(per):
                 source = order[g * per + j]
-                if turned:
-                    part = recv[source, pl.ds(c, step_c), pl.ds(r, step_r)].astype(jnp.float32)
+                block = (pl.ds(c, step_c), pl.ds(r, step_r)) if turned else at
+                if parts == 1:
+                    part = recvs[0][(source,) + block].astype(jnp.float32)
                 else:
-                    part = recv[(source,) + at].astype(jnp.float32)
+                    slot = lax.rem(source, held)
+                    own, other = (x[(slot,) + block].astype(jnp.float32) for x in recvs)
+                    part = jnp.where(source < held, own, other)
                 grad = part if grad is None else grad + part
             if turned:
                 grad = grad.T
@@ -319,7 +324,8 @@
 
 
 def optimize(order, recv, weight, first, second, outer, position, turned=False, member=None, before=None):
-    sources = recv.shape[0]
+    held = recv[0].shape[0]
+    sources = held * len(recv)
     stacked = weight.ndim == 3
     rows, cols = weight.shape[-2:]
     members = weight.shape[0] if stacked and member is None else 1
@@ -336,9 +342,9 @@
         return (base + m,) if stacked else ()
 
     if turned:
-        recv_spec = pl.BlockSpec((sources, bc, br), lambda m, i: (0, 0, i))
+        recv_spec = pl.BlockSpec((held, bc, br), lambda m, i: (0, 0, i))
     else:
-        recv_spec = pl.BlockSpec((sources, br, bc), lambda m, i: (0, i, m))
+        recv_spec = pl.BlockSpec((held, br, bc), lambda m, i: (0, i, m))
     one = pl.BlockSpec(lead + (br, bc), lambda m, i: pick(m) + (i, 0))
     many = pl.BlockSpec((GROUPS,) + lead + (br, bc), lambda m, i: (0,) + pick(m) + (i, 0))
     f32 = jnp.float32
@@ -350,8 +356,8 @@
         jax.ShapeDtypeStruct(weight.shape, f32),
         jax.ShapeDtypeStruct(weight.shape, jnp.bfloat16),
     ]
-    operands = [order, recv, first, second, weight, outer]
-    specs = [pl.BlockSpec(memory_space=pltpu.SMEM), recv_spec, many, many, one, one]
+    operands = [order, *recv, first, second, weight, outer]
+    specs = [pl.BlockSpec(memory_space=pltpu.SMEM)] + [recv_spec] * len(recv) + [many, many, one, one]
     aliases = {}
     if before is not None:
         aliases = {len(operands) + k: k for k in range(6)}
@@ -360,7 +366,7 @@
     count = members * rows * cols
     return pl.pallas_call(
         functools.partial(
-            opt_kernel, sources // GROUPS, turned, inner_rates[position], decays[position]
+            opt_kernel, sources // GROUPS, turned, len(recv), inner_rates[position], decays[position]
         ),
         out_shape=outs,
         grid=(members, blocks),
@@ -427,6 +433,25 @@
         part.astype(jnp.bfloat16), "tensor", scatter_dimension=0, tiled=True
     )
     return summed.astype(jnp.float32)
+
+
+def to_half(grad):
+    count = lax.axis_size("dp")
+    near = count // 2
+    blocks = grad.astype(jnp.bfloat16).reshape((near, grad.shape[0] // near) + grad.shape[1:])
+    halves = [list(range(near)), list(range(near, count))]
+    return lax.all_to_all(blocks, "dp", split_axis=0, concat_axis=0, axis_index_groups=halves)
+
+
+def to_partner(part):
+    count = lax.axis_size("dp")
+    return lax.ppermute(part, "dp", [(i, (i + count // 2) % count) for i in range(count)])
+
+
+def half_cols(rows):
+    near = lax.axis_size("dp") // 2
+    wide = rows.shape[1] // 2
+    return lax.dynamic_slice_in_dim(rows, lax.axis_index("dp") // near * wide, wide, axis=1)
 
 
 def to_owners(grad):
@@ -473,6 +498,7 @@
     down_full = gather_rows(down_weight.T.astype(bf16), "dp")
     cotan_all = spread_rows(after(cotangent, normed_all))
 
+    other_cotan = to_partner(cotangent)
     lo, hi, info = layout_of(seq_ids, block_ids, TILE, TILE)
     cosine, sine_table = rope_tables(lo)
     order = jnp.argsort(groups, stable=True).astype(jnp.int32)
@@ -484,23 +510,20 @@
     attn_rows = sum_rows(dot_cols(mixed_all, out_full).astype(bf16))
     residual = field_in + attn_rows
     normed_two, scaled_two, factor_two = normed(residual, norm_gains[1])
-    normed_two, gate_full, up_full, down_full = lax.optimization_barrier(
-        (normed_two, gate_full, up_full, down_full)
-    )
-    ffn_input = gather_rows(normed_two, "tensor")
+    other_two = to_partner(normed_two)
+    normed_two, gate_full, up_full = lax.optimization_barrier((normed_two, gate_full, up_full, tick(normed_two)))[:3]
+    ffn_input = spread_rows(normed_two)
+    other_dy = gather_rows(after(other_cotan, ffn_input), "tensor")
+    other_input = gather_rows(other_two, "tensor")
+
     gate_pre = dot(ffn_input, gate_full)
     up_pre = dot(ffn_input, up_full)
     sigmoid_gate = jax.nn.sigmoid(gate_pre)
     swish = gate_pre * sigmoid_gate
     hidden = (swish * up_pre).astype(bf16)
-    down_grad = dot_rows(cotan_all, hidden).astype(bf16)
-    down_recv = to_owners(down_grad)
-    mark = tick(down_grad)
-    hidden, cotan_all = lax.optimization_barrier((hidden, cotan_all, mark))[:2]
-    ffn_sum = dot_cols(hidden, down_full).astype(bf16)
-    ffn_part = scatter_rows(ffn_sum)
-    cotan_all = after(cotan_all, ffn_sum)
-    layer_out = (residual + ffn_part).astype(bf16)
+    down_grad = dot_rows(half_cols(cotan_all), hidden).astype(bf16)
+    down_recv = to_half(down_grad)
+    cotan_all = after(cotan_all, tick(down_grad))
     hidden_grad = dot(cotan_all, down_full)
     gate_grad_low = (
         hidden_grad * up_pre * sigmoid_gate * (1.0 + gate_pre * (1.0 - sigmoid_gate))
@@ -508,13 +531,43 @@
     up_grad_low = (hidden_grad * swish).astype(bf16)
     ffn_back = (dot_cols(gate_grad_low, gate_full) + dot_cols(up_grad_low, up_full)).astype(bf16)
     ffn_back_rows = scatter_rows(ffn_back)
-    ffn_kept = after(ffn_input, ffn_back)
-    gate_recv = to_owners(dot_rows(ffn_kept, gate_grad_low))
-    up_recv = to_owners(dot_rows(ffn_kept, up_grad_low))
+    input_half = half_cols(after(ffn_input, ffn_back))
+    gate_grad = dot_rows(input_half, gate_grad_low).astype(bf16)
+    gate_recv = to_half(gate_grad)
+    up_grad = dot_rows(input_half, up_grad_low).astype(bf16)
+    up_recv = to_half(up_grad)
+    hidden = after(hidden, gate_grad, up_grad)
+    ffn_sum = dot_cols(hidden, down_full).astype(bf16)
+    ffn_part = scatter_rows(ffn_sum)
+    layer_out = (residual + ffn_part).astype(bf16)
+
+    other_input = after(other_input, ffn_sum)
+    gate_pre = dot(other_input, gate_full)
+    up_pre = dot(other_input, up_full)
+    sigmoid_gate = jax.nn.sigmoid(gate_pre)
+    swish = gate_pre * sigmoid_gate
+    hidden = (swish * up_pre).astype(bf16)
+    mark = tick(hidden)
+    other_dy = after(other_dy, mark)
+    down_grad = dot_rows(half_cols(other_dy), hidden).astype(bf16)
+    down_recv2 = to_half(down_grad)
+    hidden_grad = dot(after(other_dy, down_grad), down_full)
+    gate_grad_low = (
+        hidden_grad * up_pre * sigmoid_gate * (1.0 + gate_pre * (1.0 - sigmoid_gate))
+    ).astype(bf16)
+    up_grad_low = (hidden_grad * swish).astype(bf16)
+    input_half = half_cols(other_input)
+    gate_grad = dot_rows(input_half, gate_grad_low).astype(bf16)
+    gate_recv2 = to_half(gate_grad)
+    up_grad = dot_rows(input_half, up_grad_low).astype(bf16)
+    up_recv2 = to_half(up_grad)
+    mark = tick(up_grad)
+
     cotan_rows = cotangent.astype(jnp.float32)
     resid_grad = cotan_rows + norm_back(ffn_back_rows, scaled_two, factor_two, norm_gains[1])
     gain_two = jnp.sum(ffn_back_rows * scaled_two, axis=0)
     resid_all = gather_rows(resid_grad.astype(bf16), "tensor")
+    resid_all = after(resid_all, mark)
     mixed_grad = dot(resid_all, out_full).astype(bf16)
     out_recv = to_owners(dot_rows(resid_all, mixed_all))
     raw_grads = attn_bwd(
@@ -532,21 +585,24 @@
     gain_slots = own_group[:, None, None] * jnp.stack([gain_one, gain_two])[None]
     gain_grad = lax.psum(gain_slots, ("dp", "tensor"))
     order = after(order, gain_slots)
+    near = lax.axis_size("dp") // 2
+    side = order // near != lax.axis_index("dp") // near
+    near_order = order % near + near * side.astype(jnp.int32)
 
     down_new = optimize(
-        order, down_recv, down_weight, down_first, down_second, down_outer, 3, turned=True
+        near_order, (down_recv, down_recv2), down_weight, down_first, down_second, down_outer, 3, turned=True
     )
     gate_half = optimize(
-        order, gate_recv, gate_weight, gate_first, gate_second, gate_outer, 2, member=0
+        near_order, (gate_recv, gate_recv2), gate_weight, gate_first, gate_second, gate_outer, 2, member=0
     )
     gate_new = optimize(
-        order, up_recv, gate_weight, gate_first, gate_second, gate_outer, 2, member=1, before=gate_half
+        near_order, (up_recv, up_recv2), gate_weight, gate_first, gate_second, gate_outer, 2, member=1, before=gate_half
     )
     out_new = optimize(
-        order, out_recv, out_weight, out_first, out_second, out_outer, 1, turned=True
+        order, (out_recv,), out_weight, out_first, out_second, out_outer, 1, turned=True
     )
     qkv_new = optimize(
-        order, after(qkv_recv, gain_grad), qkv_weight, qkv_first, qkv_second, qkv_outer, 0
+        order, (after(qkv_recv, gain_grad),), qkv_weight, qkv_first, qkv_second, qkv_outer, 0
     )
     gains_new = update(
         norm_gains, gain_grad, gains_first, gains_second, gains_outer, inner_rates[4], decays[4]

time: 1530 us -> 1490 us (0.974)
  waiting for transfers between devices: 757 us -> 488 us
  matrix products: 315 us -> 418 us
  starting transfers between devices: 39.8 us -> 96.8 us
  blocking collectives: 88.1 us -> 140 us
    all_to_all x5 -> x2, waiting for transfers between devices: 422 us -> 81.3 us  [to_owners(): return lax.all_to_all(blocks, 'dp', split_axis=0, concat_axis=0)]
    all_gather x7 -> x8, waiting for transfers between devices: 195 us -> 0.01 us  [gather_rows(): return lax.all_gather(part, axis, axis=0, tiled=True)]
    ppermute x0 -> x2, waiting for transfers between devices: none -> 189 us  [to_partner(): lax.ppermute(part, 'dp', [(i, (i + count // 2) % count) for i in range(co...]
    dot_general x5 -> x8, matrix products: 116 us -> 193 us  [dot(): return jnp.dot(left, right, preferred_element_type=jnp.float32)]
    all_to_all x2 -> x3, waiting for transfers between devices: 80.1 us -> 154 us  [spread_rows(): parts = lax.all_to_all(copies, 'tensor', split_axis=0, concat_axis=0)]
    all_to_all x0 -> x5, waiting for transfers between devices: none -> 60.8 us  [to_half(): lax.all_to_all(blocks, 'dp', split_axis=0, concat_axis=0, axis_index_grou...]
    reduce_scatter x3, waiting for transfers between devices: 57 us -> 0.04 us  [scatter_rows(): lax.psum_scatter(part.astype(jnp.bfloat16), 'tensor', scatter_dimension=0...]
    all_to_all x0 -> x1, blocking collectives: none -> 52.2 us  [to_half(): lax.all_to_all(blocks, 'dp', split_axis=0, concat_axis=0, axis_index_grou...]
  transfers between devices with their start and end apart: 18 -> 24, of which waited for: 10 -> 9; matrix products, arithmetic and copies ran while one was open for 16% -> 33% of each run, Pallas kernels for 14% -> 15%
where the time goes in v3:
time: 1490 us; the launch traced here: 1480 us
  waiting for transfers between devices  488 us (33%)
  matrix products  418 us (28%)
  Pallas kernels  241 us (16%)
  blocking collectives  140 us (9%)
  starting transfers between devices  96.8 us (6%)
  other arithmetic  53.3 us (4%)
  local copies, waits for them, and re-layouts  28.7 us (2%)
  between operations  15.2 us (1%)
    dot_general x8, matrix products, dot(): return jnp.dot(left, right, preferred_element_type=jnp.float32)  193 us
    ppermute x2, waiting for transfers between devices, to_partner(): lax.ppermute(part, 'dp', [(i, (i + count // 2) % count) for i in range(co...  189 us
    all_to_all x3, waiting for transfers between devices, spread_rows(): parts = lax.all_to_all(copies, 'tensor', split_axis=0, concat_axis=0)  154 us
    dot_general x8, matrix products, dot_rows(): lax.dot_general(left, right, (((0,), (0,)), ((), ())), preferred_element_...  127 us
    dot_general x5, matrix products, dot_cols(): lax.dot_general(left, right, (((1,), (1,)), ((), ())), preferred_element_...  97.8 us
    pallas_call x5, Pallas kernels, optimize(): pl.pallas_call(functools.partial(opt_kernel, sources // GROUPS, turned, l...  88.4 us
    all_to_all x1, blocking collectives, sum_rows(): parts = lax.all_to_all(blocks, 'tensor', split_axis=0, concat_axis=0)  88 us
    all_to_all x2, waiting for transfers between devices, to_owners(): return lax.all_to_all(blocks, 'dp', split_axis=0, concat_axis=0)  81.3 us
  transfers between devices with their start and end apart: 24, of which 9 were waited for; matrix products, arithmetic and copies ran while one was open for 33% of the time, Pallas kernels for 15%

profile of v3, /device:TPU:1, one launch (start us, length us, event | category | flops | bytes accessed | tf_op | source)
XLA Modules:
  0.0 1480.9 jit_solution(7085444814649584890)
XLA Ops:
  11.7 2.5 convert.10
  17.4 4.8 broadcast_in_dim.12
  22.2 5.8 all-to-all-start
  35.4 3.7 fusion.38
  40.8 79.8 %all-to-all-done = bf16[4,512,2048]{2,1,0:T(8,128)(2,1)} async-done(((bf16[4,512,2048]{2,1,0:T(8,128)(2,1)}), bf16[4,512,2048]{2,1,0:T(8,128)(2,1)}, u32[]{:S(2)}, u32[]{:S(2)}) %all-to-all-start) | async-done | bytes 8388640 | tf_op jit(solution)/shard_map/all_to_all | solution.py:420
  120.6 19.5 %fusion.57.q_ref.k_ref.v_ref = f32[2048,1536]{1,0:T(8,128)} fusion(bf16[2048,2048]{1,0:T(8,128)(2,1)} %bitcast.7, bf16[2048,1536]{1,0:T(8,128)(2,1)} %all-gather.11.cloned.1.call-done), kind=kOutput, calls=%fused_computation.119 | convolution fusion | flops 12884901888 | bytes 27262976 | tf_op jit(solution)/shard_map/dot_general | solution.py:385
  140.1 73.8 %attn_fwd.1 = (bf16[2048,512]{1,0:T(8,128)(2,1)}, bf16[2048,512]{1,0:T(8,128)(2,1)}, bf16[2048,512]{1,0:T(8,128)(2,1)}, bf16[2048,512]{1,0:T(8,128)(2,1)}, f32[4,2,2048]{2,1,0:T(2,128)S(1)}) custom-call(s32[6,4]{1,0:T(8,128)S(1)} %stack.36.info, f32[2048,1536]{1,0:T(8,128)} %fusion.57.q_ref.k_ref.v_ref, f32[2048,1536]{1,0:T(8,128)} %fusion.57.q_ref.k_ref.v_ref, ...), custom_call_target="tpu_custom_call" | custom-call | flops 5153960960 | bytes 12582912 | tf_op jit(solution)/shard_map/attn_fwd/pallas_call | solution.py:106
  213.9 6.7 convolution_convert_fusion.2
  220.7 88.0 %all_to_all.60 = bf16[4,512,2048]{2,1,0:T(8,128)(2,1)S(1)} all-to-all(bf16[4,512,2048]{2,1,0:T(8,128)(2,1)S(1)} %bitcast.79), channel_id=1, replica_groups=mesh['dp'=8,'tensor'=4] {'tensor'}, dimensions={0} | all-to-all | bytes 16777216 | tf_op jit(solution)/shard_map/all_to_all | solution.py:427
  308.7 3.9 convert_reduce_fusion
  312.6 2.8 multiply_reduce_fusion
  315.5 2.0 copy-done.16
  319.8 6.1 broadcast_in_dim.14
  325.9 5.7 all-to-all-start.2
  331.6 14.9 %collective-permute-start = (bf16[512,2048]{1,0:T(8,128)(2,1)}, bf16[512,2048]{1,0:T(8,128)(2,1)}, u32[]{:S(2)}, u32[]{:S(2)}) collective-permute-start(bf16[512,2048]{1,0:T(8,128)(2,1)} %multiply_convert_fusion.8.source), channel_id=1, source_target_pairs={{0,16},{4,20},{8,24},{12,28},{16,0},{20,4},{24,8},{28,12},{1,17},{... | collective-permute-start | bytes 6291464 | tf_op jit(solution)/shard_map/ppermute | solution.py:448
  346.5 98.0 %collective-permute-done = bf16[512,2048]{1,0:T(8,128)(2,1)} collective-permute-done((bf16[512,2048]{1,0:T(8,128)(2,1)}, bf16[512,2048]{1,0:T(8,128)(2,1)}, u32[]{:S(2)}, u32[]{:S(2)}) %collective-permute-start) | collective-permute-done | bytes 2097184 | tf_op jit(solution)/shard_map/ppermute | solution.py:448
  444.6 6.1 broadcast_in_dim.15
  450.7 5.9 all-to-all-start.3
  456.6 24.2 %fusion.58 = f32[2048,2048]{1,0:T(8,128)} fusion(bf16[2048,2048]{1,0:T(8,128)(2,1)} %bitcast.18, bf16[2048,2048]{1,0:T(8,128)(2,1)} %bitcast.104), kind=kOutput, calls=%fused_computation.120 | convolution fusion | flops 17179869184 | bytes 33554432 | tf_op jit(solution)/shard_map/dot_general | solution.py:385
  480.8 28.1 %multiply_convert_fusion.5 = (bf16[2048,2048]{1,0:T(8,128)(2,1)}, f32[2048,2048]{1,0:T(8,128)}) fusion(f32[2048,2048]{1,0:T(8,128)} %fusion.58, bf16[2048,2048]{1,0:T(8,128)(2,1)} %bitcast.18, bf16[2048,2048]{1,0:T(8,128)(2,1)} %bitcast.101), kind=kOutput, calls=%fused_computation.8 | convolution fusion | flops 17205035008 | bytes 58720256 | tf_op jit(solution)/shard_map/dot_general | solution.py:385
  508.9 74.5 %all-to-all-done.3 = bf16[4,512,2048]{2,1,0:T(8,128)(2,1)} async-done(((bf16[4,512,2048]{2,1,0:T(8,128)(2,1)}), bf16[4,512,2048]{2,1,0:T(8,128)(2,1)}, u32[]{:S(2)}, u32[]{:S(2)}) %all-to-all-start.3) | async-done | bytes 8388640 | tf_op jit(solution)/shard_map/all_to_all | solution.py:420
  583.3 14.2 fusion.25.source
  598.1 34.4 %multiply_convert_fusion.3 = (bf16[2048,2048]{1,0:T(8,128)(2,1)}, bf16[2048,2048]{1,0:T(8,128)(2,1)}) fusion(f32[2048,2048]{1,0:T(8,128)} %fusion.58, f32[2048,2048]{1,0:T(8,128)} %get-tuple-element.170, bf16[2048,2048]{1,0:T(8,128)(2,1)} %bitcast.19, bf16[2048,2048]{0,1:T(8,128)(2,1)} %all-gather.15.cloned.1.call-done), kind=kOutput, calls=%fused_computation.6 | convolution fusion | flops 17234395136 | bytes 67108864 | tf_op jit(solution)/shard_map/dot_general | solution.py:385
  632.4 24.5 %fusion.59 = f32[2048,2048]{1,0:T(8,128)} fusion(bf16[2048,2048]{1,0:T(8,128)(2,1)} %get-tuple-element.156, bf16[2048,2048]{1,0:T(8,128)(2,1)} %bitcast.105), kind=kOutput, calls=%fused_computation.121 | convolution fusion | flops 17179869184 | bytes 33554432 | tf_op jit(solution)/shard_map/dot_general | solution.py:389
  657.0 25.5 %add_convert_fusion = bf16[2048,2048]{1,0:T(8,128)(2,1)} fusion(f32[2048,2048]{1,0:T(8,128)} %fusion.59, bf16[2048,2048]{1,0:T(8,128)(2,1)} %get-tuple-element.155, bf16[2048,2048]{1,0:T(8,128)(2,1)} %bitcast.102), kind=kOutput, calls=%fused_computation.5 | convolution fusion | flops 17188257792 | bytes 41943040 | tf_op jit(solution)/shard_map/dot_general | solution.py:389
  682.6 2.3 collective-permute-start.1
  684.9 90.6 %collective-permute-done.1 = bf16[512,2048]{1,0:T(8,128)(2,1)} collective-permute-done((bf16[512,2048]{1,0:T(8,128)(2,1)}, bf16[512,2048]{1,0:T(8,128)(2,1)}, u32[]{:S(2)}, u32[]{:S(2)}) %collective-permute-start.1) | collective-permute-done | bytes 2097184 | tf_op jit(solution)/shard_map/ppermute | solution.py:448
  775.5 14.4 convolution_convert_fusion.5
  789.9 14.0 convolution_convert_fusion.4
  803.9 6.2 all-to-all-start.6
  810.1 23.7 %convolution_convert_fusion.1 = bf16[2048,2048]{1,0:T(8,128)(2,1)} fusion(bf16[2048,2048]{1,0:T(8,128)(2,1)} %get-tuple-element.92, bf16[2048,2048]{0,1:T(8,128)(2,1)} %all-gather.15.cloned.1.call-done), kind=kOutput, calls=%fused_computation.17 | convolution fusion | flops 17184063488 | bytes 25165824 | tf_op jit(solution)/shard_map/dot_general | solution.py:389
  833.8 24.2 %fusion.60 = f32[2048,2048]{1,0:T(8,128)} fusion(bf16[2048,2048]{1,0:T(8,128)(2,1)} %all-gather.19.cloned.1.call-done, bf16[2048,2048]{1,0:T(8,128)(2,1)} %bitcast.106), kind=kOutput, calls=%fused_computation.122 | convolution fusion | flops 17179869184 | bytes 33554432 | tf_op jit(solution)/shard_map/dot_general | solution.py:385
  858.0 4.7 fusion.16
  863.3 5.0 fusion.50
  868.3 28.5 %multiply_convert_fusion.2 = (bf16[2048,2048]{1,0:T(8,128)(2,1)}, f32[2048,2048]{1,0:T(8,128)}) fusion(f32[2048,2048]{1,0:T(8,128)} %fusion.60, bf16[2048,2048]{1,0:T(8,128)(2,1)} %all-gather.19.cloned.1.call-done, bf16[2048,2048]{1,0:T(8,128)(2,1)} %bitcast.103), kind=kOutput, calls=%fused_computation.2 | convolution fusion | flops 17205035008 | bytes 58720256 | tf_op jit(solution)/shard_map/dot_general | solution.py:385
  897.4 14.0 fusion.28
  911.4 5.4 all-to-all-start.8
  916.7 24.4 %fusion.61 = f32[2048,2048]{1,0:T(8,128)} fusion(bf16[2048,2048]{1,0:T(8,128)(2,1)} %all-gather.21.cloned.1.call-done, bf16[2048,2048]{0,1:T(8,128)(2,1)} %all-gather.15.cloned.1.call-done), kind=kOutput, calls=%fused_computation.123 | convolution fusion | flops 17179869184 | bytes 33554432 | tf_op jit(solution)/shard_map/dot_general | solution.py:385
  941.1 17.8 %fusion.32.source = bf16[1024,2048]{1,0:T(8,128)(2,1)} fusion(f32[2048,2048]{1,0:T(8,128)} %fusion.61, bf16[2048,2048]{1,0:T(8,128)(2,1)} %all-gather.19.cloned.1.call-done, s32[]{:T(128)S(6)} %select_n.30, f32[2048,2048]{1,0:T(8,128)} %fusion.60), kind=kOutput, calls=%fused_computation.55 | convolution fusion | flops 8617197568 | bytes 41943044 | tf_op jit(solution)/shard_map/dot_general | solution.py:393
  959.5 9.9 convolution_convert_fusion.7.do_ref
  969.4 5.0 all-to-all-start.10
  974.4 76.0 %attn_bwd.1 = (bf16[2048,512]{1,0:T(8,128)(2,1)S(1)}, bf16[2048,512]{1,0:T(8,128)(2,1)}, bf16[2048,512]{1,0:T(8,128)(2,1)}) custom-call(s32[6,4]{1,0:T(8,128)S(1)} %stack.36.info, bf16[2048,512]{1,0:T(8,128)(2,1)} %get-tuple-element.93.q_ref, bf16[2048,512]{1,0:T(8,128)(2,1)} %get-tuple-element.94.k_ref, bf16[2048,512]{1,0:T(8,128)(2,1)} %get-tuple-element.95.v_ref, ...), custom_call_target="tpu_custom_call" | custom-call | flops 12884901888 | bytes 16777216 | tf_op jit(solution)/shard_map/attn_bwd/pallas_call | solution.py:202
  1050.5 1.9 constant_dynamic-update-slice_fusion.1
  1052.8 2.7 copy-done.21
  1055.5 17.4 %convolution_convert_fusion = bf16[2048,2048]{1,0:T(8,128)(2,1)} fusion(bf16[2048,1536]{1,0:T(8,128)(2,1)S(1)} %constant_dynamic-update-slice_fusion, bf16[2048,1536]{1,0:T(8,128)(2,1)} %all-gather.11.cloned.1.call-done), kind=kOutput, calls=%fused_computation.16 | convolution fusion | flops 12889096192 | bytes 20971520 | tf_op jit(solution)/shard_map/dot_general | solution.py:389
  1072.9 28.7 %all-to-all-start.7 = ((bf16[4,256,2048]{2,1,0:T(8,128)(2,1)}), bf16[4,256,2048]{2,1,0:T(8,128)(2,1)}, u32[]{:S(2)}, u32[]{:S(2)}) async-start(bf16[4,256,2048]{2,1,0:T(8,128)(2,1)} %bitcast.78), calls=%async_computation.10 | async-start | bytes 8388608 | tf_op jit(solution)/shard_map/all_to_all | solution.py:443
  1101.6 24.4 %fusion.31 = bf16[1024,2048]{1,0:T(8,128)(2,1)} fusion(f32[2048,2048]{1,0:T(8,128)} %fusion.60, f32[2048,2048]{1,0:T(8,128)} %fusion.61, f32[2048,2048]{1,0:T(8,128)} %get-tuple-element.172, bf16[2048,2048]{1,0:T(8,128)(2,1)} %all-gather.19.cloned.1.call-done, s32[]{:T(128)S(6)} %select_n.30), kind=kOutput, calls=%fused_computation.54 | convolution fusion | flops 8633974784 | bytes 58720260 | tf_op jit(solution)/shard_map/dot_general | solution.py:393
  1126.0 23.7 %all-to-all-done.7.refs_1_ = bf16[4,256,2048]{2,1,0:T(8,128)(2,1)} async-done(((bf16[4,256,2048]{2,1,0:T(8,128)(2,1)}), bf16[4,256,2048]{2,1,0:T(8,128)(2,1)}, u32[]{:S(2)}, u32[]{:S(2)}) %all-to-all-start.7) | async-done | bytes 4194336 | tf_op jit(solution)/shard_map/all_to_all | solution.py:443
  1149.7 52.2 %all_to_all.61.refs_1_ = bf16[4,256,2048]{2,1,0:T(8,128)(2,1)} all-to-all(bf16[4,256,2048]{2,1,0:T(8,128)(2,1)} %bitcast.84), channel_id=1, replica_groups={{0,4,8,12},{16,20,24,28},{1,5,9,13},{17,21,25,29},{2,6,10,14},{18,22,26..., dimensions={0} | all-to-all | bytes 8388608 | tf_op jit(solution)/shard_map/all_to_all | solution.py:443
  1201.9 6.0 all-to-all-start.11
  1208.6 9.4 convolution_convert_fusion.6
  1218.1 37.1 %all-to-all-done.11.refs_1_ = bf16[4,256,2048]{2,1,0:T(8,128)(2,1)} async-done(((bf16[4,256,2048]{2,1,0:T(8,128)(2,1)}), bf16[4,256,2048]{2,1,0:T(8,128)(2,1)}, u32[]{:S(2)}, u32[]{:S(2)}) %all-to-all-start.11) | async-done | bytes 4194336 | tf_op jit(solution)/shard_map/all_to_all | solution.py:443
  1255.2 4.5 all-to-all-start.5
  1259.7 19.2 %convolution_convert_fusion.3 = bf16[2048,1536]{1,0:T(8,128)(2,1)} fusion(bf16[2048,2048]{1,0:T(8,128)(2,1)} %bitcast.7, bf16[2048,1536]{1,0:T(8,128)(2,1)} %copy-done.21), kind=kOutput, calls=%fused_computation.19 | convolution fusion | flops 12888047616 | bytes 20971520 | tf_op jit(solution)/shard_map/dot_general | solution.py:393
  1278.9 28.9 %all-to-all-done.5.refs_0_ = bf16[8,256,512]{2,1,0:T(8,128)(2,1)S(1)} async-done(((bf16[8,256,512]{2,1,0:T(8,128)(2,1)}), bf16[8,256,512]{2,1,0:T(8,128)(2,1)S(1)}, u32[]{:S(2)}, u32[]{:S(2)}) %all-to-all-start.5) | async-done | bytes 2097184 | tf_op jit(solution)/shard_map/all_to_all | solution.py:460
  1307.8 5.7 all-to-all-start.4
  1316.1 3.6 fusion.19
  1320.5 8.4 fusion.12
  1329.0 4.7 optimize.6
  1333.7 22.3 %optimize.7 = (f32[4,2,256,2048]{3,2,1,0:T(8,128)}, f32[4,2,256,2048]{3,2,1,0:T(8,128)}, f32[2,256,2048]{2,1,0:T(8,128)}, f32[2,256,2048]{2,1,0:T(8,128)}, f32[2...) custom-call(s32[8]{0:T(128)S(1)} %fusion.47.order, bf16[4,256,2048]{2,1,0:T(8,128)(2,1)} %all-to-all-done.8.refs_0_, ...), custom_call_target="tpu_custom_call" | custom-call | flops 31457280 | bytes 53477376 | tf_op jit(solution)/shard_map/optimize/pallas_call | solution.py:367
  1356.0 21.6 %optimize.9 = (f32[4,2048,256]{2,1,0:T(8,128)}, f32[4,2048,256]{2,1,0:T(8,128)}, f32[2048,256]{1,0:T(8,128)}, f32[2048,256]{1,0:T(8,128)}, f32[2048,256]{1,0:T(8,128)}, /*index=5*/bf16[2048,256]{1,0:T(8,128)(2,1)}) custom-call(s32[8]{0:T(128)S(1)} %fusion.47.order, bf16[4,256,2048]{2,1,0:T(8,128)(2,1)} %all-to-all-done.10.refs_0_, ...), custom_call_target="tpu_custom_call" | custom-call | flops 31457280 | bytes 53477376 | tf_op jit(solution)/shard_map/optimize/pallas_call | solution.py:367
  1377.7 23.3 %optimize.8 = (f32[4,2,256,2048]{3,2,1,0:T(8,128)}, f32[4,2,256,2048]{3,2,1,0:T(8,128)}, f32[2,256,2048]{2,1,0:T(8,128)}, f32[2,256,2048]{2,1,0:T(8,128)}, f32[2...) custom-call(s32[8]{0:T(128)S(1)} %fusion.47.order, ...), custom_call_target="tpu_custom_call", output_to_operand_aliasing={{0}: (7, {}), {1}: (8, {}), {2}: (9, {}), {3}: (10, {}), {4... | custom-call | flops 31457280 | bytes 53477376 | tf_op jit(solution)/shard_map/optimize/pallas_call | solution.py:367
  1401.0 52.4 %all-to-all-done.4.refs_0_ = bf16[8,256,1536]{2,1,0:T(8,128)(2,1)} async-done(((bf16[8,256,1536]{2,1,0:T(8,128)(2,1)}), bf16[8,256,1536]{2,1,0:T(8,128)(2,1)}, u32[]{:S(2)}, u32[]{:S(2)}) %all-to-all-start.4) | async-done | bytes 6291488 | tf_op jit(solution)/shard_map/all_to_all | solution.py:460
  1457.3 16.5 %optimize.5 = (f32[4,3,256,512]{3,2,1,0:T(8,128)}, f32[4,3,256,512]{3,2,1,0:T(8,128)}, f32[3,256,512]{2,1,0:T(8,128)}, f32[3,256,512]{2,1,0:T(8,128)}, f32[3,256...) custom-call(s32[8]{0:T(128)S(1)} %get-tuple-element.106.order, bf16[8,256,1536]{2,1,0:T(8,128)(2,1)} %all-to-all-done.4.refs_0_, ...), custom_call_target="tpu_custom_call" | custom-call | flops 23592960 | bytes 40108032 | tf_op jit(solution)/shard_map/optimize/pallas_call | solution.py:367
  (171 shorter events, 29.9 us)
Async XLA Ops:
  7.2 113.4 %all-gather.11.cloned.1.call-start = ((), (), s32[]{:S(2)}) async-start(), calls=%async_computation.15 | async-start | bytes 7077888 | tf_op jit(solution)/shard_map/all_gather | solution.py:414
  8.8 7.4 copy-start.18
  9.8 7.0 copy-start.27
  9.8 204.1 %all-gather.13.cloned.1.call-start = ((), (), s32[]{:S(2)}) async-start(), calls=%async_computation.16 | async-start | bytes 2359296 | tf_op jit(solution)/shard_map/all_gather | solution.py:414
  11.6 308.2 %all-gather.23.cloned.1.call-start = ((), (), s32[]{:S(2)}) async-start(), calls=%async_computation.25 | async-start | bytes 9437184 | tf_op jit(solution)/shard_map/all_gather | solution.py:414
  15.7 304.1 %all-gather.25.cloned.1.call-start = ((), (), s32[]{:S(2)}) async-start(), calls=%async_computation.26 | async-start | bytes 9437184 | tf_op jit(solution)/shard_map/all_gather | solution.py:414
  16.8 5.5 copy-start.34
  16.8 5.4 copy-start.25
  16.8 298.7 %copy-start.22 = (f32[1,2048]{1,0:T(1,128)}, f32[1,2048]{1,0:T(1,128)S(1)}, u32[]{:S(2)}) copy-start(f32[1,2048]{1,0:T(1,128)S(1)} %get-tuple-element.164) | copy-start | bytes 24580
  22.2 6.1 copy-start.2
  22.2 7.2 copy-start.40
  22.2 7.2 copy-start.41
  22.2 98.4 %all-to-all-start = ((bf16[4,512,2048]{2,1,0:T(8,128)(2,1)}), bf16[4,512,2048]{2,1,0:T(8,128)(2,1)}, u32[]{:S(2)}, u32[]{:S(2)}) async-start(bf16[4,512,2048]{2,1,0:T(8,128)(2,1)} %broadcast_in_dim.12), calls=%async_computation | async-start | bytes 16777216 | tf_op jit(solution)/shard_map/all_to_all | solution.py:420
  28.1 570.0 %all-gather.15.cloned.1.call-start = ((), (), s32[]{:S(2)}) async-start(), calls=%async_computation.17 | async-start | bytes 9437184 | tf_op jit(solution)/shard_map/all_gather | solution.py:414
  31.2 7.9 copy-start.14
  33.0 6.1 copy-start.12
  120.6 19.5 %copy-start.5 = (s32[2048,1]{1,0:T(8,128)S(1)}, s32[2048,1]{1,0:T(8,128)}, u32[]{:S(2)}) copy-start(s32[2048,1]{1,0:T(8,128)} %copy.69.hi_ref) | copy-start | bytes 24580
  308.7 3.9 copy-start.19
  315.5 10.4 copy-start.31
  325.9 118.7 %all-to-all-start.2 = ((bf16[4,512,2048]{2,1,0:T(8,128)(2,1)}), bf16[4,512,2048]{2,1,0:T(8,128)(2,1)}, u32[]{:S(2)}, u32[]{:S(2)}) async-start(bf16[4,512,2048]{2,1,0:T(8,128)(2,1)} %broadcast_in_dim.14), calls=%async_computation.2 | async-start | bytes 16777216 | tf_op jit(solution)/shard_map/all_to_all | solution.py:420
  331.5 502.2 %all-gather.19.cloned.1.call-start = ((), (), s32[]{:S(2)}) async-start(), calls=%async_computation.21 | async-start | bytes 10485760 | tf_op jit(solution)/shard_map/all_gather | solution.py:414
  331.6 112.9 %collective-permute-start = (bf16[512,2048]{1,0:T(8,128)(2,1)}, bf16[512,2048]{1,0:T(8,128)(2,1)}, u32[]{:S(2)}, u32[]{:S(2)}) collective-permute-start(bf16[512,2048]{1,0:T(8,128)(2,1)} %multiply_convert_fusion.8.source), channel_id=1, source_target_pairs={{0,16},{4,20},{8,24},{12,28},{16,0},{20,4},{24,8},{28,12},{1,17},{... | collective-permute-start | bytes 6291464 | tf_op jit(solution)/shard_map/ppermute | solution.py:448
  450.7 132.7 %all-to-all-start.3 = ((bf16[4,512,2048]{2,1,0:T(8,128)(2,1)}), bf16[4,512,2048]{2,1,0:T(8,128)(2,1)}, u32[]{:S(2)}, u32[]{:S(2)}) async-start(bf16[4,512,2048]{2,1,0:T(8,128)(2,1)} %broadcast_in_dim.15), calls=%async_computation.3 | async-start | bytes 16777216 | tf_op jit(solution)/shard_map/all_to_all | solution.py:420
  456.5 401.5 %reduce-scatter.6.cloned.1.call-start = ((), (), s32[]{:S(2)}) async-start(), calls=%async_computation.19 | async-start | bytes 10485760 | tf_op jit(solution)/shard_map/reduce_scatter | solution.py:432
  682.5 214.9 %all-gather.21.cloned.1.call-start = ((), (), s32[]{:S(2)}) async-start(), calls=%async_computation.22 | async-start | bytes 10485760 | tf_op jit(solution)/shard_map/all_gather | solution.py:414
  682.6 92.9 %collective-permute-start.1 = (bf16[512,2048]{1,0:T(8,128)(2,1)}, bf16[512,2048]{1,0:T(8,128)(2,1)}, u32[]{:S(2)}, u32[]{:S(2)}) collective-permute-start(bf16[512,2048]{1,0:T(8,128)(2,1)} %param.26), channel_id=1, source_target_pairs={{0,16},{4,20},{8,24},{12,28},{16,0},{20,4},{24,8},{28,12},{1,17},{... | collective-permute-start | bytes 6291464 | tf_op jit(solution)/shard_map/ppermute | solution.py:448
  803.9 107.5 %all-to-all-start.6 = ((bf16[4,256,2048]{2,1,0:T(8,128)(2,1)}), bf16[4,256,2048]{2,1,0:T(8,128)(2,1)}, u32[]{:S(2)}, u32[]{:S(2)}) async-start(bf16[4,256,2048]{2,1,0:T(8,128)(2,1)} %bitcast.83), calls=%async_computation.9 | async-start | bytes 8388608 | tf_op jit(solution)/shard_map/all_to_all | solution.py:443
  810.1 149.4 %all-gather.17.cloned.1.call-start = ((), (), s32[]{:S(2)}) async-start(), calls=%async_computation.20 | async-start | bytes 10485760 | tf_op jit(solution)/shard_map/all_gather | solution.py:414
  833.7 24.2 %copy-start.23 = (f32[1,2048]{1,0:T(1,128)S(1)}, f32[1,2048]{1,0:T(1,128)}, u32[]{:S(2)}) copy-start(f32[1,2048]{1,0:T(1,128)} %copy-done.22) | copy-start | bytes 24580
  833.8 24.2 %copy-start.32 = (f32[512]{0:T(512)S(1)}, f32[512]{0:T(512)}, u32[]{:S(2)}) copy-start(f32[512]{0:T(512)} %copy-done.31) | copy-start | bytes 6148
  858.0 5.3 copy-start.17
  911.4 58.0 %all-to-all-start.8 = ((bf16[4,256,2048]{2,1,0:T(8,128)(2,1)}), bf16[4,256,2048]{2,1,0:T(8,128)(2,1)}, u32[]{:S(2)}, u32[]{:S(2)}) async-start(bf16[4,256,2048]{2,1,0:T(8,128)(2,1)} %bitcast.82), calls=%async_computation.11 | async-start | bytes 8388608 | tf_op jit(solution)/shard_map/all_to_all | solution.py:443
  969.4 5.0 copy-start.13
  969.4 5.1 copy-start.15
  969.4 103.5 %all-to-all-start.10 = ((bf16[4,256,2048]{2,1,0:T(8,128)(2,1)}), bf16[4,256,2048]{2,1,0:T(8,128)(2,1)}, u32[]{:S(2)}, u32[]{:S(2)}) async-start(bf16[4,256,2048]{2,1,0:T(8,128)(2,1)} %bitcast.77), calls=%async_computation.13 | async-start | bytes 8388608 | tf_op jit(solution)/shard_map/all_to_all | solution.py:443
  974.4 341.7 %reduce-scatter.8.cloned.1.call-start = ((), (), s32[]{:S(2)}) async-start(), calls=%async_computation.23 | async-start | bytes 10485760 | tf_op jit(solution)/shard_map/reduce_scatter | solution.py:432
  1072.9 76.9 %all-to-all-start.7 = ((bf16[4,256,2048]{2,1,0:T(8,128)(2,1)}), bf16[4,256,2048]{2,1,0:T(8,128)(2,1)}, u32[]{:S(2)}, u32[]{:S(2)}) async-start(bf16[4,256,2048]{2,1,0:T(8,128)(2,1)} %bitcast.78), calls=%async_computation.10 | async-start | bytes 8388608 | tf_op jit(solution)/shard_map/all_to_all | solution.py:443
  1201.9 6.7 copy-start.42
  1201.9 53.3 %all-to-all-start.11 = ((bf16[4,256,2048]{2,1,0:T(8,128)(2,1)}), bf16[4,256,2048]{2,1,0:T(8,128)(2,1)}, u32[]{:S(2)}, u32[]{:S(2)}) async-start(bf16[4,256,2048]{2,1,0:T(8,128)(2,1)} %bitcast.81), calls=%async_computation.14 | async-start | bytes 8388608 | tf_op jit(solution)/shard_map/all_to_all | solution.py:443
  1207.9 112.5 %reduce-scatter.4.cloned.1.call-start = ((), (), s32[]{:S(2)}) async-start(), calls=%async_computation.18 | async-start | bytes 10485760 | tf_op jit(solution)/shard_map/reduce_scatter | solution.py:432
  1255.2 52.6 %all-to-all-start.5 = ((bf16[8,256,512]{2,1,0:T(8,128)(2,1)}), bf16[8,256,512]{2,1,0:T(8,128)(2,1)S(1)}, u32[]{:S(2)}, u32[]{:S(2)}) async-start(bf16[8,256,512]{2,1,0:T(8,128)(2,1)} %bitcast.85), calls=%async_computation.8 | async-start | bytes 4194304 | tf_op jit(solution)/shard_map/all_to_all | solution.py:460
  1278.8 35.0 %copy-start.43 = (s32[8]{0:T(128)S(1)}, s32[8]{0:T(128)}, u32[]{:S(2)}) copy-start(s32[8]{0:T(128)} %param.29) | copy-start | bytes 100
  1278.8 37.2 %copy-start.26 = (f32[1,2048]{1,0:T(1,128)S(1)}, f32[1,2048]{1,0:T(1,128)}, u32[]{:S(2)}) copy-start(f32[1,2048]{1,0:T(1,128)} %copy-done.25) | copy-start | bytes 24580
  1278.9 37.2 %copy-start.35 = (f32[512]{0:T(512)S(1)}, f32[512]{0:T(512)}, u32[]{:S(2)}) copy-start(f32[512]{0:T(512)} %copy-done.34) | copy-start | bytes 6148
  1307.8 11.8 copy-start.36
  1307.8 12.7 copy-start.24
  1307.8 12.7 copy-start.33
  1307.8 12.7 copy-start.38
  1307.8 145.6 %all-to-all-start.4 = ((bf16[8,256,1536]{2,1,0:T(8,128)(2,1)}), bf16[8,256,1536]{2,1,0:T(8,128)(2,1)}, u32[]{:S(2)}, u32[]{:S(2)}) async-start(bf16[8,256,1536]{2,1,0:T(8,128)(2,1)} %bitcast.80), calls=%async_computation.7 | async-start | bytes 12582912 | tf_op jit(solution)/shard_map/all_to_all | solution.py:460
  1313.5 141.4 %all-reduce.2.cloned.1.call-start = ((), (), s32[]{:S(2)}) async-start(), calls=%async_computation.24 | async-start | bytes 131072 | tf_op jit(solution)/shard_map/psum | solution.py:586
  1320.4 8.6 copy-start.8
  1320.4 8.5 copy-start.11
  1320.5 8.5 copy-start.6
  1320.5 8.5 copy-start.7
  1320.5 13.2 copy-start.1
  1328.9 4.8 copy-start
  1333.7 22.3 %copy-start.3 = (f32[2048,256]{1,0:T(8,128)S(1)}, f32[2048,256]{1,0:T(8,128)}, u32[]{:S(2)}) copy-start(f32[2048,256]{1,0:T(8,128)} %refs_4_.9) | copy-start | bytes 6291460
  1333.7 22.3 %copy-start.9 = (f32[2048,256]{1,0:T(8,128)S(1)}, f32[2048,256]{1,0:T(8,128)}, u32[]{:S(2)}) copy-start(f32[2048,256]{1,0:T(8,128)} %refs_5_.5) | copy-start | bytes 6291460
  1377.6 77.3 %copy-start.29 = (f32[4,2,2048]{2,1,0:T(2,128)S(1)}, f32[4,2,2048]{2,1,0:T(2,128)}, u32[]{:S(2)}) copy-start(f32[4,2,2048]{2,1,0:T(2,128)} %param.44) | copy-start | bytes 196612
  1377.6 77.3 %copy-start.30 = (f32[4,2,2048]{2,1,0:T(2,128)S(1)}, f32[4,2,2048]{2,1,0:T(2,128)}, u32[]{:S(2)}) copy-start(f32[4,2,2048]{2,1,0:T(2,128)} %param.39) | copy-start | bytes 196612
  1377.6 79.0 %copy-start.28 = (f32[2,2048]{1,0:T(2,128)S(1)}, f32[2,2048]{1,0:T(2,128)}, u32[]{:S(2)}) copy-start(f32[2,2048]{1,0:T(2,128)} %param.34) | copy-start | bytes 49156
  1377.7 79.0 %copy-start.39 = (f32[2,2048]{1,0:T(2,128)S(1)}, f32[2,2048]{1,0:T(2,128)}, u32[]{:S(2)}) copy-start(f32[2,2048]{1,0:T(2,128)} %param.49) | copy-start | bytes 49156
  1377.7 79.6 %copy-start.4 = (f32[3,256,512]{2,1,0:T(8,128)S(1)}, f32[3,256,512]{2,1,0:T(8,128)}, u32[]{:S(2)}) copy-start(f32[3,256,512]{2,1,0:T(8,128)} %refs_3_.5) | copy-start | bytes 4718596
  1377.7 79.6 %copy-start.10 = (f32[3,256,512]{2,1,0:T(8,128)S(1)}, f32[3,256,512]{2,1,0:T(8,128)}, u32[]{:S(2)}) copy-start(f32[3,256,512]{2,1,0:T(8,128)} %refs_4_.5) | copy-start | bytes 4718596
  (4 other events, 7.5 us)
Sparse Core Ops, SparseCore 0:
  10.2 67.1 all-gather.10
  79.6 29.2 all-gather.12
  111.1 80.9 all-gather.22
  194.0 80.4 all-gather.24
  276.6 134.0 all-gather.14
  444.7 168.4 all-gather.18
  682.6 86.5 reduce-scatter.5
  775.6 87.2 all-gather.20
  868.5 86.0 all-gather.16
  1073.0 108.5 reduce-scatter.7
  1212.4 83.2 reduce-scatter.3
  1320.5 134.3 all-reduce.1

commit v4 on v3

--- a/solution.py
+++ b/solution.py
@@ -345,6 +345,13 @@
         recv_spec = pl.BlockSpec((held, bc, br), lambda m, i: (0, 0, i))
     else:
         recv_spec = pl.BlockSpec((held, br, bc), lambda m, i: (0, i, m))
+    recv_specs = [recv_spec]
+    if len(recv) > 1:
+        place = 2 if turned else base
+        if turned:
+            recv_specs.append(pl.BlockSpec((held, bc, br), lambda m, i: (0, place, i)))
+        else:
+            recv_specs.append(pl.BlockSpec((held, br, bc), lambda m, i: (0, place * blocks + i, 0)))
     one = pl.BlockSpec(lead + (br, bc), lambda m, i: pick(m) + (i, 0))
     many = pl.BlockSpec((GROUPS,) + lead + (br, bc), lambda m, i: (0,) + pick(m) + (i, 0))
     f32 = jnp.float32
@@ -357,7 +364,7 @@
         jax.ShapeDtypeStruct(weight.shape, jnp.bfloat16),
     ]
     operands = [order, *recv, first, second, weight, outer]
-    specs = [pl.BlockSpec(memory_space=pltpu.SMEM)] + [recv_spec] * len(recv) + [many, many, one, one]
+    specs = [pl.BlockSpec(memory_space=pltpu.SMEM)] + recv_specs + [many, many, one, one]
     aliases = {}
     if before is not None:
         aliases = {len(operands) + k: k for k in range(6)}
@@ -397,28 +404,30 @@
     return lax.optimization_barrier((value,) + others)[0]
 
 
-def tick_kernel(source, mark):
-    mark[...] = jnp.zeros_like(mark)
-
-
-def tick(value):
+def tick_kernel(*refs):
+    refs[-1][...] = jnp.zeros_like(refs[-1])
+
+
+def tick(*values):
     return pl.pallas_call(
         tick_kernel,
         out_shape=jax.ShapeDtypeStruct((8, LANES), jnp.float32),
-        in_specs=[pl.BlockSpec(memory_space=pl.ANY)],
+        in_specs=[pl.BlockSpec(memory_space=pl.ANY)] * len(values),
         compiler_params=pltpu.CompilerParams(has_side_effects=True),
-    )(value)
+    )(*values)
 
 
 def gather_rows(part, axis):
     return lax.all_gather(part, axis, axis=0, tiled=True)
 
 
-def spread_rows(part):
-    count = lax.axis_size("tensor")
-    copies = jnp.broadcast_to(part[None], (count,) + part.shape)
+def copies_of(part):
+    return jnp.broadcast_to(part[None], (lax.axis_size("tensor"),) + part.shape)
+
+
+def spread_rows(copies):
     parts = lax.all_to_all(copies, "tensor", split_axis=0, concat_axis=0)
-    return parts.reshape((-1,) + part.shape[1:])
+    return parts.reshape((-1,) + copies.shape[2:])
 
 
 def sum_rows(part):
@@ -490,78 +499,81 @@
     bf16 = jnp.bfloat16
     field_in = tokens.astype(jnp.float32)
     normed_one, scaled_one, factor_one = normed(field_in, norm_gains[0])
-    normed_all = spread_rows(normed_one)
+    normed_all = spread_rows(copies_of(normed_one))
     qkv_full = gather_rows(jnp.concatenate([qkv_weight[m].astype(bf16) for m in range(3)], axis=1), "dp")
     out_full = gather_rows(out_weight.T.astype(bf16), "dp")
     gate_full = gather_rows(gate_weight[0].astype(bf16), "dp")
     up_full = gather_rows(gate_weight[1].astype(bf16), "dp")
     down_full = gather_rows(down_weight.T.astype(bf16), "dp")
-    cotan_all = spread_rows(after(cotangent, normed_all))
 
     other_cotan = to_partner(cotangent)
     lo, hi, info = layout_of(seq_ids, block_ids, TILE, TILE)
     cosine, sine_table = rope_tables(lo)
+    lo_col, hi_col = lo[:, None], hi[:, None]
+    cotan_copies = copies_of(cotangent)
+    cosine, sine_table, lo_col, hi_col, info, cotan_copies = lax.optimization_barrier(
+        (cosine, sine_table, lo_col, hi_col, info, cotan_copies)
+    )
+    mark = tick(cosine, sine_table, lo_col, hi_col, info, cotan_copies)
+    cotan_all = spread_rows(after(cotan_copies, normed_all))
+    normed_all = after(normed_all, mark)
     order = jnp.argsort(groups, stable=True).astype(jnp.int32)
 
     projected = dot(normed_all, qkv_full)
     mixed_all, queries, keys_all, values_all, logsums = attn_fwd(
-        info, projected, cosine, sine_table, lo[:, None], hi[:, None], TILE, TILE
+        info, projected, cosine, sine_table, lo_col, hi_col, TILE, TILE
     )
     attn_rows = sum_rows(dot_cols(mixed_all, out_full).astype(bf16))
     residual = field_in + attn_rows
     normed_two, scaled_two, factor_two = normed(residual, norm_gains[1])
     other_two = to_partner(normed_two)
     normed_two, gate_full, up_full = lax.optimization_barrier((normed_two, gate_full, up_full, tick(normed_two)))[:3]
-    ffn_input = spread_rows(normed_two)
+    ffn_input = spread_rows(copies_of(normed_two))
     other_dy = gather_rows(after(other_cotan, ffn_input), "tensor")
-    other_input = gather_rows(other_two, "tensor")
+    other_input = spread_rows(copies_of(after(other_two, ffn_input)))
 
     gate_pre = dot(ffn_input, gate_full)
-    up_pre = dot(ffn_input, up_full)
+    up_pre = dot(after(ffn_input, tick(gate_pre)), up_full)
     sigmoid_gate = jax.nn.sigmoid(gate_pre)
     swish = gate_pre * sigmoid_gate
     hidden = (swish * up_pre).astype(bf16)
     down_grad = dot_rows(half_cols(cotan_all), hidden).astype(bf16)
     down_recv = to_half(down_grad)
-    cotan_all = after(cotan_all, tick(down_grad))
-    hidden_grad = dot(cotan_all, down_full)
+    hidden_grad = dot(after(cotan_all, down_grad), down_full)
     gate_grad_low = (
         hidden_grad * up_pre * sigmoid_gate * (1.0 + gate_pre * (1.0 - sigmoid_gate))
     ).astype(bf16)
     up_grad_low = (hidden_grad * swish).astype(bf16)
     ffn_back = (dot_cols(gate_grad_low, gate_full) + dot_cols(up_grad_low, up_full)).astype(bf16)
     ffn_back_rows = scatter_rows(ffn_back)
-    input_half = half_cols(after(ffn_input, ffn_back))
+    mark = tick(ffn_back)
+    input_half = half_cols(after(ffn_input, mark))
     gate_grad = dot_rows(input_half, gate_grad_low).astype(bf16)
     gate_recv = to_half(gate_grad)
     up_grad = dot_rows(input_half, up_grad_low).astype(bf16)
     up_recv = to_half(up_grad)
-    hidden = after(hidden, gate_grad, up_grad)
-    ffn_sum = dot_cols(hidden, down_full).astype(bf16)
-    ffn_part = scatter_rows(ffn_sum)
-    layer_out = (residual + ffn_part).astype(bf16)
-
-    other_input = after(other_input, ffn_sum)
+    hidden_own = hidden
+
+    other_input = after(other_input, gate_grad, up_grad)
     gate_pre = dot(other_input, gate_full)
-    up_pre = dot(other_input, up_full)
+    up_pre = dot(after(other_input, tick(gate_pre)), up_full)
     sigmoid_gate = jax.nn.sigmoid(gate_pre)
     swish = gate_pre * sigmoid_gate
     hidden = (swish * up_pre).astype(bf16)
     mark = tick(hidden)
     other_dy = after(other_dy, mark)
+    near = lax.axis_size("dp") // 2
     down_grad = dot_rows(half_cols(other_dy), hidden).astype(bf16)
-    down_recv2 = to_half(down_grad)
     hidden_grad = dot(after(other_dy, down_grad), down_full)
     gate_grad_low = (
         hidden_grad * up_pre * sigmoid_gate * (1.0 + gate_pre * (1.0 - sigmoid_gate))
     ).astype(bf16)
     up_grad_low = (hidden_grad * swish).astype(bf16)
-    input_half = half_cols(other_input)
-    gate_grad = dot_rows(input_half, gate_grad_low).astype(bf16)
-    gate_recv2 = to_half(gate_grad)
-    up_grad = dot_rows(input_half, up_grad_low).astype(bf16)
-    up_recv2 = to_half(up_grad)
-    mark = tick(up_grad)
+    input_half = half_cols(after(other_input, tick(gate_grad_low, up_grad_low)))
+    rest = [dot_rows(input_half, low).astype(bf16) for low in (gate_grad_low, up_grad_low)]
+    rest = jnp.stack([x.reshape(near, -1, x.shape[1]) for x in rest + [down_grad]], axis=1)
+    rest_recv = to_half(rest.reshape(-1, rest.shape[-1]))
+    mark = tick(rest)
 
     cotan_rows = cotangent.astype(jnp.float32)
     resid_grad = cotan_rows + norm_back(ffn_back_rows, scaled_two, factor_two, norm_gains[1])
@@ -569,40 +581,45 @@
     resid_all = gather_rows(resid_grad.astype(bf16), "tensor")
     resid_all = after(resid_all, mark)
     mixed_grad = dot(resid_all, out_full).astype(bf16)
-    out_recv = to_owners(dot_rows(resid_all, mixed_all))
+    out_grad = dot_rows(resid_all, mixed_all).astype(bf16)
+    out_recv = to_owners(out_grad)
+    mixed_grad = after(mixed_grad, out_grad)
     raw_grads = attn_bwd(
         info, queries, keys_all, values_all, mixed_all, mixed_grad, logsums,
         cosine, sine_table, lo[None], hi[None], TILE, TILE,
     )
     raw_all = jnp.concatenate(raw_grads, axis=1)
-    in_grad_rows = scatter_rows(dot_cols(raw_all, qkv_full))
-    qkv_recv = to_owners(dot_rows(normed_all, raw_all))
+    in_grad = dot_cols(raw_all, qkv_full).astype(bf16)
+    in_grad_rows = scatter_rows(in_grad)
+    qkv_grad = dot_rows(after(normed_all, tick(in_grad)), raw_all).astype(bf16)
+    qkv_recv = to_owners(qkv_grad)
+    ffn_part = scatter_rows(dot_cols(after(hidden_own, qkv_grad), down_full))
+    layer_out = (residual + ffn_part).astype(bf16)
     tokens_grad = resid_grad + norm_back(in_grad_rows, scaled_one, factor_one, norm_gains[0])
     gain_one = jnp.sum(in_grad_rows * scaled_one, axis=0)
-    own_group = (jnp.arange(GROUPS, dtype=jnp.int32) == groups[lax.axis_index("dp")]).astype(
-        jnp.float32
-    )
-    gain_slots = own_group[:, None, None] * jnp.stack([gain_one, gain_two])[None]
-    gain_grad = lax.psum(gain_slots, ("dp", "tensor"))
-    order = after(order, gain_slots)
-    near = lax.axis_size("dp") // 2
+    gain_part = jnp.stack([gain_one, gain_two])
+    gain_part = jnp.sum(lax.all_gather(gain_part, "tensor", axis=0), axis=0)
+    gain_all = lax.all_gather(gain_part, "dp", axis=0)
+    picker = groups[None, :] == jnp.arange(GROUPS, dtype=jnp.int32)[:, None]
+    gain_grad = jnp.sum(jnp.where(picker[:, :, None, None], gain_all[None], 0.0), axis=1)
+    order = after(order, gain_all)
     side = order // near != lax.axis_index("dp") // near
     near_order = order % near + near * side.astype(jnp.int32)
 
     down_new = optimize(
-        near_order, (down_recv, down_recv2), down_weight, down_first, down_second, down_outer, 3, turned=True
+        near_order, (down_recv, rest_recv), down_weight, down_first, down_second, down_outer, 3, turned=True
     )
     gate_half = optimize(
-        near_order, (gate_recv, gate_recv2), gate_weight, gate_first, gate_second, gate_outer, 2, member=0
+        near_order, (gate_recv, rest_recv), gate_weight, gate_first, gate_second, gate_outer, 2, member=0
     )
     gate_new = optimize(
-        near_order, (up_recv, up_recv2), gate_weight, gate_first, gate_second, gate_outer, 2, member=1, before=gate_half
+        near_order, (up_recv, rest_recv), gate_weight, gate_first, gate_second, gate_outer, 2, member=1, before=gate_half
     )
     out_new = optimize(
         order, (out_recv,), out_weight, out_first, out_second, out_outer, 1, turned=True
     )
     qkv_new = optimize(
-        order, (after(qkv_recv, gain_grad),), qkv_weight, qkv_first, qkv_second, qkv_outer, 0
+        order, (qkv_recv,), qkv_weight, qkv_first, qkv_second, qkv_outer, 0
     )
     gains_new = update(
         norm_gains, gain_grad, gains_first, gains_second, gains_outer, inner_rates[4], decays[4]

time: 1490 us -> 1650 us (1.11)
  blocking collectives: 140 us -> 284 us
  waiting for transfers between devices: 488 us -> 507 us
    all_to_all x3 -> x4, waiting for transfers between devices: 154 us -> 292 us  [spread_rows(): parts = lax.all_to_all(copies, 'tensor', split_axis=0, concat_axis=0)]
    all_to_all x1, blocking collectives: 52.2 us -> 144 us  [to_owners(): return lax.all_to_all(blocks, 'dp', split_axis=0, concat_axis=0)]
    all_to_all x2 -> x1, waiting for transfers between devices: 81.3 us -> 24.2 us  [to_owners(): return lax.all_to_all(blocks, 'dp', split_axis=0, concat_axis=0)]
    all_to_all x5 -> x4, waiting for transfers between devices: 60.8 us -> 9 us  [to_half(): lax.all_to_all(blocks, 'dp', split_axis=0, concat_axis=0, axis_index_grou...]
    all_gather x0 -> x2, blocking collectives: none -> 51.7 us  [the longest x1 44.7 us: step(): gain_all = lax.all_gather(gain_part, 'dp', axis=0)]
    all_to_all x5 -> x4, starting transfers between devices: 51.3 us -> 22.9 us  [to_half(): lax.all_to_all(blocks, 'dp', split_axis=0, concat_axis=0, axis_index_grou...]
    dot_general x8, matrix products: 127 us -> 110 us  [dot_rows(): lax.dot_general(left, right, (((0,), (0,)), ((), ())), preferred_element_...]
  transfers between devices with their start and end apart: 24 -> 21, of which waited for: 9 -> 8; matrix products, arithmetic and copies ran while one was open for 33% -> 25% of each run, Pallas kernels for 15% -> 13%
where the time goes in v4:
time: 1650 us
  waiting for transfers between devices  507 us (31%)
  matrix products  413 us (25%)
  blocking collectives  284 us (17%)
  Pallas kernels  243 us (15%)
  starting transfers between devices  81.2 us (5%)
  other arithmetic  58.9 us (4%)
  local copies, waits for them, and re-layouts  44.4 us (3%)
    all_to_all x4, waiting for transfers between devices, spread_rows(): parts = lax.all_to_all(copies, 'tensor', split_axis=0, concat_axis=0)  292 us
    dot_general x8, matrix products, dot(): return jnp.dot(left, right, preferred_element_type=jnp.float32)  204 us
    ppermute x2, waiting for transfers between devices, to_partner(): lax.ppermute(part, 'dp', [(i, (i + count // 2) % count) for i in range(co...  181 us
    all_to_all x1, blocking collectives, to_owners(): return lax.all_to_all(blocks, 'dp', split_axis=0, concat_axis=0)  144 us
    dot_general x8, matrix products, dot_rows(): lax.dot_general(left, right, (((0,), (0,)), ((), ())), preferred_element_...  110 us
    dot_general x5, matrix products, dot_cols(): lax.dot_general(left, right, (((1,), (1,)), ((), ())), preferred_element_...  98.2 us
    pallas_call x5, Pallas kernels, optimize(): pl.pallas_call(functools.partial(opt_kernel, sources // GROUPS, turned, l...  88.7 us
    all_to_all x1, blocking collectives, sum_rows(): parts = lax.all_to_all(blocks, 'tensor', split_axis=0, concat_axis=0)  87.5 us
  transfers between devices with their start and end apart: 21, of which 8 were waited for; matrix products, arithmetic and copies ran while one was open for 25% of the time, Pallas kernels for 13%

profile of v4, /device:TPU:1, one launch (start us, length us, event | category | flops | bytes accessed | tf_op | source)
XLA Modules:
  0.0 1645.9 jit_solution(15915948613154563550)
XLA Ops:
  16.8 4.6 broadcast_in_dim.29
  21.4 5.7 all-to-all-start
  32.6 3.7 fusion.33
  36.4 3.0 pad_maximum_fusion.1
  39.4 4.5 broadcast_in_dim.28.refs_5_
  47.1 73.0 %all-to-all-done = bf16[4,512,2048]{2,1,0:T(8,128)(2,1)} async-done(((bf16[4,512,2048]{2,1,0:T(8,128)(2,1)}), bf16[4,512,2048]{2,1,0:T(8,128)(2,1)}, u32[]{:S(2)}, u32[]{:S(2)}) %all-to-all-start) | async-done | bytes 8388640 | tf_op jit(solution)/shard_map/all_to_all | solution.py:429
  120.2 20.1 %fusion.50.q_ref.k_ref.v_ref = f32[2048,1536]{1,0:T(8,128)} fusion(bf16[2048,2048]{1,0:T(8,128)(2,1)} %bitcast.9, bf16[2048,1536]{1,0:T(8,128)(2,1)} %all-gather.14.cloned.1.call-done), kind=kOutput, calls=%fused_computation.116 | convolution fusion | flops 12884901888 | bytes 27262976 | tf_op jit(solution)/shard_map/dot_general | solution.py:392
  140.3 73.6 %attn_fwd.1 = (bf16[2048,512]{1,0:T(8,128)(2,1)}, bf16[2048,512]{1,0:T(8,128)(2,1)}, bf16[2048,512]{1,0:T(8,128)(2,1)}, bf16[2048,512]{1,0:T(8,128)(2,1)}, f32[4,2,2048]{2,1,0:T(2,128)S(1)}) custom-call(s32[6,4]{1,0:T(8,128)S(1)} %copy-done.21, f32[2048,1536]{1,0:T(8,128)} %fusion.50.q_ref.k_ref.v_ref, f32[2048,1536]{1,0:T(8,128)} %fusion.50.q_ref.k_ref.v_ref, ...), custom_call_target="tpu_custom_call" | custom-call | flops 5153960960 | bytes 12582912 | tf_op jit(solution)/shard_map/attn_fwd/pallas_call | solution.py:106
  213.8 6.7 convolution_convert_fusion.2
  220.6 87.5 %all_to_all.55 = bf16[4,512,2048]{2,1,0:T(8,128)(2,1)S(1)} all-to-all(bf16[4,512,2048]{2,1,0:T(8,128)(2,1)S(1)} %bitcast.84), channel_id=1, replica_groups=mesh['dp'=8,'tensor'=4] {'tensor'}, dimensions={0} | all-to-all | bytes 16777216 | tf_op jit(solution)/shard_map/all_to_all | solution.py:436
  308.1 3.9 convert_reduce_fusion
  312.0 2.8 multiply_reduce_fusion
  319.2 6.1 broadcast_in_dim.30
  325.3 5.6 all-to-all-start.2
  333.7 89.1 %all-to-all-done.2 = bf16[4,512,2048]{2,1,0:T(8,128)(2,1)} async-done(((bf16[4,512,2048]{2,1,0:T(8,128)(2,1)}), bf16[4,512,2048]{2,1,0:T(8,128)(2,1)}, u32[]{:S(2)}, u32[]{:S(2)}) %all-to-all-start.2) | async-done | bytes 8388640 | tf_op jit(solution)/shard_map/all_to_all | solution.py:429
  422.8 5.6 all-to-all-start.3
  428.4 24.4 %fusion.51.refs_0_ = f32[2048,2048]{1,0:T(8,128)} fusion(bf16[2048,2048]{1,0:T(8,128)(2,1)} %bitcast.18, bf16[2048,2048]{1,0:T(8,128)(2,1)} %bitcast.109), kind=kOutput, calls=%fused_computation.117 | convolution fusion | flops 17179869184 | bytes 33554432 | tf_op jit(solution)/shard_map/dot_general | solution.py:392
  453.4 28.1 %multiply_convert_fusion.5 = (bf16[2048,2048]{1,0:T(8,128)(2,1)}, f32[2048,2048]{1,0:T(8,128)}) fusion(f32[2048,2048]{1,0:T(8,128)} %fusion.51.refs_0_, bf16[2048,2048]{1,0:T(8,128)(2,1)} %bitcast.18, bf16[2048,2048]{1,0:T(8,128)(2,1)} %bitcast.112), kind=kOutput, calls=%fused_computation.8 | convolution fusion | flops 17205035008 | bytes 58720256 | tf_op jit(solution)/shard_map/dot_general | solution.py:392
  481.5 38.8 %all-to-all-done.3 = bf16[4,512,2048]{2,1,0:T(8,128)(2,1)} async-done(((bf16[4,512,2048]{2,1,0:T(8,128)(2,1)}), bf16[4,512,2048]{2,1,0:T(8,128)(2,1)}, u32[]{:S(2)}, u32[]{:S(2)}) %all-to-all-start.3) | async-done | bytes 8388640 | tf_op jit(solution)/shard_map/all_to_all | solution.py:429
  520.3 14.2 fusion.23
  534.4 34.4 %multiply_convert_fusion.3 = (bf16[2048,2048]{1,0:T(8,128)(2,1)}, bf16[2048,2048]{1,0:T(8,128)(2,1)}) fusion(f32[2048,2048]{1,0:T(8,128)} %fusion.51.refs_0_, f32[2048,2048]{1,0:T(8,128)} %get-tuple-element.196, bf16[2048,2048]{1,0:T(8,128)(2,1)} %bitcast.19, bf16[2048,2048]{0,1:T(8,128)(2,1)} %all-gather.18.cloned.1.call-done), kind=kOutput, calls=%fused_computation.6 | convolution fusion | flops 17234395136 | bytes 67108864 | tf_op jit(solution)/shard_map/dot_general | solution.py:392
  568.8 24.7 %fusion.52 = f32[2048,2048]{1,0:T(8,128)} fusion(bf16[2048,2048]{1,0:T(8,128)(2,1)} %get-tuple-element.182, bf16[2048,2048]{1,0:T(8,128)(2,1)} %bitcast.110), kind=kOutput, calls=%fused_computation.118 | convolution fusion | flops 17179869184 | bytes 33554432 | tf_op jit(solution)/shard_map/dot_general | solution.py:396
  593.6 25.5 %add_convert_fusion.refs_0_ = bf16[2048,2048]{1,0:T(8,128)(2,1)} fusion(f32[2048,2048]{1,0:T(8,128)} %fusion.52, bf16[2048,2048]{1,0:T(8,128)(2,1)} %get-tuple-element.181, bf16[2048,2048]{1,0:T(8,128)(2,1)} %bitcast.113), kind=kOutput, calls=%fused_computation.5 | convolution fusion | flops 17188257792 | bytes 41943040 | tf_op jit(solution)/shard_map/dot_general | solution.py:396
  619.1 15.3 collective-permute-start.1
  634.4 135.9 %collective-permute-done.1 = bf16[512,2048]{1,0:T(8,128)(2,1)} collective-permute-done((bf16[512,2048]{1,0:T(8,128)(2,1)}, bf16[512,2048]{1,0:T(8,128)(2,1)}, u32[]{:S(2)}, u32[]{:S(2)}) %collective-permute-start.1) | collective-permute-done | bytes 2097184 | tf_op jit(solution)/shard_map/ppermute | solution.py:457
  770.4 44.9 %collective-permute-done = bf16[512,2048]{1,0:T(8,128)(2,1)} collective-permute-done((bf16[512,2048]{1,0:T(8,128)(2,1)}, bf16[512,2048]{1,0:T(8,128)(2,1)}, u32[]{:S(2)}, u32[]{:S(2)}) %collective-permute-start) | collective-permute-done | bytes 2097184 | tf_op jit(solution)/shard_map/ppermute | solution.py:457
  815.3 6.1 broadcast_in_dim.31
  821.4 5.8 all-to-all-start.4
  827.8 14.0 convolution_convert_fusion.7
  841.8 14.0 convolution_convert_fusion.6
  855.8 91.4 %all-to-all-done.4 = bf16[4,512,2048]{2,1,0:T(8,128)(2,1)} async-done(((bf16[4,512,2048]{2,1,0:T(8,128)(2,1)}), bf16[4,512,2048]{2,1,0:T(8,128)(2,1)}, u32[]{:S(2)}, u32[]{:S(2)}) %all-to-all-start.4) | async-done | bytes 8388640 | tf_op jit(solution)/shard_map/all_to_all | solution.py:429
  947.2 5.6 all-to-all-start.9
  952.8 24.4 %fusion.53.refs_0_ = f32[2048,2048]{1,0:T(8,128)} fusion(bf16[2048,2048]{1,0:T(8,128)(2,1)} %bitcast.21, bf16[2048,2048]{1,0:T(8,128)(2,1)} %bitcast.111), kind=kOutput, calls=%fused_computation.119 | convolution fusion | flops 17179869184 | bytes 33554432 | tf_op jit(solution)/shard_map/dot_general | solution.py:392
  977.9 4.7 fusion.14
  983.2 5.0 fusion.43
  988.3 28.1 %multiply_convert_fusion.2 = (bf16[2048,2048]{1,0:T(8,128)(2,1)}, f32[2048,2048]{1,0:T(8,128)}) fusion(f32[2048,2048]{1,0:T(8,128)} %fusion.53.refs_0_, bf16[2048,2048]{1,0:T(8,128)(2,1)} %bitcast.21, bf16[2048,2048]{1,0:T(8,128)(2,1)} %bitcast.114), kind=kOutput, calls=%fused_computation.2 | convolution fusion | flops 17205035008 | bytes 58720256 | tf_op jit(solution)/shard_map/dot_general | solution.py:392
  1016.9 14.4 fusion.26
  1031.4 5.0 all-to-all-start.10
  1036.3 34.9 %multiply_convert_fusion.1 = (bf16[2048,2048]{1,0:T(8,128)(2,1)}, bf16[2048,2048]{1,0:T(8,128)(2,1)}) fusion(f32[2048,2048]{1,0:T(8,128)} %fusion.53.refs_0_, f32[2048,2048]{1,0:T(8,128)} %get-tuple-element.198, bf16[2048,2048]{1,0:T(8,128)(2,1)} %all-gather.22.cloned.1.call-done, bf16[2048,2048]{0,1:T(8,128)(2,1)} %all-gather.18.cloned.1.call-done), kind=kOutput, calls=%fused_computation.1 | convolution fusion | flops 17234395136 | bytes 67108864 | tf_op jit(solution)/shard_map/dot_general | solution.py:392
  1071.8 12.8 convolution_convert_fusion.4
  1084.7 11.5 convolution_convert_fusion.5
  1096.2 5.5 pad_maximum_fusion.refs_0_
  1102.3 9.9 convolution_convert_fusion.8
  1112.1 6.3 all-to-all-start.8
  1118.5 9.9 convolution_convert_fusion.9.do_ref
  1128.4 75.7 %attn_bwd.1 = (bf16[2048,512]{1,0:T(8,128)(2,1)S(1)}, bf16[2048,512]{1,0:T(8,128)(2,1)}, bf16[2048,512]{1,0:T(8,128)(2,1)}) custom-call(s32[6,4]{1,0:T(8,128)S(1)} %copy-done.21, bf16[2048,512]{1,0:T(8,128)(2,1)} %get-tuple-element.109.q_ref, bf16[2048,512]{1,0:T(8,128)(2,1)} %get-tuple-element.110.k_ref, bf16[2048,512]{1,0:T(8,128)(2,1)} %get-tuple-element.111.v_ref, ...), custom_call_target="tpu_custom_call" | custom-call | flops 12884901888 | bytes 16777216 | tf_op jit(solution)/shard_map/attn_bwd/pallas_call | solution.py:202
  1209.2 17.4 %convolution_convert_fusion.1.refs_0_ = bf16[2048,2048]{1,0:T(8,128)(2,1)} fusion(bf16[2048,1536]{1,0:T(8,128)(2,1)S(1)} %constant_dynamic-update-slice_fusion, bf16[2048,1536]{1,0:T(8,128)(2,1)} %all-gather.14.cloned.1.call-done), kind=kOutput, calls=%fused_computation.16 | convolution fusion | flops 12889096192 | bytes 20971520 | tf_op jit(solution)/shard_map/dot_general | solution.py:396
  1227.2 19.5 %convolution_convert_fusion.3 = bf16[2048,1536]{1,0:T(8,128)(2,1)} fusion(bf16[2048,2048]{1,0:T(8,128)(2,1)} %bitcast.9, bf16[2048,1536]{1,0:T(8,128)(2,1)} %copy-done.31), kind=kOutput, calls=%fused_computation.18 | convolution fusion | flops 12888047616 | bytes 20971520 | tf_op jit(solution)/shard_map/dot_general | solution.py:400
  1246.7 9.0 all-to-all-done.8.refs_1_
  1255.7 19.6 %all-to-all-start.6 = ((bf16[8,256,512]{2,1,0:T(8,128)(2,1)}), bf16[8,256,512]{2,1,0:T(8,128)(2,1)S(1)}, u32[]{:S(2)}, u32[]{:S(2)}) async-start(bf16[8,256,512]{2,1,0:T(8,128)(2,1)} %bitcast.92), calls=%async_computation.9 | async-start | bytes 4194304 | tf_op jit(solution)/shard_map/all_to_all | solution.py:469
  1275.3 23.9 %convolution_convert_fusion = bf16[2048,2048]{1,0:T(8,128)(2,1)} fusion(bf16[2048,2048]{1,0:T(8,128)(2,1)} %get-tuple-element.129, bf16[2048,2048]{0,1:T(8,128)(2,1)} %all-gather.18.cloned.1.call-done), kind=kOutput, calls=%fused_computation.15 | convolution fusion | flops 17184063488 | bytes 25165824 | tf_op jit(solution)/shard_map/dot_general | solution.py:396
  1299.2 24.2 %all-to-all-done.6.refs_0_ = bf16[8,256,512]{2,1,0:T(8,128)(2,1)S(1)} async-done(((bf16[8,256,512]{2,1,0:T(8,128)(2,1)}), bf16[8,256,512]{2,1,0:T(8,128)(2,1)S(1)}, u32[]{:S(2)}, u32[]{:S(2)}) %all-to-all-start.6) | async-done | bytes 2097184 | tf_op jit(solution)/shard_map/all_to_all | solution.py:469
  1323.4 144.3 %all_to_all.56.refs_0_ = bf16[8,256,1536]{2,1,0:T(8,128)(2,1)} all-to-all(bf16[8,256,1536]{2,1,0:T(8,128)(2,1)} %bitcast.85), channel_id=1, replica_groups=mesh['dp'=8,'tensor'=4] {'dp'}, dimensions={0} | all-to-all | bytes 12582912 | tf_op jit(solution)/shard_map/all_to_all | solution.py:469
  1467.7 6.0 all-to-all-start.7
  1474.7 3.6 fusion.17
  1478.3 7.0 all-gather.4
  1485.4 44.7 %all-gather.5 = f32[8,2,2048]{2,1,0:T(2,128)S(1)} all-gather(f32[1,2,2048]{2,1,0:T(2,128)S(1)} %bitcast.100), channel_id=5, replica_groups=mesh['dp'=8,'tensor'=4] {'dp'}, dimensions={0}, use_global_device_ids=true | all-gather | bytes 147456 | tf_op jit(solution)/shard_map/all_gather | solution.py:602
  1533.3 4.9 optimize.6
  1538.2 2.8 copy-done.2
  1541.0 16.0 optimize.5
  1557.0 23.2 %optimize.7 = (f32[4,2,256,2048]{3,2,1,0:T(8,128)}, f32[4,2,256,2048]{3,2,1,0:T(8,128)}, f32[2,256,2048]{2,1,0:T(8,128)}, f32[2,256,2048]{2,1,0:T(8,128)}, f32[2...) custom-call(s32[8]{0:T(128)S(1)} %fusion.42.order, bf16[4,256,2048]{2,1,0:T(8,128)(2,1)} %all-to-all-done.9.refs_0_, ...), custom_call_target="tpu_custom_call" | custom-call | flops 31457280 | bytes 53477376 | tf_op jit(solution)/shard_map/optimize/pallas_call | solution.py:374
  1580.2 21.7 %optimize.9 = (f32[4,2048,256]{2,1,0:T(8,128)}, f32[4,2048,256]{2,1,0:T(8,128)}, f32[2048,256]{1,0:T(8,128)}, f32[2048,256]{1,0:T(8,128)}, f32[2048,256]{1,0:T(8,128)}, /*index=5*/bf16[2048,256]{1,0:T(8,128)(2,1)}) custom-call(s32[8]{0:T(128)S(1)} %fusion.42.order, bf16[4,256,2048]{2,1,0:T(8,128)(2,1)} %all-to-all-done.10.refs_0_, ...), custom_call_target="tpu_custom_call" | custom-call | flops 31457280 | bytes 53477376 | tf_op jit(solution)/shard_map/optimize/pallas_call | solution.py:374
  1603.8 7.7 fusion.10
  1615.8 23.0 %optimize.8 = (f32[4,2,256,2048]{3,2,1,0:T(8,128)}, f32[4,2,256,2048]{3,2,1,0:T(8,128)}, f32[2,256,2048]{2,1,0:T(8,128)}, f32[2,256,2048]{2,1,0:T(8,128)}, f32[2...) custom-call(s32[8]{0:T(128)S(1)} %fusion.42.order, ...), custom_call_target="tpu_custom_call", output_to_operand_aliasing={{0}: (7, {}), {1}: (8, {}), {2}: (9, {}), {3}: (10, {}), {4... | custom-call | flops 31457280 | bytes 53477376 | tf_op jit(solution)/shard_map/optimize/pallas_call | solution.py:374
  (191 shorter events, 45.9 us)
Async XLA Ops:
  7.2 113.0 %all-gather.14.cloned.1.call-start = ((), (), s32[]{:S(2)}) async-start(), calls=%async_computation.14 | async-start | bytes 7077888 | tf_op jit(solution)/shard_map/all_gather | solution.py:421
  8.8 6.9 copy-start.24
  8.8 7.4 copy-start.37
  9.8 204.0 %all-gather.16.cloned.1.call-start = ((), (), s32[]{:S(2)}) async-start(), calls=%async_computation.15 | async-start | bytes 2359296 | tf_op jit(solution)/shard_map/all_gather | solution.py:421
  11.7 307.5 %all-gather.24.cloned.1.call-start = ((), (), s32[]{:S(2)}) async-start(), calls=%async_computation.22 | async-start | bytes 9437184 | tf_op jit(solution)/shard_map/all_gather | solution.py:421
  16.2 5.2 copy-start.44
  16.2 5.1 copy-start.35
  16.2 298.6 %copy-start.32 = (f32[1,2048]{1,0:T(1,128)}, f32[1,2048]{1,0:T(1,128)S(1)}, u32[]{:S(2)}) copy-start(f32[1,2048]{1,0:T(1,128)S(1)} %get-tuple-element.190) | copy-start | bytes 24580
  21.4 6.4 copy-start.50
  21.4 6.4 copy-start.51
  21.4 98.7 %all-to-all-start = ((bf16[4,512,2048]{2,1,0:T(8,128)(2,1)}), bf16[4,512,2048]{2,1,0:T(8,128)(2,1)}, u32[]{:S(2)}, u32[]{:S(2)}) async-start(bf16[4,512,2048]{2,1,0:T(8,128)(2,1)} %broadcast_in_dim.29), calls=%async_computation | async-start | bytes 16777216 | tf_op jit(solution)/shard_map/all_to_all | solution.py:429
  27.1 12.2 copy-start.27
  27.1 292.0 %all-gather.26.cloned.1.call-start = ((), (), s32[]{:S(2)}) async-start(), calls=%async_computation.23 | async-start | bytes 9437184 | tf_op jit(solution)/shard_map/all_gather | solution.py:421
  29.6 15.6 copy-start.19
  31.4 12.5 copy-start.17
  120.1 20.1 %copy-start.5 = (f32[2048,128]{1,0:T(8,128)S(1)}, f32[2048,128]{1,0:T(8,128)}, u32[]{:S(2)}) copy-start(f32[2048,128]{1,0:T(8,128)} %get-tuple-element.98.refs_0_.cos_ref) | copy-start | bytes 3145732
  120.1 20.1 %copy-start.6 = (f32[2048,128]{1,0:T(8,128)S(1)}, f32[2048,128]{1,0:T(8,128)}, u32[]{:S(2)}) copy-start(f32[2048,128]{1,0:T(8,128)} %get-tuple-element.99.refs_1_.sin_ref) | copy-start | bytes 3145732
  120.1 20.1 %copy-start.7 = (s32[2048,1]{1,0:T(8,128)S(1)}, s32[2048,1]{1,0:T(8,128)}, u32[]{:S(2)}) copy-start(s32[2048,1]{1,0:T(8,128)} %copy.77.refs_2_.lo_ref) | copy-start | bytes 24580
  120.1 20.1 %copy-start.21 = (s32[6,4]{1,0:T(8,128)S(1)}, s32[6,4]{1,0:T(8,128)}, u32[]{:S(2)}) copy-start(s32[6,4]{1,0:T(8,128)} %stack.39.refs_4_.info) | copy-start | bytes 292
  120.2 20.1 %copy-start.8 = (s32[2048,1]{1,0:T(8,128)S(1)}, s32[2048,1]{1,0:T(8,128)}, u32[]{:S(2)}) copy-start(s32[2048,1]{1,0:T(8,128)} %copy.78.refs_3_.hi_ref) | copy-start | bytes 24580
  308.1 3.9 copy-start.25
  314.8 10.4 copy-start.41
  325.3 97.5 %all-to-all-start.2 = ((bf16[4,512,2048]{2,1,0:T(8,128)(2,1)}), bf16[4,512,2048]{2,1,0:T(8,128)(2,1)}, u32[]{:S(2)}, u32[]{:S(2)}) async-start(bf16[4,512,2048]{2,1,0:T(8,128)(2,1)} %broadcast_in_dim.30), calls=%async_computation.2 | async-start | bytes 16777216 | tf_op jit(solution)/shard_map/all_to_all | solution.py:429
  330.9 203.5 %all-gather.18.cloned.1.call-start = ((), (), s32[]{:S(2)}) async-start(), calls=%async_computation.16 | async-start | bytes 9437184 | tf_op jit(solution)/shard_map/all_gather | solution.py:421
  422.8 97.5 %all-to-all-start.3 = ((bf16[4,512,2048]{2,1,0:T(8,128)(2,1)}), bf16[4,512,2048]{2,1,0:T(8,128)(2,1)}, u32[]{:S(2)}, u32[]{:S(2)}) async-start(bf16[4,512,2048]{2,1,0:T(8,128)(2,1)} %broadcast_in_dim.28.refs_5_), calls=%async_computation.3 | async-start | bytes 16777216 | tf_op jit(solution)/shard_map/all_to_all | solution.py:429
  428.4 549.4 %reduce-scatter.4.cloned.1.call-start = ((), (), s32[]{:S(2)}) async-start(), calls=%async_computation.17 | async-start | bytes 10485760 | tf_op jit(solution)/shard_map/reduce_scatter | solution.py:441
  619.1 397.9 %all-gather.22.cloned.1.call-start = ((), (), s32[]{:S(2)}) async-start(), calls=%async_computation.19 | async-start | bytes 10485760 | tf_op jit(solution)/shard_map/all_gather | solution.py:421
  619.1 151.3 %collective-permute-start.1 = (bf16[512,2048]{1,0:T(8,128)(2,1)}, bf16[512,2048]{1,0:T(8,128)(2,1)}, u32[]{:S(2)}, u32[]{:S(2)}) collective-permute-start(bf16[512,2048]{1,0:T(8,128)(2,1)} %param.26), channel_id=1, source_target_pairs={{0,16},{4,20},{8,24},{12,28},{16,0},{20,4},{24,8},{28,12},{1,17},{... | collective-permute-start | bytes 6291464 | tf_op jit(solution)/shard_map/ppermute | solution.py:457
  634.4 180.9 %collective-permute-start = (bf16[512,2048]{1,0:T(8,128)(2,1)}, bf16[512,2048]{1,0:T(8,128)(2,1)}, u32[]{:S(2)}, u32[]{:S(2)}) collective-permute-start(bf16[512,2048]{1,0:T(8,128)(2,1)} %multiply_convert_fusion.6.refs_0_), channel_id=1, source_target_pairs={{0,16},{4,20},{8,24},{12,28},{16,0},{20,4},{24,8},{28,12},{1,17},{... | collective-permute-start | bytes 6291464 | tf_op jit(solution)/shard_map/ppermute | solution.py:457
  821.4 125.9 %all-to-all-start.4 = ((bf16[4,512,2048]{2,1,0:T(8,128)(2,1)}), bf16[4,512,2048]{2,1,0:T(8,128)(2,1)}, u32[]{:S(2)}, u32[]{:S(2)}) async-start(bf16[4,512,2048]{2,1,0:T(8,128)(2,1)} %broadcast_in_dim.31), calls=%async_computation.5 | async-start | bytes 16777216 | tf_op jit(solution)/shard_map/all_to_all | solution.py:429
  947.2 84.1 %all-to-all-start.9 = ((bf16[4,256,2048]{2,1,0:T(8,128)(2,1)}), bf16[4,256,2048]{2,1,0:T(8,128)(2,1)}, u32[]{:S(2)}, u32[]{:S(2)}) async-start(bf16[4,256,2048]{2,1,0:T(8,128)(2,1)} %bitcast.88), calls=%async_computation.12 | async-start | bytes 8388608 | tf_op jit(solution)/shard_map/all_to_all | solution.py:452
  952.8 149.5 %all-gather.20.cloned.1.call-start = ((), (), s32[]{:S(2)}) async-start(), calls=%async_computation.18 | async-start | bytes 10485760 | tf_op jit(solution)/shard_map/all_gather | solution.py:421
  977.9 5.3 copy-start.23
  1031.4 80.7 %all-to-all-start.10 = ((bf16[4,256,2048]{2,1,0:T(8,128)(2,1)}), bf16[4,256,2048]{2,1,0:T(8,128)(2,1)}, u32[]{:S(2)}, u32[]{:S(2)}) async-start(bf16[4,256,2048]{2,1,0:T(8,128)(2,1)} %bitcast.87), calls=%async_computation.13 | async-start | bytes 8388608 | tf_op jit(solution)/shard_map/all_to_all | solution.py:452
  1071.8 12.8 copy-start.28
  1084.7 11.5 copy-start.29
  1112.1 143.6 %all-to-all-start.8 = ((bf16[4,768,2048]{2,1,0:T(8,128)(2,1)}), bf16[4,768,2048]{2,1,0:T(8,128)(2,1)}, u32[]{:S(2)}, u32[]{:S(2)}) async-start(bf16[4,768,2048]{2,1,0:T(8,128)(2,1)} %bitcast.83), calls=%async_computation.11 | async-start | bytes 25165824 | tf_op jit(solution)/shard_map/all_to_all | solution.py:452
  1118.5 9.9 copy-start.18
  1118.5 9.9 copy-start.20
  1118.5 356.2 %reduce-scatter.8.cloned.1.call-start = ((), (), s32[]{:S(2)}) async-start(), calls=%async_computation.21 | async-start | bytes 10485760 | tf_op jit(solution)/shard_map/reduce_scatter | solution.py:441
  1255.7 67.7 %all-to-all-start.6 = ((bf16[8,256,512]{2,1,0:T(8,128)(2,1)}), bf16[8,256,512]{2,1,0:T(8,128)(2,1)S(1)}, u32[]{:S(2)}, u32[]{:S(2)}) async-start(bf16[8,256,512]{2,1,0:T(8,128)(2,1)} %bitcast.92), calls=%async_computation.9 | async-start | bytes 4194304 | tf_op jit(solution)/shard_map/all_to_all | solution.py:469
  1275.3 328.4 %reduce-scatter.6.cloned.1.call-start = ((), (), s32[]{:S(2)}) async-start(), calls=%async_computation.20 | async-start | bytes 10485760 | tf_op jit(solution)/shard_map/reduce_scatter | solution.py:441
  1323.4 150.4 %copy-start.52 = (s32[8]{0:T(128)S(1)}, s32[8]{0:T(128)}, u32[]{:S(2)}) copy-start(s32[8]{0:T(128)} %param.29) | copy-start | bytes 100
  1323.4 151.3 %copy-start.36 = (f32[1,2048]{1,0:T(1,128)S(1)}, f32[1,2048]{1,0:T(1,128)}, u32[]{:S(2)}) copy-start(f32[1,2048]{1,0:T(1,128)} %copy-done.35) | copy-start | bytes 24580
  1323.4 151.3 %copy-start.45 = (f32[512]{0:T(512)S(1)}, f32[512]{0:T(512)}, u32[]{:S(2)}) copy-start(f32[512]{0:T(512)} %copy-done.44) | copy-start | bytes 6148
  1467.7 10.6 copy-start.46
  1467.7 62.4 %copy-start.14 = (f32[512,256]{1,0:T(8,128)S(1)}, f32[512,256]{1,0:T(8,128)}, u32[]{:S(2)}) copy-start(f32[512,256]{1,0:T(8,128)} %refs_3_.6) | copy-start | bytes 1572868
  1467.7 62.4 %copy-start.16 = (f32[512,256]{1,0:T(8,128)S(1)}, f32[512,256]{1,0:T(8,128)}, u32[]{:S(2)}) copy-start(f32[512,256]{1,0:T(8,128)} %refs_4_.6) | copy-start | bytes 1572868
  1467.7 143.7 %all-to-all-start.7 = ((bf16[4,256,2048]{2,1,0:T(8,128)(2,1)}), bf16[4,256,2048]{2,1,0:T(8,128)(2,1)}, u32[]{:S(2)}, u32[]{:S(2)}) async-start(bf16[4,256,2048]{2,1,0:T(8,128)(2,1)} %bitcast.86), calls=%async_computation.10 | async-start | bytes 8388608 | tf_op jit(solution)/shard_map/all_to_all | solution.py:452
  1485.3 52.8 %copy-start.10 = (f32[3,256,512]{2,1,0:T(8,128)S(1)}, f32[3,256,512]{2,1,0:T(8,128)}, u32[]{:S(2)}) copy-start(f32[3,256,512]{2,1,0:T(8,128)} %refs_3_.5) | copy-start | bytes 4718596
  1533.3 4.9 copy-start.15
  1538.2 2.8 copy-start.2
  1541.0 16.0 copy-start
  1541.0 16.0 copy-start.3
  1557.0 23.2 %copy-start.9 = (f32[2048,256]{1,0:T(8,128)S(1)}, f32[2048,256]{1,0:T(8,128)}, u32[]{:S(2)}) copy-start(f32[2048,256]{1,0:T(8,128)} %refs_4_.9) | copy-start | bytes 6291460
  1557.0 23.2 %copy-start.11 = (f32[2048,256]{1,0:T(8,128)S(1)}, f32[2048,256]{1,0:T(8,128)}, u32[]{:S(2)}) copy-start(f32[2048,256]{1,0:T(8,128)} %refs_5_.5) | copy-start | bytes 6291460
  1580.1 22.1 %copy-start.39 = (f32[4,2,2048]{2,1,0:T(2,128)S(1)}, f32[4,2,2048]{2,1,0:T(2,128)}, u32[]{:S(2)}) copy-start(f32[4,2,2048]{2,1,0:T(2,128)} %param.44) | copy-start | bytes 196612
  1580.2 22.1 %copy-start.40 = (f32[4,2,2048]{2,1,0:T(2,128)S(1)}, f32[4,2,2048]{2,1,0:T(2,128)}, u32[]{:S(2)}) copy-start(f32[4,2,2048]{2,1,0:T(2,128)} %param.39) | copy-start | bytes 196612
  1580.2 22.9 %copy-start.38 = (f32[2,2048]{1,0:T(2,128)S(1)}, f32[2,2048]{1,0:T(2,128)}, u32[]{:S(2)}) copy-start(f32[2,2048]{1,0:T(2,128)} %param.34) | copy-start | bytes 49156
  1580.2 22.9 %copy-start.49 = (f32[2,2048]{1,0:T(2,128)S(1)}, f32[2,2048]{1,0:T(2,128)}, u32[]{:S(2)}) copy-start(f32[2,2048]{1,0:T(2,128)} %param.49) | copy-start | bytes 49156
  1580.2 23.5 %copy-start.26 = (bf16[512,2048]{1,0:T(8,128)(2,1)S(1)}, bf16[512,2048]{1,0:T(8,128)(2,1)}, u32[]{:S(2)}) copy-start(bf16[512,2048]{1,0:T(8,128)(2,1)} %param.25) | copy-start | bytes 6291460
  1580.2 23.5 %copy-start.34 = (f32[1,2048]{1,0:T(1,128)S(1)}, f32[1,2048]{1,0:T(1,128)}, u32[]{:S(2)}) copy-start(f32[1,2048]{1,0:T(1,128)} %copy-done.32) | copy-start | bytes 24580
  1580.2 23.5 %copy-start.43 = (f32[512]{0:T(512)S(1)}, f32[512]{0:T(512)}, u32[]{:S(2)}) copy-start(f32[512]{0:T(512)} %copy-done.41) | copy-start | bytes 6148
  1580.2 23.5 %copy-start.48 = (f32[512]{0:T(512)S(1)}, f32[512]{0:T(512)}, u32[]{:S(2)}) copy-start(f32[512]{0:T(512)} %copy-done.47) | copy-start | bytes 6148
  (10 other events, 16.5 us)
Sparse Core Ops, SparseCore 0:
  10.2 67.1 all-gather.13
  79.6 29.2 all-gather.15
  111.1 80.8 all-gather.23
  194.0 80.5 all-gather.25
  333.8 98.7 all-gather.17
  619.2 99.3 reduce-scatter.3
  770.5 158.5 all-gather.21
  988.4 87.1 all-gather.19
  1226.8 109.6 reduce-scatter.7
  1339.3 86.3 reduce-scatter.5

commit v5 on v4

--- a/solution.py
+++ b/solution.py
@@ -239,6 +239,7 @@
     return jnp.concatenate([cos] * 4, axis=1), jnp.concatenate([-sin, sin, -sin, sin], axis=1)
 
 
+DP, TP = "dp", "tensor"
 GROUPS = 4
 STEP = 4
 
@@ -347,11 +348,10 @@
         recv_spec = pl.BlockSpec((held, br, bc), lambda m, i: (0, i, m))
     recv_specs = [recv_spec]
     if len(recv) > 1:
-        place = 2 if turned else base
         if turned:
-            recv_specs.append(pl.BlockSpec((held, bc, br), lambda m, i: (0, place, i)))
+            recv_specs.append(recv_spec)
         else:
-            recv_specs.append(pl.BlockSpec((held, br, bc), lambda m, i: (0, place * blocks + i, 0)))
+            recv_specs.append(pl.BlockSpec((held, br, bc), lambda m, i: (0, base * blocks + i, 0)))
     one = pl.BlockSpec(lead + (br, bc), lambda m, i: pick(m) + (i, 0))
     many = pl.BlockSpec((GROUPS,) + lead + (br, bc), lambda m, i: (0,) + pick(m) + (i, 0))
     f32 = jnp.float32
@@ -422,51 +422,51 @@
 
 
 def copies_of(part):
-    return jnp.broadcast_to(part[None], (lax.axis_size("tensor"),) + part.shape)
+    return jnp.broadcast_to(part[None], (lax.axis_size(TP),) + part.shape)
 
 
 def spread_rows(copies):
-    parts = lax.all_to_all(copies, "tensor", split_axis=0, concat_axis=0)
+    parts = lax.all_to_all(copies, TP, split_axis=0, concat_axis=0)
     return parts.reshape((-1,) + copies.shape[2:])
 
 
 def sum_rows(part):
-    count = lax.axis_size("tensor")
+    count = lax.axis_size(TP)
     blocks = part.reshape((count, part.shape[0] // count) + part.shape[1:])
-    parts = lax.all_to_all(blocks, "tensor", split_axis=0, concat_axis=0)
+    parts = lax.all_to_all(blocks, TP, split_axis=0, concat_axis=0)
     return jnp.sum(parts.astype(jnp.float32), axis=0)
 
 
 def scatter_rows(part):
     summed = lax.psum_scatter(
-        part.astype(jnp.bfloat16), "tensor", scatter_dimension=0, tiled=True
+        part.astype(jnp.bfloat16), TP, scatter_dimension=0, tiled=True
     )
     return summed.astype(jnp.float32)
 
 
 def to_half(grad):
-    count = lax.axis_size("dp")
+    count = lax.axis_size(DP)
     near = count // 2
     blocks = grad.astype(jnp.bfloat16).reshape((near, grad.shape[0] // near) + grad.shape[1:])
     halves = [list(range(near)), list(range(near, count))]
-    return lax.all_to_all(blocks, "dp", split_axis=0, concat_axis=0, axis_index_groups=halves)
+    return lax.all_to_all(blocks, DP, split_axis=0, concat_axis=0, axis_index_groups=halves)
 
 
 def to_partner(part):
-    count = lax.axis_size("dp")
-    return lax.ppermute(part, "dp", [(i, (i + count // 2) % count) for i in range(count)])
+    count = lax.axis_size(DP)
+    return lax.ppermute(part, DP, [(i, (i + count // 2) % count) for i in range(count)])
 
 
 def half_cols(rows):
-    near = lax.axis_size("dp") // 2
+    near = lax.axis_size(DP) // 2
     wide = rows.shape[1] // 2
-    return lax.dynamic_slice_in_dim(rows, lax.axis_index("dp") // near * wide, wide, axis=1)
+    return lax.dynamic_slice_in_dim(rows, lax.axis_index(DP) // near * wide, wide, axis=1)
 
 
 def to_owners(grad):
-    count = lax.axis_size("dp")
+    count = lax.axis_size(DP)
     blocks = grad.astype(jnp.bfloat16).reshape((count, grad.shape[0] // count) + grad.shape[1:])
-    return lax.all_to_all(blocks, "dp", split_axis=0, concat_axis=0)
+    return lax.all_to_all(blocks, DP, split_axis=0, concat_axis=0)
 
 
 def step(
@@ -500,11 +500,11 @@
     field_in = tokens.astype(jnp.float32)
     normed_one, scaled_one, factor_one = normed(field_in, norm_gains[0])
     normed_all = spread_rows(copies_of(normed_one))
-    qkv_full = gather_rows(jnp.concatenate([qkv_weight[m].astype(bf16) for m in range(3)], axis=1), "dp")
-    out_full = gather_rows(out_weight.T.astype(bf16), "dp")
-    gate_full = gather_rows(gate_weight[0].astype(bf16), "dp")
-    up_full = gather_rows(gate_weight[1].astype(bf16), "dp")
-    down_full = gather_rows(down_weight.T.astype(bf16), "dp")
+    qkv_full = gather_rows(jnp.concatenate([qkv_weight[m].astype(bf16) for m in range(3)], axis=1), DP)
+    out_full = gather_rows(out_weight.T.astype(bf16), DP)
+    gate_full = gather_rows(gate_weight[0].astype(bf16), DP)
+    up_full = gather_rows(gate_weight[1].astype(bf16), DP)
+    down_full = gather_rows(down_weight.T.astype(bf16), DP)
 
     other_cotan = to_partner(cotangent)
     lo, hi, info = layout_of(seq_ids, block_ids, TILE, TILE)
@@ -526,28 +526,29 @@
     attn_rows = sum_rows(dot_cols(mixed_all, out_full).astype(bf16))
     residual = field_in + attn_rows
     normed_two, scaled_two, factor_two = normed(residual, norm_gains[1])
-    other_two = to_partner(normed_two)
-    normed_two, gate_full, up_full = lax.optimization_barrier((normed_two, gate_full, up_full, tick(normed_two)))[:3]
+    normed_two, gate_full, up_full = lax.optimization_barrier((normed_two, gate_full, up_full))
     ffn_input = spread_rows(copies_of(normed_two))
-    other_dy = gather_rows(after(other_cotan, ffn_input), "tensor")
-    other_input = spread_rows(copies_of(after(other_two, ffn_input)))
+    other_two = to_partner(after(normed_two, down_full))
+    mark = tick(ffn_input)
+    ffn_input = after(ffn_input, mark)
+    other_dy = gather_rows(other_cotan, TP)
+    other_input = gather_rows(other_two, TP)
 
     gate_pre = dot(ffn_input, gate_full)
-    up_pre = dot(after(ffn_input, tick(gate_pre)), up_full)
+    up_pre = dot(ffn_input, up_full)
     sigmoid_gate = jax.nn.sigmoid(gate_pre)
     swish = gate_pre * sigmoid_gate
     hidden = (swish * up_pre).astype(bf16)
     down_grad = dot_rows(half_cols(cotan_all), hidden).astype(bf16)
     down_recv = to_half(down_grad)
-    hidden_grad = dot(after(cotan_all, down_grad), down_full)
+    hidden_grad = dot(after(cotan_all, tick(down_grad)), down_full)
     gate_grad_low = (
         hidden_grad * up_pre * sigmoid_gate * (1.0 + gate_pre * (1.0 - sigmoid_gate))
     ).astype(bf16)
     up_grad_low = (hidden_grad * swish).astype(bf16)
     ffn_back = (dot_cols(gate_grad_low, gate_full) + dot_cols(up_grad_low, up_full)).astype(bf16)
     ffn_back_rows = scatter_rows(ffn_back)
-    mark = tick(ffn_back)
-    input_half = half_cols(after(ffn_input, mark))
+    input_half = half_cols(after(ffn_input, ffn_back))
     gate_grad = dot_rows(input_half, gate_grad_low).astype(bf16)
     gate_recv = to_half(gate_grad)
     up_grad = dot_rows(input_half, up_grad_low).astype(bf16)
@@ -556,14 +557,15 @@
 
     other_input = after(other_input, gate_grad, up_grad)
     gate_pre = dot(other_input, gate_full)
-    up_pre = dot(after(other_input, tick(gate_pre)), up_full)
+    up_pre = dot(other_input, up_full)
     sigmoid_gate = jax.nn.sigmoid(gate_pre)
     swish = gate_pre * sigmoid_gate
     hidden = (swish * up_pre).astype(bf16)
     mark = tick(hidden)
     other_dy = after(other_dy, mark)
-    near = lax.axis_size("dp") // 2
+    near = lax.axis_size(DP) // 2
     down_grad = dot_rows(half_cols(other_dy), hidden).astype(bf16)
+    down_recv2 = to_half(down_grad)
     hidden_grad = dot(after(other_dy, down_grad), down_full)
     gate_grad_low = (
         hidden_grad * up_pre * sigmoid_gate * (1.0 + gate_pre * (1.0 - sigmoid_gate))
@@ -571,14 +573,14 @@
     up_grad_low = (hidden_grad * swish).astype(bf16)
     input_half = half_cols(after(other_input, tick(gate_grad_low, up_grad_low)))
     rest = [dot_rows(input_half, low).astype(bf16) for low in (gate_grad_low, up_grad_low)]
-    rest = jnp.stack([x.reshape(near, -1, x.shape[1]) for x in rest + [down_grad]], axis=1)
+    rest = jnp.stack([x.reshape(near, -1, x.shape[1]) for x in rest], axis=1)
     rest_recv = to_half(rest.reshape(-1, rest.shape[-1]))
     mark = tick(rest)
 
     cotan_rows = cotangent.astype(jnp.float32)
     resid_grad = cotan_rows + norm_back(ffn_back_rows, scaled_two, factor_two, norm_gains[1])
     gain_two = jnp.sum(ffn_back_rows * scaled_two, axis=0)
-    resid_all = gather_rows(resid_grad.astype(bf16), "tensor")
+    resid_all = gather_rows(resid_grad.astype(bf16), TP)
     resid_all = after(resid_all, mark)
     mixed_grad = dot(resid_all, out_full).astype(bf16)
     out_grad = dot_rows(resid_all, mixed_all).astype(bf16)
@@ -597,17 +599,17 @@
     layer_out = (residual + ffn_part).astype(bf16)
     tokens_grad = resid_grad + norm_back(in_grad_rows, scaled_one, factor_one, norm_gains[0])
     gain_one = jnp.sum(in_grad_rows * scaled_one, axis=0)
-    gain_part = jnp.stack([gain_one, gain_two])
-    gain_part = jnp.sum(lax.all_gather(gain_part, "tensor", axis=0), axis=0)
-    gain_all = lax.all_gather(gain_part, "dp", axis=0)
-    picker = groups[None, :] == jnp.arange(GROUPS, dtype=jnp.int32)[:, None]
-    gain_grad = jnp.sum(jnp.where(picker[:, :, None, None], gain_all[None], 0.0), axis=1)
-    order = after(order, gain_all)
-    side = order // near != lax.axis_index("dp") // near
+    own_group = (jnp.arange(GROUPS, dtype=jnp.int32) == groups[lax.axis_index(DP)]).astype(
+        jnp.float32
+    )
+    gain_slots = own_group[:, None, None] * jnp.stack([gain_one, gain_two])[None]
+    gain_grad = lax.psum(gain_slots, (DP, TP))
+    order = after(order, gain_slots)
+    side = order // near != lax.axis_index(DP) // near
     near_order = order % near + near * side.astype(jnp.int32)
 
     down_new = optimize(
-        near_order, (down_recv, rest_recv), down_weight, down_first, down_second, down_outer, 3, turned=True
+        near_order, (down_recv, down_recv2), down_weight, down_first, down_second, down_outer, 3, turned=True
     )
     gate_half = optimize(
         near_order, (gate_recv, rest_recv), gate_weight, gate_first, gate_second, gate_outer, 2, member=0
@@ -629,59 +631,59 @@
 
 def solution(mesh):
     in_specs = (
-        P(("dp", "tensor"), None),
-        P(("dp", "tensor"), None),
-        P("dp"),
-        P("dp"),
-        P(),
-        P(None, "dp", "tensor"),
-        P("tensor", "dp"),
-        P(None, "dp", "tensor"),
-        P("tensor", "dp"),
-        P(),
-        P(None, None, "dp", "tensor"),
-        P(None, "tensor", "dp"),
-        P(None, None, "dp", "tensor"),
-        P(None, "tensor", "dp"),
-        P(),
-        P(None, None, "dp", "tensor"),
-        P(None, "tensor", "dp"),
-        P(None, None, "dp", "tensor"),
-        P(None, "tensor", "dp"),
-        P(),
-        P(None, "dp", "tensor"),
-        P("tensor", "dp"),
-        P(None, "dp", "tensor"),
-        P("tensor", "dp"),
+        P((DP, TP), None),
+        P((DP, TP), None),
+        P(DP),
+        P(DP),
+        P(),
+        P(None, DP, TP),
+        P(TP, DP),
+        P(None, DP, TP),
+        P(TP, DP),
+        P(),
+        P(None, None, DP, TP),
+        P(None, TP, DP),
+        P(None, None, DP, TP),
+        P(None, TP, DP),
+        P(),
+        P(None, None, DP, TP),
+        P(None, TP, DP),
+        P(None, None, DP, TP),
+        P(None, TP, DP),
+        P(),
+        P(None, DP, TP),
+        P(TP, DP),
+        P(None, DP, TP),
+        P(TP, DP),
         P(),
     )
     out_specs = (
-        P(("dp", "tensor"), None),
-        P(("dp", "tensor"), None),
-        P(None, None, "dp", "tensor"),
-        P(None, None, "dp", "tensor"),
-        P(None, "dp", "tensor"),
-        P(None, "dp", "tensor"),
-        P(None, "dp", "tensor"),
-        P(None, "dp", "tensor"),
-        P(None, "tensor", "dp"),
-        P(None, "tensor", "dp"),
-        P("tensor", "dp"),
-        P("tensor", "dp"),
-        P("tensor", "dp"),
-        P("tensor", "dp"),
-        P(None, None, "dp", "tensor"),
-        P(None, None, "dp", "tensor"),
-        P(None, "dp", "tensor"),
-        P(None, "dp", "tensor"),
-        P(None, "dp", "tensor"),
-        P(None, "dp", "tensor"),
-        P(None, "tensor", "dp"),
-        P(None, "tensor", "dp"),
-        P("tensor", "dp"),
-        P("tensor", "dp"),
-        P("tensor", "dp"),
-        P("tensor", "dp"),
+        P((DP, TP), None),
+        P((DP, TP), None),
+        P(None, None, DP, TP),
+        P(None, None, DP, TP),
+        P(None, DP, TP),
+        P(None, DP, TP),
+        P(None, DP, TP),
+        P(None, DP, TP),
+        P(None, TP, DP),
+        P(None, TP, DP),
+        P(TP, DP),
+        P(TP, DP),
+        P(TP, DP),
+        P(TP, DP),
+        P(None, None, DP, TP),
+        P(None, None, DP, TP),
+        P(None, DP, TP),
+        P(None, DP, TP),
+        P(None, DP, TP),
+        P(None, DP, TP),
+        P(None, TP, DP),
+        P(None, TP, DP),
+        P(TP, DP),
+        P(TP, DP),
+        P(TP, DP),
+        P(TP, DP),
         P(),
         P(),
         P(),

time: 1650 us -> 1550 us (0.939)
  blocking collectives: 284 us -> 232 us
  waiting for transfers between devices: 507 us -> 466 us
    all_to_all x9, waiting for transfers between devices: 325 us -> 243 us  [the longest x3 147 us: spread_rows(): parts = lax.all_to_all(copies, TP, split_axis=0, concat_axis=0)]
    all_gather x2 -> x0, blocking collectives: 51.7 us -> none  [the longest x1 44.7 us: step(): gain_all = lax.all_gather(gain_part, 'dp', axis=0)]
    all_gather x7 -> x8, waiting for transfers between devices: 0.03 us -> 26.7 us  [gather_rows(): return lax.all_gather(part, axis, axis=0, tiled=True)]
  transfers between devices with their start and end apart: 21 -> 23, of which waited for: 8 -> 8; matrix products, arithmetic and copies ran while one was open for 25% -> 32% of each run, Pallas kernels for 13% -> 16%
where the time goes in v5:
time: 1550 us; the launch traced here: 1540 us
  waiting for transfers between devices  466 us (30%)
  matrix products  417 us (27%)
  Pallas kernels  242 us (16%)
  blocking collectives  232 us (15%)
  starting transfers between devices  73.3 us (5%)
  other arithmetic  62.5 us (4%)
  local copies, waits for them, and re-layouts  35.8 us (2%)
    dot_general x8, matrix products, dot(): return jnp.dot(left, right, preferred_element_type=jnp.float32)  205 us
    ppermute x2, waiting for transfers between devices, to_partner(): lax.ppermute(part, DP, [(i, (i + count // 2) % count) for i in range(coun...  182 us
    all_to_all x3, waiting for transfers between devices, spread_rows(): parts = lax.all_to_all(copies, TP, split_axis=0, concat_axis=0)  147 us
    all_to_all x1, blocking collectives, to_owners(): return lax.all_to_all(blocks, DP, split_axis=0, concat_axis=0)  144 us
    dot_general x8, matrix products, dot_rows(): lax.dot_general(left, right, (((0,), (0,)), ((), ())), preferred_element_...  114 us
    dot_general x5, matrix products, dot_cols(): lax.dot_general(left, right, (((1,), (1,)), ((), ())), preferred_element_...  97.7 us
    pallas_call x5, Pallas kernels, optimize(): pl.pallas_call(functools.partial(opt_kernel, sources // GROUPS, turned, l...  88.6 us
    all_to_all x1, blocking collectives, sum_rows(): parts = lax.all_to_all(blocks, TP, split_axis=0, concat_axis=0)  88 us
  transfers between devices with their start and end apart: 23, of which 8 were waited for; matrix products, arithmetic and copies ran while one was open for 32% of the time, Pallas kernels for 16%

profile of v5, /device:TPU:1, one launch (start us, length us, event | category | flops | bytes accessed | tf_op | source)
XLA Modules:
  0.0 1544.3 jit_solution(168249385021269257)
XLA Ops:
  11.7 2.5 convert.10
  17.4 4.8 broadcast_in_dim.14
  22.2 5.8 all-to-all-start
  34.3 3.7 fusion.33
  38.0 3.0 pad_maximum_fusion.1
  41.0 4.5 broadcast_in_dim.13.refs_5_
  48.8 71.8 %all-to-all-done = bf16[4,512,2048]{2,1,0:T(8,128)(2,1)} async-done(((bf16[4,512,2048]{2,1,0:T(8,128)(2,1)}), bf16[4,512,2048]{2,1,0:T(8,128)(2,1)}, u32[]{:S(2)}, u32[]{:S(2)}) %all-to-all-start) | async-done | bytes 8388640 | tf_op jit(solution)/shard_map/all_to_all | solution.py:429
  120.7 19.6 %fusion.50.q_ref.k_ref.v_ref = f32[2048,1536]{1,0:T(8,128)} fusion(bf16[2048,2048]{1,0:T(8,128)(2,1)} %bitcast.9, bf16[2048,1536]{1,0:T(8,128)(2,1)} %all-gather.11.cloned.1.call-done), kind=kOutput, calls=%fused_computation.116 | convolution fusion | flops 12884901888 | bytes 27262976 | tf_op jit(solution)/shard_map/dot_general | solution.py:392
  140.3 73.6 %attn_fwd.1 = (bf16[2048,512]{1,0:T(8,128)(2,1)}, bf16[2048,512]{1,0:T(8,128)(2,1)}, bf16[2048,512]{1,0:T(8,128)(2,1)}, bf16[2048,512]{1,0:T(8,128)(2,1)}, f32[4,2,2048]{2,1,0:T(2,128)S(1)}) custom-call(s32[6,4]{1,0:T(8,128)S(1)} %copy-done.22, f32[2048,1536]{1,0:T(8,128)} %fusion.50.q_ref.k_ref.v_ref, f32[2048,1536]{1,0:T(8,128)} %fusion.50.q_ref.k_ref.v_ref, ...), custom_call_target="tpu_custom_call" | custom-call | flops 5153960960 | bytes 12582912 | tf_op jit(solution)/shard_map/attn_fwd/pallas_call | solution.py:106
  213.9 6.7 convolution_convert_fusion.2
  220.6 88.0 %all_to_all.55 = bf16[4,512,2048]{2,1,0:T(8,128)(2,1)S(1)} all-to-all(bf16[4,512,2048]{2,1,0:T(8,128)(2,1)S(1)} %bitcast.82), channel_id=1, replica_groups=mesh['dp'=8,'tensor'=4] {'tensor'}, dimensions={0} | all-to-all | bytes 16777216 | tf_op jit(solution)/shard_map/all_to_all | solution.py:436
  308.6 3.9 convert_reduce_fusion
  312.5 2.8 multiply_reduce_fusion
  319.2 6.1 broadcast_in_dim.15
  325.2 5.7 all-to-all-start.2
  331.0 26.6 %all-gather.15.cloned.1.call-done = bf16[2048,2048]{0,1:T(8,128)(2,1)} async-done(((bf16[256,2048]{0,1:T(8,128)(2,1)}), bf16[2048,2048]{0,1:T(8,128)(2,1)}) %all-gather.15.cloned.1.call-update) | async-done | bytes 8388624 | tf_op jit(solution)/shard_map/all_gather | solution.py:421
  359.5 90.4 %collective-permute-done = bf16[512,2048]{1,0:T(8,128)(2,1)} collective-permute-done((bf16[512,2048]{1,0:T(8,128)(2,1)}, bf16[512,2048]{1,0:T(8,128)(2,1)}, u32[]{:S(2)}, u32[]{:S(2)}) %collective-permute-start) | collective-permute-done | bytes 2097184 | tf_op jit(solution)/shard_map/ppermute | solution.py:457
  449.9 5.6 all-to-all-start.3
  456.2 25.8 %fusion.51 = f32[2048,2048]{1,0:T(8,128)} fusion(bf16[2048,2048]{1,0:T(8,128)(2,1)} %bitcast.18.refs_0_, bf16[2048,2048]{1,0:T(8,128)(2,1)} %bitcast.108), kind=kOutput, calls=%fused_computation.117 | convolution fusion | flops 17179869184 | bytes 33554432 | tf_op jit(solution)/shard_map/dot_general | solution.py:392
  481.9 28.1 %multiply_convert_fusion.5 = (bf16[2048,2048]{1,0:T(8,128)(2,1)}, f32[2048,2048]{1,0:T(8,128)}) fusion(f32[2048,2048]{1,0:T(8,128)} %fusion.51, bf16[2048,2048]{1,0:T(8,128)(2,1)} %bitcast.18.refs_0_, bf16[2048,2048]{1,0:T(8,128)(2,1)} %bitcast.105), kind=kOutput, calls=%fused_computation.8 | convolution fusion | flops 17205035008 | bytes 58720256 | tf_op jit(solution)/shard_map/dot_general | solution.py:392
  510.0 75.2 %all-to-all-done.3 = bf16[4,512,2048]{2,1,0:T(8,128)(2,1)} async-done(((bf16[4,512,2048]{2,1,0:T(8,128)(2,1)}), bf16[4,512,2048]{2,1,0:T(8,128)(2,1)}, u32[]{:S(2)}, u32[]{:S(2)}) %all-to-all-start.3) | async-done | bytes 8388640 | tf_op jit(solution)/shard_map/all_to_all | solution.py:429
  585.2 14.2 fusion.23.refs_0_
  599.9 34.3 %multiply_convert_fusion.3 = (bf16[2048,2048]{1,0:T(8,128)(2,1)}, bf16[2048,2048]{1,0:T(8,128)(2,1)}) fusion(f32[2048,2048]{1,0:T(8,128)} %fusion.51, f32[2048,2048]{1,0:T(8,128)} %get-tuple-element.192, bf16[2048,2048]{1,0:T(8,128)(2,1)} %bitcast.19, bf16[2048,2048]{0,1:T(8,128)(2,1)} %all-gather.15.cloned.1.call-done), kind=kOutput, calls=%fused_computation.6 | convolution fusion | flops 17234395136 | bytes 67108864 | tf_op jit(solution)/shard_map/dot_general | solution.py:392
  634.3 24.5 %fusion.52 = f32[2048,2048]{1,0:T(8,128)} fusion(bf16[2048,2048]{1,0:T(8,128)(2,1)} %get-tuple-element.178, bf16[2048,2048]{1,0:T(8,128)(2,1)} %bitcast.109), kind=kOutput, calls=%fused_computation.118 | convolution fusion | flops 17179869184 | bytes 33554432 | tf_op jit(solution)/shard_map/dot_general | solution.py:396
  658.8 25.5 %add_convert_fusion = bf16[2048,2048]{1,0:T(8,128)(2,1)} fusion(f32[2048,2048]{1,0:T(8,128)} %fusion.52, bf16[2048,2048]{1,0:T(8,128)(2,1)} %get-tuple-element.177, bf16[2048,2048]{1,0:T(8,128)(2,1)} %bitcast.106), kind=kOutput, calls=%fused_computation.5 | convolution fusion | flops 17188257792 | bytes 41943040 | tf_op jit(solution)/shard_map/dot_general | solution.py:396
  684.5 91.5 %collective-permute-done.1 = bf16[512,2048]{1,0:T(8,128)(2,1)} collective-permute-done((bf16[512,2048]{1,0:T(8,128)(2,1)}, bf16[512,2048]{1,0:T(8,128)(2,1)}, u32[]{:S(2)}, u32[]{:S(2)}) %collective-permute-start.1) | collective-permute-done | bytes 2097184 | tf_op jit(solution)/shard_map/ppermute | solution.py:457
  776.0 14.1 convolution_convert_fusion.7
  790.0 5.3 all-to-all-start.8
  795.4 14.4 convolution_convert_fusion.6
  809.8 24.2 %fusion.53 = f32[2048,2048]{1,0:T(8,128)} fusion(bf16[2048,2048]{1,0:T(8,128)(2,1)} %all-gather.19.cloned.1.call-done, bf16[2048,2048]{1,0:T(8,128)(2,1)} %bitcast.110), kind=kOutput, calls=%fused_computation.119 | convolution fusion | flops 17179869184 | bytes 33554432 | tf_op jit(solution)/shard_map/dot_general | solution.py:392
  834.0 4.7 fusion.14
  839.4 5.0 fusion.43
  844.4 28.7 %multiply_convert_fusion.2 = (bf16[2048,2048]{1,0:T(8,128)(2,1)}, f32[2048,2048]{1,0:T(8,128)}) fusion(f32[2048,2048]{1,0:T(8,128)} %fusion.53, bf16[2048,2048]{1,0:T(8,128)(2,1)} %all-gather.19.cloned.1.call-done, bf16[2048,2048]{1,0:T(8,128)(2,1)} %bitcast.107), kind=kOutput, calls=%fused_computation.2 | convolution fusion | flops 17205035008 | bytes 58720256 | tf_op jit(solution)/shard_map/dot_general | solution.py:392
  873.6 14.8 fusion.26
  888.5 5.2 all-to-all-start.9
  893.7 34.9 %multiply_convert_fusion.1 = (bf16[2048,2048]{1,0:T(8,128)(2,1)}, bf16[2048,2048]{1,0:T(8,128)(2,1)}) fusion(f32[2048,2048]{1,0:T(8,128)} %fusion.53, f32[2048,2048]{1,0:T(8,128)} %get-tuple-element.194, bf16[2048,2048]{1,0:T(8,128)(2,1)} %all-gather.21.cloned.1.call-done, bf16[2048,2048]{0,1:T(8,128)(2,1)} %all-gather.15.cloned.1.call-done), kind=kOutput, calls=%fused_computation.1 | convolution fusion | flops 17234395136 | bytes 67108864 | tf_op jit(solution)/shard_map/dot_general | solution.py:392
  929.2 14.1 convolution_convert_fusion.4
  943.3 12.9 convolution_convert_fusion.5
  956.2 7.6 pad_maximum_fusion.refs_0_
  964.4 9.9 convolution_convert_fusion.8
  974.3 4.8 all-to-all-start.10
  979.2 9.9 convolution_convert_fusion.9.do_ref
  989.1 75.7 %attn_bwd.1 = (bf16[2048,512]{1,0:T(8,128)(2,1)S(1)}, bf16[2048,512]{1,0:T(8,128)(2,1)}, bf16[2048,512]{1,0:T(8,128)(2,1)}) custom-call(s32[6,4]{1,0:T(8,128)S(1)} %copy-done.22, bf16[2048,512]{1,0:T(8,128)(2,1)} %get-tuple-element.107.q_ref, bf16[2048,512]{1,0:T(8,128)(2,1)} %get-tuple-element.108.k_ref, bf16[2048,512]{1,0:T(8,128)(2,1)} %get-tuple-element.109.v_ref, ...), custom_call_target="tpu_custom_call" | custom-call | flops 12884901888 | bytes 16777216 | tf_op jit(solution)/shard_map/attn_bwd/pallas_call | solution.py:202
  1067.1 2.7 copy-done.30
  1069.8 17.4 %convolution_convert_fusion.1.refs_0_ = bf16[2048,2048]{1,0:T(8,128)(2,1)} fusion(bf16[2048,1536]{1,0:T(8,128)(2,1)S(1)} %constant_dynamic-update-slice_fusion, bf16[2048,1536]{1,0:T(8,128)(2,1)} %all-gather.11.cloned.1.call-done), kind=kOutput, calls=%fused_computation.16 | convolution fusion | flops 12889096192 | bytes 20971520 | tf_op jit(solution)/shard_map/dot_general | solution.py:396
  1087.3 28.8 %all-to-all-start.7 = ((bf16[4,512,2048]{2,1,0:T(8,128)(2,1)}), bf16[4,512,2048]{2,1,0:T(8,128)(2,1)}, u32[]{:S(2)}, u32[]{:S(2)}) async-start(bf16[4,512,2048]{2,1,0:T(8,128)(2,1)} %bitcast.80), calls=%async_computation.10 | async-start | bytes 16777216 | tf_op jit(solution)/shard_map/all_to_all | solution.py:452
  1116.7 19.2 %convolution_convert_fusion.3 = bf16[2048,1536]{1,0:T(8,128)(2,1)} fusion(bf16[2048,2048]{1,0:T(8,128)(2,1)} %bitcast.9, bf16[2048,1536]{1,0:T(8,128)(2,1)} %copy-done.30), kind=kOutput, calls=%fused_computation.18 | convolution fusion | flops 12888047616 | bytes 20971520 | tf_op jit(solution)/shard_map/dot_general | solution.py:400
  1135.9 73.2 %all-to-all-done.7.refs_1_ = bf16[4,512,2048]{2,1,0:T(8,128)(2,1)} async-done(((bf16[4,512,2048]{2,1,0:T(8,128)(2,1)}), bf16[4,512,2048]{2,1,0:T(8,128)(2,1)}, u32[]{:S(2)}, u32[]{:S(2)}) %all-to-all-start.7) | async-done | bytes 8388640 | tf_op jit(solution)/shard_map/all_to_all | solution.py:452
  1209.2 3.6 all-to-all-start.5
  1212.8 23.5 %convolution_convert_fusion = bf16[2048,2048]{1,0:T(8,128)(2,1)} fusion(bf16[2048,2048]{1,0:T(8,128)(2,1)} %get-tuple-element.125, bf16[2048,2048]{0,1:T(8,128)(2,1)} %all-gather.15.cloned.1.call-done), kind=kOutput, calls=%fused_computation.15 | convolution fusion | flops 17184063488 | bytes 25165824 | tf_op jit(solution)/shard_map/dot_general | solution.py:396
  1236.3 23.1 %all-to-all-done.5.refs_0_ = bf16[8,256,512]{2,1,0:T(8,128)(2,1)S(1)} async-done(((bf16[8,256,512]{2,1,0:T(8,128)(2,1)}), bf16[8,256,512]{2,1,0:T(8,128)(2,1)S(1)}, u32[]{:S(2)}, u32[]{:S(2)}) %all-to-all-start.5) | async-done | bytes 2097184 | tf_op jit(solution)/shard_map/all_to_all | solution.py:469
  1259.4 144.3 %all_to_all.56.refs_0_ = bf16[8,256,1536]{2,1,0:T(8,128)(2,1)} all-to-all(bf16[8,256,1536]{2,1,0:T(8,128)(2,1)} %bitcast.83), channel_id=1, replica_groups=mesh['dp'=8,'tensor'=4] {'dp'}, dimensions={0} | all-to-all | bytes 12582912 | tf_op jit(solution)/shard_map/all_to_all | solution.py:469
  1403.7 6.0 all-to-all-start.6
  1411.9 3.5 fusion.17
  1416.4 8.7 fusion.10
  1425.1 4.7 optimize.6
  1429.9 2.8 copy-done.2
  1432.7 16.0 %optimize.5 = (f32[4,3,256,512]{3,2,1,0:T(8,128)}, f32[4,3,256,512]{3,2,1,0:T(8,128)}, f32[3,256,512]{2,1,0:T(8,128)}, f32[3,256,512]{2,1,0:T(8,128)}, f32[3,256...) custom-call(s32[8]{0:T(128)S(1)} %get-tuple-element.127.order, bf16[8,256,1536]{2,1,0:T(8,128)(2,1)S(1)} %copy-done.2, ...), custom_call_target="tpu_custom_call" | custom-call | flops 23592960 | bytes 40108032 | tf_op jit(solution)/shard_map/optimize/pallas_call | solution.py:374
  1448.8 23.2 %optimize.7 = (f32[4,2,256,2048]{3,2,1,0:T(8,128)}, f32[4,2,256,2048]{3,2,1,0:T(8,128)}, f32[2,256,2048]{2,1,0:T(8,128)}, f32[2,256,2048]{2,1,0:T(8,128)}, f32[2...) custom-call(s32[8]{0:T(128)S(1)} %fusion.42.order, bf16[4,256,2048]{2,1,0:T(8,128)(2,1)} %all-to-all-done.8.refs_0_, ...), custom_call_target="tpu_custom_call" | custom-call | flops 31457280 | bytes 53477376 | tf_op jit(solution)/shard_map/optimize/pallas_call | solution.py:374
  1472.0 21.6 %optimize.9 = (f32[4,2048,256]{2,1,0:T(8,128)}, f32[4,2048,256]{2,1,0:T(8,128)}, f32[2048,256]{1,0:T(8,128)}, f32[2048,256]{1,0:T(8,128)}, f32[2048,256]{1,0:T(8,128)}, /*index=5*/bf16[2048,256]{1,0:T(8,128)(2,1)}) custom-call(s32[8]{0:T(128)S(1)} %fusion.42.order, bf16[4,256,2048]{2,1,0:T(8,128)(2,1)} %all-to-all-done.9.refs_0_, ...), custom_call_target="tpu_custom_call" | custom-call | flops 31457280 | bytes 53477376 | tf_op jit(solution)/shard_map/optimize/pallas_call | solution.py:374
  1493.6 2.2 copy-done.1
  1495.8 2.2 copy-done.4
  1498.0 23.1 %optimize.8 = (f32[4,2,256,2048]{3,2,1,0:T(8,128)}, f32[4,2,256,2048]{3,2,1,0:T(8,128)}, f32[2,256,2048]{2,1,0:T(8,128)}, f32[2,256,2048]{2,1,0:T(8,128)}, f32[2...) custom-call(s32[8]{0:T(128)S(1)} %fusion.42.order, ...), custom_call_target="tpu_custom_call", output_to_operand_aliasing={{0}: (7, {}), {1}: (8, {}), {2}: (9, {}), {3}: (10, {}), {4... | custom-call | flops 31457280 | bytes 53477376 | tf_op jit(solution)/shard_map/optimize/pallas_call | solution.py:374
  1521.1 13.8 all-reduce.2.cloned.1.call-done
  (189 shorter events, 34.9 us)
Async XLA Ops:
  7.2 113.5 %all-gather.11.cloned.1.call-start = ((), (), s32[]{:S(2)}) async-start(), calls=%async_computation.14 | async-start | bytes 7077888 | tf_op jit(solution)/shard_map/all_gather | solution.py:421
  8.8 7.4 copy-start.25
  9.8 7.0 copy-start.36
  9.8 204.1 %all-gather.13.cloned.1.call-start = ((), (), s32[]{:S(2)}) async-start(), calls=%async_computation.15 | async-start | bytes 2359296 | tf_op jit(solution)/shard_map/all_gather | solution.py:421
  11.6 307.5 %all-gather.23.cloned.1.call-start = ((), (), s32[]{:S(2)}) async-start(), calls=%async_computation.24 | async-start | bytes 9437184 | tf_op jit(solution)/shard_map/all_gather | solution.py:421
  15.7 303.5 %all-gather.25.cloned.1.call-start = ((), (), s32[]{:S(2)}) async-start(), calls=%async_computation.25 | async-start | bytes 9437184 | tf_op jit(solution)/shard_map/all_gather | solution.py:421
  16.8 5.5 copy-start.43
  16.8 5.4 copy-start.34
  16.8 298.6 %copy-start.31 = (f32[1,2048]{1,0:T(1,128)}, f32[1,2048]{1,0:T(1,128)S(1)}, u32[]{:S(2)}) copy-start(f32[1,2048]{1,0:T(1,128)S(1)} %get-tuple-element.186) | copy-start | bytes 24580
  22.2 6.1 copy-start.9
  22.2 7.2 copy-start.49
  22.2 7.2 copy-start.50
  22.2 98.4 %all-to-all-start = ((bf16[4,512,2048]{2,1,0:T(8,128)(2,1)}), bf16[4,512,2048]{2,1,0:T(8,128)(2,1)}, u32[]{:S(2)}, u32[]{:S(2)}) async-start(bf16[4,512,2048]{2,1,0:T(8,128)(2,1)} %broadcast_in_dim.14), calls=%async_computation | async-start | bytes 16777216 | tf_op jit(solution)/shard_map/all_to_all | solution.py:429
  28.1 329.5 %all-gather.15.cloned.1.call-start = ((), (), s32[]{:S(2)}) async-start(), calls=%async_computation.16 | async-start | bytes 9437184 | tf_op jit(solution)/shard_map/all_gather | solution.py:421
  29.4 11.7 copy-start.27
  31.2 15.6 %copy-start.20 = (s32[2048]{0:T(1024)}, s32[2048]{0:T(1024)S(1)}, u32[]{:S(2)}) copy-start(s32[2048]{0:T(1024)S(1)} %convert_reduce_fusion.1) | copy-start | bytes 24580
  33.1 12.5 copy-start.18
  120.6 19.6 %copy-start.5 = (f32[2048,128]{1,0:T(8,128)S(1)}, f32[2048,128]{1,0:T(8,128)}, u32[]{:S(2)}) copy-start(f32[2048,128]{1,0:T(8,128)} %get-tuple-element.96.refs_0_.cos_ref) | copy-start | bytes 3145732
  120.6 19.6 %copy-start.6 = (f32[2048,128]{1,0:T(8,128)S(1)}, f32[2048,128]{1,0:T(8,128)}, u32[]{:S(2)}) copy-start(f32[2048,128]{1,0:T(8,128)} %get-tuple-element.97.refs_1_.sin_ref) | copy-start | bytes 3145732
  120.6 19.6 %copy-start.7 = (s32[2048,1]{1,0:T(8,128)S(1)}, s32[2048,1]{1,0:T(8,128)}, u32[]{:S(2)}) copy-start(s32[2048,1]{1,0:T(8,128)} %copy.72.refs_2_.lo_ref) | copy-start | bytes 24580
  120.6 19.7 %copy-start.22 = (s32[6,4]{1,0:T(8,128)S(1)}, s32[6,4]{1,0:T(8,128)}, u32[]{:S(2)}) copy-start(s32[6,4]{1,0:T(8,128)} %stack.39.refs_4_.info) | copy-start | bytes 292
  120.7 19.6 %copy-start.8 = (s32[2048,1]{1,0:T(8,128)S(1)}, s32[2048,1]{1,0:T(8,128)}, u32[]{:S(2)}) copy-start(s32[2048,1]{1,0:T(8,128)} %copy.73.refs_3_.hi_ref) | copy-start | bytes 24580
  315.4 9.8 copy-start.40
  325.2 124.7 %all-to-all-start.2 = ((bf16[4,512,2048]{2,1,0:T(8,128)(2,1)}), bf16[4,512,2048]{2,1,0:T(8,128)(2,1)}, u32[]{:S(2)}, u32[]{:S(2)}) async-start(bf16[4,512,2048]{2,1,0:T(8,128)(2,1)} %broadcast_in_dim.15), calls=%async_computation.2 | async-start | bytes 16777216 | tf_op jit(solution)/shard_map/all_to_all | solution.py:429
  330.9 478.9 %all-gather.19.cloned.1.call-start = ((), (), s32[]{:S(2)}) async-start(), calls=%async_computation.19 | async-start | bytes 10485760 | tf_op jit(solution)/shard_map/all_gather | solution.py:421
  357.6 92.3 %collective-permute-start = (bf16[512,2048]{1,0:T(8,128)(2,1)}, bf16[512,2048]{1,0:T(8,128)(2,1)}, u32[]{:S(2)}, u32[]{:S(2)}) collective-permute-start(bf16[512,2048]{1,0:T(8,128)(2,1)} %multiply_convert_fusion.6), channel_id=1, source_target_pairs={{0,16},{4,20},{8,24},{12,28},{16,0},{20,4},{24,8},{28,12},{1,17},{... | collective-permute-start | bytes 6291464 | tf_op jit(solution)/shard_map/ppermute | solution.py:457
  449.9 135.3 %all-to-all-start.3 = ((bf16[4,512,2048]{2,1,0:T(8,128)(2,1)}), bf16[4,512,2048]{2,1,0:T(8,128)(2,1)}, u32[]{:S(2)}, u32[]{:S(2)}) async-start(bf16[4,512,2048]{2,1,0:T(8,128)(2,1)} %broadcast_in_dim.13.refs_5_), calls=%async_computation.3 | async-start | bytes 16777216 | tf_op jit(solution)/shard_map/all_to_all | solution.py:429
  455.5 378.5 %reduce-scatter.4.cloned.1.call-start = ((), (), s32[]{:S(2)}) async-start(), calls=%async_computation.17 | async-start | bytes 10485760 | tf_op jit(solution)/shard_map/reduce_scatter | solution.py:441
  684.3 189.3 %all-gather.21.cloned.1.call-start = ((), (), s32[]{:S(2)}) async-start(), calls=%async_computation.20 | async-start | bytes 10485760 | tf_op jit(solution)/shard_map/all_gather | solution.py:421
  684.4 91.6 %collective-permute-start.1 = (bf16[512,2048]{1,0:T(8,128)(2,1)}, bf16[512,2048]{1,0:T(8,128)(2,1)}, u32[]{:S(2)}, u32[]{:S(2)}) collective-permute-start(bf16[512,2048]{1,0:T(8,128)(2,1)} %param.26), channel_id=1, source_target_pairs={{0,16},{4,20},{8,24},{12,28},{16,0},{20,4},{24,8},{28,12},{1,17},{... | collective-permute-start | bytes 6291464 | tf_op jit(solution)/shard_map/ppermute | solution.py:457
  790.0 98.5 %all-to-all-start.8 = ((bf16[4,256,2048]{2,1,0:T(8,128)(2,1)}), bf16[4,256,2048]{2,1,0:T(8,128)(2,1)}, u32[]{:S(2)}, u32[]{:S(2)}) async-start(bf16[4,256,2048]{2,1,0:T(8,128)(2,1)} %bitcast.86), calls=%async_computation.11 | async-start | bytes 8388608 | tf_op jit(solution)/shard_map/all_to_all | solution.py:452
  795.4 169.1 %all-gather.17.cloned.1.call-start = ((), (), s32[]{:S(2)}) async-start(), calls=%async_computation.18 | async-start | bytes 10485760 | tf_op jit(solution)/shard_map/all_gather | solution.py:421
  809.8 24.2 %copy-start.32 = (f32[1,2048]{1,0:T(1,128)S(1)}, f32[1,2048]{1,0:T(1,128)}, u32[]{:S(2)}) copy-start(f32[1,2048]{1,0:T(1,128)} %copy-done.31) | copy-start | bytes 24580
  809.8 24.2 %copy-start.41 = (f32[512]{0:T(512)S(1)}, f32[512]{0:T(512)}, u32[]{:S(2)}) copy-start(f32[512]{0:T(512)} %copy-done.40) | copy-start | bytes 6148
  888.5 85.8 %all-to-all-start.9 = ((bf16[4,256,2048]{2,1,0:T(8,128)(2,1)}), bf16[4,256,2048]{2,1,0:T(8,128)(2,1)}, u32[]{:S(2)}, u32[]{:S(2)}) async-start(bf16[4,256,2048]{2,1,0:T(8,128)(2,1)} %bitcast.81), calls=%async_computation.12 | async-start | bytes 8388608 | tf_op jit(solution)/shard_map/all_to_all | solution.py:452
  929.2 14.1 copy-start.28
  974.3 113.0 %all-to-all-start.10 = ((bf16[4,256,2048]{2,1,0:T(8,128)(2,1)}), bf16[4,256,2048]{2,1,0:T(8,128)(2,1)}, u32[]{:S(2)}, u32[]{:S(2)}) async-start(bf16[4,256,2048]{2,1,0:T(8,128)(2,1)} %bitcast.85), calls=%async_computation.13 | async-start | bytes 8388608 | tf_op jit(solution)/shard_map/all_to_all | solution.py:452
  979.1 9.9 copy-start.19
  979.1 9.9 copy-start.21
  979.2 432.8 %reduce-scatter.8.cloned.1.call-start = ((), (), s32[]{:S(2)}) async-start(), calls=%async_computation.22 | async-start | bytes 10485760 | tf_op jit(solution)/shard_map/reduce_scatter | solution.py:441
  1087.3 121.9 %all-to-all-start.7 = ((bf16[4,512,2048]{2,1,0:T(8,128)(2,1)}), bf16[4,512,2048]{2,1,0:T(8,128)(2,1)}, u32[]{:S(2)}, u32[]{:S(2)}) async-start(bf16[4,512,2048]{2,1,0:T(8,128)(2,1)} %bitcast.80), calls=%async_computation.10 | async-start | bytes 16777216 | tf_op jit(solution)/shard_map/all_to_all | solution.py:452
  1209.2 50.2 %all-to-all-start.5 = ((bf16[8,256,512]{2,1,0:T(8,128)(2,1)}), bf16[8,256,512]{2,1,0:T(8,128)(2,1)S(1)}, u32[]{:S(2)}, u32[]{:S(2)}) async-start(bf16[8,256,512]{2,1,0:T(8,128)(2,1)} %bitcast.89), calls=%async_computation.8 | async-start | bytes 4194304 | tf_op jit(solution)/shard_map/all_to_all | solution.py:469
  1212.7 203.6 %reduce-scatter.6.cloned.1.call-start = ((), (), s32[]{:S(2)}) async-start(), calls=%async_computation.21 | async-start | bytes 10485760 | tf_op jit(solution)/shard_map/reduce_scatter | solution.py:441
  1259.4 150.3 %copy-start.51 = (s32[8]{0:T(128)S(1)}, s32[8]{0:T(128)}, u32[]{:S(2)}) copy-start(s32[8]{0:T(128)} %param.29) | copy-start | bytes 100
  1259.4 152.6 %copy-start.35 = (f32[1,2048]{1,0:T(1,128)S(1)}, f32[1,2048]{1,0:T(1,128)}, u32[]{:S(2)}) copy-start(f32[1,2048]{1,0:T(1,128)} %copy-done.34) | copy-start | bytes 24580
  1259.4 152.6 %copy-start.44 = (f32[512]{0:T(512)S(1)}, f32[512]{0:T(512)}, u32[]{:S(2)}) copy-start(f32[512]{0:T(512)} %copy-done.43) | copy-start | bytes 6148
  1403.7 11.8 copy-start.45
  1403.7 12.6 copy-start.33
  1403.7 12.6 copy-start.42
  1403.7 12.6 copy-start.47
  1403.7 89.9 %all-to-all-start.6 = ((bf16[4,256,2048]{2,1,0:T(8,128)(2,1)}), bf16[4,256,2048]{2,1,0:T(8,128)(2,1)}, u32[]{:S(2)}, u32[]{:S(2)}) async-start(bf16[4,256,2048]{2,1,0:T(8,128)(2,1)} %bitcast.84), calls=%async_computation.9 | async-start | bytes 8388608 | tf_op jit(solution)/shard_map/all_to_all | solution.py:452
  1409.7 125.2 %all-reduce.2.cloned.1.call-start = ((), (), s32[]{:S(2)}) async-start(), calls=%async_computation.23 | async-start | bytes 131072 | tf_op jit(solution)/shard_map/psum | solution.py:606
  1416.3 8.8 copy-start.14
  1416.3 8.8 copy-start.17
  1416.3 8.8 copy-start.12
  1416.4 8.8 copy-start.13
  1432.7 16.0 %copy-start = (f32[2,256,2048]{2,1,0:T(8,128)S(1)}, f32[2,256,2048]{2,1,0:T(8,128)}, u32[]{:S(2)}) copy-start(f32[2,256,2048]{2,1,0:T(8,128)} %refs_4_.8) | copy-start | bytes 12582916
  1432.7 16.0 %copy-start.3 = (f32[2,256,2048]{2,1,0:T(8,128)S(1)}, f32[2,256,2048]{2,1,0:T(8,128)}, u32[]{:S(2)}) copy-start(f32[2,256,2048]{2,1,0:T(8,128)} %refs_5_.4) | copy-start | bytes 12582916
  1448.7 23.2 %copy-start.10 = (f32[2048,256]{1,0:T(8,128)S(1)}, f32[2048,256]{1,0:T(8,128)}, u32[]{:S(2)}) copy-start(f32[2048,256]{1,0:T(8,128)} %refs_4_.9) | copy-start | bytes 6291460
  1448.8 23.2 %copy-start.15 = (f32[2048,256]{1,0:T(8,128)S(1)}, f32[2048,256]{1,0:T(8,128)}, u32[]{:S(2)}) copy-start(f32[2048,256]{1,0:T(8,128)} %refs_5_.5) | copy-start | bytes 6291460
  1498.0 36.9 %copy-start.38 = (f32[4,2,2048]{2,1,0:T(2,128)S(1)}, f32[4,2,2048]{2,1,0:T(2,128)}, u32[]{:S(2)}) copy-start(f32[4,2,2048]{2,1,0:T(2,128)} %param.44) | copy-start | bytes 196612
  1498.0 36.9 %copy-start.39 = (f32[4,2,2048]{2,1,0:T(2,128)S(1)}, f32[4,2,2048]{2,1,0:T(2,128)}, u32[]{:S(2)}) copy-start(f32[4,2,2048]{2,1,0:T(2,128)} %param.39) | copy-start | bytes 196612
  1498.0 38.6 %copy-start.37 = (f32[2,2048]{1,0:T(2,128)S(1)}, f32[2,2048]{1,0:T(2,128)}, u32[]{:S(2)}) copy-start(f32[2,2048]{1,0:T(2,128)} %param.34) | copy-start | bytes 49156
  1498.0 38.6 %copy-start.48 = (f32[2,2048]{1,0:T(2,128)S(1)}, f32[2,2048]{1,0:T(2,128)}, u32[]{:S(2)}) copy-start(f32[2,2048]{1,0:T(2,128)} %param.49) | copy-start | bytes 49156
  (11 other events, 33.6 us)
Sparse Core Ops, SparseCore 0:
  10.2 67.1 all-gather.10
  79.6 29.2 all-gather.12
  111.1 80.8 all-gather.22
  194.0 80.5 all-gather.24
  276.6 80.9 all-gather.14
  450.0 165.8 all-gather.18
  684.4 86.5 reduce-scatter.3
  776.1 85.5 all-gather.20
  864.1 87.4 all-gather.16
  1087.4 108.5 reduce-scatter.7
  1236.4 83.5 reduce-scatter.5
  1416.4 118.4 all-reduce.1
